TPU v7x, 32 devices: a whole 2x2x4 slice. The times are simulated.
32 devices in a mesh: win: 8 (over z, x), atom: 4 (over y, core).
Axes of the slice: x: 2, y: 2, z: 4, core: 2. Of those that a mesh axis runs over, the one named last changes fastest.
Arguments:
- retarded: bfloat16 [64, 8, 2, 128, 128], P(('win', 'atom')), may hold values from -0.375 to 0.375
- sigma_in: bfloat16 [64, 8, 2, 128, 128], P(('win', 'atom')), may hold values from -6 to 6
- bit_shifts: int32 [3], replicated, may hold values from 0 to 2, as said below
- occupation: float32 [3], replicated, may hold values from 0.3 to 3
- neighbors: int32 [8, 3], replicated, may hold values from 0 to 7, as said below
- coupling: bfloat16 [3, 128, 128], replicated, may hold values from -0.375 to 0.375
Outputs:
- self_energy: bfloat16 [64, 8, 2, 128, 128], P('win', 'atom')
Inputs may be any that keep to these rules, and one draw needn't show every extreme that they name: `bit_shifts`: three different values; among them are 0 and 2, in an order drawn afresh. `neighbors`: column 0 of row b is b itself; the other columns of row b lie within b - 1 to b + 1.
All inputs are finite; a program needn't handle non-finite values.
Results may differ from a plain program's by a relative error of at most 0.007.
Values may be sent and summed in bfloat16 or wider, within the bound.
No kernel may reach another device: no remote copies, remote signals or barrier semaphores. Data moves between devices by JAX's collectives and lax.ppermute only.
A program may use at most 128 MiB of HBM per device.

v0:
```python
import functools

import jax
import jax.numpy as jnp
from jax import lax
from jax.experimental import pallas as pl
from jax.experimental.pallas import tpu as pltpu
from jax.sharding import PartitionSpec as P


SMEM = pl.BlockSpec(memory_space=pltpu.SMEM)
VMEM = pl.BlockSpec(memory_space=pltpu.VMEM)
ANY = pl.BlockSpec(memory_space=pl.ANY)
UNROLL = 8
GROUP = 4
RESIDENT_BYTES = 1600 * 1024


def flip(value, axis, mask):
    pairs = [(source, source ^ mask) for source in range(lax.axis_size(axis))]
    return lax.ppermute(value, axis, pairs)


def contract(left, right, dims):
    return lax.dot_general(
        left, right, (dims, ((), ())), preferred_element_type=jnp.float32
    )


def over_blocks(count, step):
    chunk = UNROLL if count % UNROLL == 0 else 1
    if count == chunk:
        for block in range(count):
            step(block)
        return

    @pl.loop(0, count // chunk)
    def _(outer):
        for inner in range(chunk):
            step(outer * chunk + inner)


def lesser_of(real, imag, sigma_real, sigma_imag):
    left = jnp.concatenate([real, imag], axis=1)
    right = jnp.concatenate(
        [
            jnp.concatenate([sigma_real, sigma_imag], axis=1),
            jnp.concatenate([-sigma_imag, sigma_real], axis=1),
        ],
        axis=0,
    )
    product = contract(left, right, ((1,), (0,))).astype(jnp.bfloat16)
    flipped = jnp.concatenate(
        [
            jnp.concatenate([real, -imag], axis=1),
            jnp.concatenate([imag, real], axis=1),
        ],
        axis=0,
    )
    return contract(product, flipped, ((1,), (1,)))


def bend(coupling_ref, both, bent_ref, block):
    directions, size, _ = coupling_ref.shape
    stacked = coupling_ref[...].reshape(directions * size, size)
    bent = contract(stacked, both, ((1,), (0,))).astype(jnp.bfloat16)
    for direction in range(directions):
        rows = bent[direction * size : (direction + 1) * size]
        bent_ref[block, direction, 0] = rows[:, :size]
        bent_ref[block, direction, 1] = rows[:, size:]


def unbend(place, neighbors_ref, coupling_ref, bent_ref, out_refs):
    directions, size, _ = coupling_ref.shape
    wide = jnp.concatenate([coupling_ref[d] for d in range(directions)], axis=1)
    own = out_refs[0].shape[1]
    for distance, out_ref in enumerate(out_refs):
        for at in range(own):
            block = (place ^ distance) * own + at
            from_d = [neighbors_ref[block, d] for d in range(directions)]
            left = jnp.concatenate(
                [
                    jnp.concatenate(
                        [bent_ref[from_d[d], d, part] for d in range(directions)], axis=1
                    )
                    for part in range(2)
                ],
                axis=0,
            )
            total = contract(left, wide, ((1,), (1,))).astype(jnp.bfloat16)
            out_ref[0, at, 0] = total[:size]
            out_ref[0, at, 1] = total[size:]


def lesser_kernel(first, retarded_ref, sigma_ref, lesser_ref, green, sigma, result, sems):
    count, blocks, _, size, _ = lesser_ref.shape
    items = [(e, b) for e in range(count) for b in range(blocks)]
    loads = [
        (
            pltpu.make_async_copy(retarded_ref.at[first + e, b], green.at[i], sems.at[0, i]),
            pltpu.make_async_copy(sigma_ref.at[first + e, b], sigma.at[i], sems.at[1, i]),
        )
        for i, (e, b) in enumerate(items)
    ]
    for pair in loads:
        for copy in pair:
            copy.start()
    stores = []
    for start in range(0, len(items), GROUP):
        group = range(start, min(start + GROUP, len(items)))
        for i in group:
            for copy in loads[i]:
                copy.wait()
        for i in group:
            both = lesser_of(green[i, 0], green[i, 1], sigma[i, 0], sigma[i, 1])
            both = both.astype(jnp.bfloat16)
            result[i, 0] = both[:, :size]
            result[i, 1] = both[:, size:]
        for i in group:
            store = pltpu.make_async_copy(result.at[i], lesser_ref.at[items[i]], sems.at[2, i])
            store.start()
            stores.append(store)
    for store in stores:
        store.wait()


def lesser(retarded, sigma_in, first, count):
    _, blocks, parts, size, _ = retarded.shape
    slots = pltpu.VMEM((count * blocks, parts, size, size), jnp.bfloat16)
    return pl.pallas_call(
        functools.partial(lesser_kernel, first),
        out_shape=jax.ShapeDtypeStruct((count, blocks, parts, size, size), jnp.bfloat16),
        in_specs=[ANY, ANY],
        out_specs=ANY,
        scratch_shapes=[slots, slots, slots, pltpu.SemaphoreType.DMA((3, count * blocks))],
        cost_estimate=pl.CostEstimate(
            flops=count * blocks * 16 * size**3,
            bytes_accessed=count * blocks * 12 * size**2,
            transcendentals=0,
        ),
        name="lesser",
    )(retarded, sigma_in)


def lesser_couple_kernel(
    place_ref, neighbors_ref, coupling_ref, retarded_ref, sigma_ref, *refs
):
    out_refs, bent_ref = refs[:-1], refs[-1]

    def one(block):
        both = lesser_of(
            retarded_ref[0, block, 0],
            retarded_ref[0, block, 1],
            sigma_ref[0, block, 0],
            sigma_ref[0, block, 1],
        ).astype(jnp.bfloat16)
        bend(coupling_ref, both, bent_ref, block)

    over_blocks(retarded_ref.shape[1], one)
    unbend(place_ref[0], neighbors_ref, coupling_ref, bent_ref, out_refs)


def sum_couple_kernel(
    taken, place_ref, bit_shifts_ref, occupation_ref, neighbors_ref, coupling_ref, *refs
):
    arrived, out_refs, bent_ref = refs[:taken], refs[taken:-1], refs[-1]
    weights = weights_of(taken, bit_shifts_ref, occupation_ref)

    def one(block):
        parts = []
        for part in range(2):
            total = weights[0] * arrived[0][0, block, part].astype(jnp.float32)
            for bit in range(1, taken):
                total += weights[bit] * arrived[bit][0, block, part].astype(jnp.float32)
            parts.append(total.astype(jnp.bfloat16))
        bend(coupling_ref, jnp.concatenate(parts, axis=1), bent_ref, block)

    over_blocks(arrived[0].shape[1], one)
    unbend(place_ref[0], neighbors_ref, coupling_ref, bent_ref, out_refs)


def weights_of(bits, bit_shifts_ref, occupation_ref):
    weights = []
    for bit in range(bits):
        weight = jnp.float32(0)
        for mode in range(bit_shifts_ref.shape[0]):
            weight += jnp.where(bit_shifts_ref[mode] == bit, occupation_ref[mode], 0.0)
        weights.append(weight)
    return weights


def coupled(kernel, scalars, coupling, arrays, first, count, atoms):
    _, blocks, parts, size, _ = arrays[0].shape
    directions = coupling.shape[0]
    own = blocks // atoms
    return pl.pallas_call(
        kernel,
        out_shape=[
            jax.ShapeDtypeStruct((count, own, parts, size, size), jnp.bfloat16)
            for _ in range(atoms)
        ],
        grid=(count,),
        in_specs=[SMEM] * len(scalars)
        + [VMEM]
        + [
            pl.BlockSpec((1, blocks, parts, size, size), lambda e: (first + e, 0, 0, 0, 0))
            for _ in arrays
        ],
        out_specs=[
            pl.BlockSpec((1, own, parts, size, size), lambda e: (e, 0, 0, 0, 0))
            for _ in range(atoms)
        ],
        scratch_shapes=[pltpu.VMEM((blocks, directions, parts, size, size), jnp.bfloat16)],
        cost_estimate=pl.CostEstimate(
            flops=count * blocks * directions * 8 * size**3,
            bytes_accessed=count * blocks * 12 * size**2,
            transcendentals=0,
        ),
    )(*scalars, coupling, *arrays)


def gather_kernel(distances, place_ref, *refs):
    pieces, out_ref, sems = refs[:distances], refs[distances], refs[distances + 1]
    count = pieces[0].shape[0]
    per = out_ref.shape[0] // distances
    copies = []
    for distance, piece in enumerate(pieces):
        rows = pl.ds((place_ref[0] ^ distance) * per, count)
        copies.append(pltpu.make_async_copy(piece, out_ref.at[rows], sems.at[distance]))
        copies[-1].start()
    for copy in copies:
        copy.wait()


def in_vmem(arrays):
    if sum(array.size * array.dtype.itemsize for array in arrays) > RESIDENT_BYTES:
        return arrays
    return [pltpu.with_memory_space_constraint(array, pltpu.VMEM) for array in arrays]


def place_first(place, pieces, energies):
    own = pieces[0].shape[1:]
    return pl.pallas_call(
        functools.partial(gather_kernel, len(pieces)),
        out_shape=jax.ShapeDtypeStruct((len(pieces) * energies, *own), jnp.bfloat16),
        in_specs=[SMEM] + [VMEM] * len(pieces),
        out_specs=ANY,
        scratch_shapes=[pltpu.SemaphoreType.DMA((len(pieces),))],
        name="place_first",
    )(place, *in_vmem(pieces))


def weighted_kernel(
    taken, energies, first, place_ref, bit_shifts_ref, occupation_ref, *refs
):
    arrived, out_ref, result, sems = refs[:taken], *refs[taken + 1 :]
    weights = weights_of(taken, bit_shifts_ref, occupation_ref)
    distances, count = arrived[0].shape[:2]
    stores = []
    for d in range(distances):
        for e in range(count):
            total = weights[0] * arrived[0][d, e].astype(jnp.float32)
            for bit in range(1, taken):
                total += weights[bit] * arrived[bit][d, e].astype(jnp.float32)
            result[d, e] = total.astype(jnp.bfloat16)
            row = (place_ref[0] ^ d) * energies + first + e
            store = pltpu.make_async_copy(result.at[d, e], out_ref.at[row], sems.at[d, e])
            store.start()
            stores.append(store)
    for store in stores:
        store.wait()


def place_second(place, bit_shifts, occupation, arrived, out, energies, first):
    taken = len(arrived)
    return pl.pallas_call(
        functools.partial(weighted_kernel, taken, energies, first),
        out_shape=jax.ShapeDtypeStruct(out.shape, out.dtype),
        in_specs=[SMEM] * 3 + [VMEM] * taken + [ANY],
        out_specs=ANY,
        scratch_shapes=[
            pltpu.VMEM(arrived[0].shape, jnp.bfloat16),
            pltpu.SemaphoreType.DMA(arrived[0].shape[:2]),
        ],
        input_output_aliases={3 + taken: 0},
        name="place_second",
    )(place, bit_shifts, occupation, *in_vmem(arrived), out)


def on_device(retarded, sigma_in, bit_shifts, occupation, neighbors, coupling):
    energies = retarded.shape[0]
    atoms = lax.axis_size("atom")
    bits = lax.axis_size("win").bit_length() - 1
    half = energies // 2
    rest = energies - half
    place = lax.axis_index("atom").astype(jnp.int32).reshape(1)
    lesser_a = lesser(retarded, sigma_in, 0, half)
    arrived_a = {}
    for bit in reversed(range(bits)):
        arrived_a[bit] = flip(lesser_a, "win", 2**bit)

    coupled_b = coupled(
        lesser_couple_kernel, (place, neighbors), coupling, (retarded, sigma_in), half, rest, atoms
    )
    exchanged_b = [coupled_b[0]]
    for distance in range(1, atoms):
        exchanged_b.append(flip(coupled_b[distance], "atom", distance))
    exchanged_b = jnp.stack(exchanged_b)
    arrived_b = {}
    for bit in reversed(range(bits)):
        arrived_b[bit] = flip(exchanged_b, "win", 2**bit)

    coupled_a = coupled(
        functools.partial(sum_couple_kernel, bits),
        (place, bit_shifts, occupation, neighbors),
        coupling,
        tuple(arrived_a[bit] for bit in range(bits)),
        0,
        half,
        atoms,
    )
    exchanged_a = [coupled_a[0]]
    for distance in range(1, atoms):
        exchanged_a.append(flip(coupled_a[distance], "atom", distance))
    out = place_first(place, exchanged_a, energies)
    arrived_b = tuple(arrived_b[bit] for bit in range(bits))
    return place_second(place, bit_shifts, occupation, arrived_b, out, energies, half)


def solution(mesh):
    return jax.shard_map(
        on_device,
        mesh=mesh,
        in_specs=(
            P(("win", "atom"), None, None, None, None),
            P(("win", "atom"), None, None, None, None),
            P(),
            P(),
            P(),
            P(),
        ),
        out_specs=P("win", "atom", None, None, None),
        check_vma=False,
    )
```

profile of v0, /device:TPU:0, one launch (start us, length us, event | category | flops | bytes accessed | tf_op | source)
XLA Modules:
  0.0 64.1 jit_solution(3068658396920031513)
XLA Ops:
  0.0 2.9 %lesser.1 = bf16[1,8,2,128,128]{4,3,2,1,0:T(8,128)(2,1)} custom-call(bf16[2,8,2,128,128]{4,3,2,1,0:T(8,128)(2,1)} %retarded_ref.3, bf16[2,8,2,128,128]{4,3,2,1,0:T(8,128)(2,1)} %sigma_ref.3), custom_call_target="tpu_custom_call" | custom-call | flops 268435456 | bytes 1572864 | tf_op jit(solution)/shard_map/lesser/pallas_call | solution.py:130
  2.9 3.0 %collective-permute-start.6 = (bf16[1,8,2,128,128]{4,3,2,1,0:T(8,128)(2,1)}, bf16[1,8,2,128,128]{4,3,2,1,0:T(8,128)(2,1)S(1)}, u32[]{:S(2)}, u32[]{:S(2)}) collective-permute-start(bf16[1,8,2,128,128]{4,3,2,1,0:T(8,128)(2,1)} %lesser.1), channel_id=1, source_target_pairs={{0,4},{4,0},{8,12},{12,8},{16,20},{20,16},{24,28},{28,24},{1,5},{5... | collective-permute-start | bytes 1572872 | tf_op jit(solution)/shard_map/ppermute | solution.py:21
  6.0 0.7 %copy-done.4 = s32[8,3]{0,1:T(4,128)S(1)} copy-done((s32[8,3]{0,1:T(4,128)S(1)}, s32[8,3]{0,1:T(4,128)}, u32[]{:S(2)}) %copy-start.4) | copy-done | bytes 120
  6.7 0.7 %copy.8.neighbors_ref = s32[8,3]{1,0:T(8,128)} copy(s32[8,3]{0,1:T(4,128)S(1)} %copy-done.4) | data formatting | bytes 192 | tf_op args[4]
  7.3 4.8 %shard_map.64 = (bf16[1,2,2,128,128]{4,3,2,1,0:T(8,128)(2,1)}, bf16[1,2,2,128,128]{4,3,2,1,0:T(8,128)(2,1)}, bf16[1,2,2,128,128]{4,3,2,1,0:T(8,128)(2,1)}, bf16[1,2,2,128,128]{4,3,2,1,0:T(8,128)(2,1)}) custom-call(s32[1]{0:T(128)} %bitcast.place_ref, s32[8,3]{1,0:T(8,128)} %copy.8.neighbors_ref, bf16[3,128,128]{2,1,0:T(8,128)(2,1)} %coupling_ref.3, ...), custom_call_target="tpu_custom_call" | custom-call | flops 402653184 | bytes 1572864 | tf_op jit(solution)/shard_map/pallas_call | solution.py:196
  12.1 0.0 collective-permute-start
  12.2 1.6 %collective-permute-start.7 = (bf16[1,8,2,128,128]{4,3,2,1,0:T(8,128)(2,1)S(1)}, bf16[1,8,2,128,128]{4,3,2,1,0:T(8,128)(2,1)S(1)}, u32[]{:S(2)}, u32[]{:S(2)}) collective-permute-start(bf16[1,8,2,128,128]{4,3,2,1,0:T(8,128)(2,1)S(1)} %copy-done.1), channel_id=1, source_target_pairs={{0,8},{4,12},{8,0},{12,4},{16,24},{20,28},{24,16},{28,20},{1,9},{5... | collective-permute-start | bytes 1572872 | tf_op jit(solution)/shard_map/ppermute | solution.py:21
  13.8 2.6 %collective-permute-start.8 = (bf16[1,8,2,128,128]{4,3,2,1,0:T(8,128)(2,1)S(1)}, bf16[1,8,2,128,128]{4,3,2,1,0:T(8,128)(2,1)}, u32[]{:S(2)}, u32[]{:S(2)}) collective-permute-start(bf16[1,8,2,128,128]{4,3,2,1,0:T(8,128)(2,1)S(1)} %copy-done.1), channel_id=1, source_target_pairs={{0,16},{4,20},{8,24},{12,28},{16,0},{20,4},{24,8},{28,12},{1,17},{... | collective-permute-start | bytes 1572872 | tf_op jit(solution)/shard_map/ppermute | solution.py:21
  16.4 1.5 %collective-permute-start.1 = (bf16[1,2,2,128,128]{4,3,2,1,0:T(8,128)(2,1)}, bf16[1,2,2,128,128]{4,3,2,1,0:T(8,128)(2,1)S(1)}, u32[]{:S(2)}, u32[]{:S(2)}) collective-permute-start(bf16[1,2,2,128,128]{4,3,2,1,0:T(8,128)(2,1)} %get-tuple-element.15), channel_id=1, source_target_pairs={{0,2},{1,3},{2,0},{3,1},{4,6},{5,7},{6,4},{7,5},{8,10},{9,11},{10,... | collective-permute-start | bytes 393224 | tf_op jit(solution)/shard_map/ppermute | solution.py:21
  17.9 0.0 collective-permute-done
  17.9 4.7 %collective-permute-done.1 = bf16[1,2,2,128,128]{4,3,2,1,0:T(8,128)(2,1)S(1)} collective-permute-done((bf16[1,2,2,128,128]{4,3,2,1,0:T(8,128)(2,1)}, bf16[1,2,2,128,128]{4,3,2,1,0:T(8,128)(2,1)S(1)}, u32[]{:S(2)}, u32[]{:S(2)}) %collective-permute-start.1) | collective-permute-done | bytes 131104 | tf_op jit(solution)/shard_map/ppermute | solution.py:21
  22.6 1.3 %collective-permute-done.2 = bf16[1,2,2,128,128]{4,3,2,1,0:T(8,128)(2,1)S(1)} collective-permute-done((bf16[1,2,2,128,128]{4,3,2,1,0:T(8,128)(2,1)}, bf16[1,2,2,128,128]{4,3,2,1,0:T(8,128)(2,1)S(1)}, u32[]{:S(2)}, u32[]{:S(2)}) %collective-permute-start.2) | collective-permute-done | bytes 131104 | tf_op jit(solution)/shard_map/ppermute | solution.py:21
  23.9 1.0 %pad_maximum_fusion = bf16[4,1,2,2,128,128]{5,4,3,2,1,0:T(8,128)(2,1)S(1)} fusion(bf16[1,1,2,2,128,128]{5,4,3,2,1,0:T(8,128)(2,1)S(1)} %bitcast.8, bf16[1,1,2,2,128,128]{5,4,3,2,1,0:T(8,128)(2,1)S(1)} %bitcast.7, bf16[1,1,2,2,128,128]{5,4,3,2,1,0:T(8,128)(2,1)S(1)} %bitcast.6, bf16[1,1,2,2,128,128]{5,4,3,2,1,0:T(8,128)(2,1)} %bitcast.5), kind=kLoop, calls=%fused_computation | loop fusion | flops 786432 | bytes 1048576 | tf_op jit(solution)/shard_map/stack | solution.py:308
  24.9 0.6 collective-permute-start.3
  25.5 0.5 collective-permute-start.4
  25.9 0.0 collective-permute-done.6.refs_0_
  25.9 0.3 collective-permute-start.5
  26.3 11.9 %collective-permute-done.7.refs_1_ = bf16[1,8,2,128,128]{4,3,2,1,0:T(8,128)(2,1)S(1)} collective-permute-done((bf16[1,8,2,128,128]{4,3,2,1,0:T(8,128)(2,1)S(1)}, bf16[1,8,2,128,128]{4,3,2,1,0:T(8,128)(2,1)S(1)}, u32[]{:S(2)}, u32[]{:S(2)}) %collective-permute-start.7) | collective-permute-done | bytes 524320 | tf_op jit(solution)/shard_map/ppermute | solution.py:21
  38.1 0.8 %copy-done.3 = bf16[1,8,2,128,128]{4,3,2,1,0:T(8,128)(2,1)} copy-done((bf16[1,8,2,128,128]{4,3,2,1,0:T(8,128)(2,1)}, bf16[1,8,2,128,128]{4,3,2,1,0:T(8,128)(2,1)S(1)}, u32[]{:S(2)}) %copy-start.3) | copy-done | bytes 524312
  38.9 1.0 %collective-permute-done.8.refs_2_ = bf16[1,8,2,128,128]{4,3,2,1,0:T(8,128)(2,1)} collective-permute-done((bf16[1,8,2,128,128]{4,3,2,1,0:T(8,128)(2,1)S(1)}, bf16[1,8,2,128,128]{4,3,2,1,0:T(8,128)(2,1)}, u32[]{:S(2)}, u32[]{:S(2)}) %collective-permute-start.8) | collective-permute-done | bytes 524320 | tf_op jit(solution)/shard_map/ppermute | solution.py:21
  39.9 3.2 %shard_map.65 = (bf16[1,2,2,128,128]{4,3,2,1,0:T(8,128)(2,1)}, bf16[1,2,2,128,128]{4,3,2,1,0:T(8,128)(2,1)}, bf16[1,2,2,128,128]{4,3,2,1,0:T(8,128)(2,1)}, bf16[1,2,2,128,128]{4,3,2,1,0:T(8,128)(2,1)}) custom-call(s32[1]{0:T(128)} %bitcast.place_ref, s32[3]{0:T(128)} %bit_shifts_ref.3, f32[3]{0:T(128)} %occupation_ref.3, s32[8,3]{1,0:T(8,128)} %copy.8.neighbors_ref, ...), custom_call_target="tpu_custom_call" | custom-call | flops 402653184 | bytes 1572864 | tf_op jit(solution)/shard_map/pallas_call | solution.py:196
  43.2 1.5 %collective-permute-start.10 = (bf16[1,2,2,128,128]{4,3,2,1,0:T(8,128)(2,1)}, bf16[1,2,2,128,128]{4,3,2,1,0:T(8,128)(2,1)S(1)}, u32[]{:S(2)}, u32[]{:S(2)}) collective-permute-start(bf16[1,2,2,128,128]{4,3,2,1,0:T(8,128)(2,1)} %get-tuple-element.19), channel_id=1, source_target_pairs={{0,2},{1,3},{2,0},{3,1},{4,6},{5,7},{6,4},{7,5},{8,10},{9,11},{10,... | collective-permute-start | bytes 393224 | tf_op jit(solution)/shard_map/ppermute | solution.py:21
  44.7 0.0 collective-permute-start.11
  44.7 4.1 %collective-permute-done.10.refs_2_ = bf16[1,2,2,128,128]{4,3,2,1,0:T(8,128)(2,1)S(1)} collective-permute-done((bf16[1,2,2,128,128]{4,3,2,1,0:T(8,128)(2,1)}, bf16[1,2,2,128,128]{4,3,2,1,0:T(8,128)(2,1)S(1)}, u32[]{:S(2)}, u32[]{:S(2)}) %collective-permute-start.10) | collective-permute-done | bytes 131104 | tf_op jit(solution)/shard_map/ppermute | solution.py:21
  48.8 0.0 collective-permute-start.9
  48.8 1.9 %collective-permute-done.11.refs_3_ = bf16[1,2,2,128,128]{4,3,2,1,0:T(8,128)(2,1)S(1)} collective-permute-done((bf16[1,2,2,128,128]{4,3,2,1,0:T(8,128)(2,1)}, bf16[1,2,2,128,128]{4,3,2,1,0:T(8,128)(2,1)S(1)}, u32[]{:S(2)}, u32[]{:S(2)}) %collective-permute-start.11) | collective-permute-done | bytes 131104 | tf_op jit(solution)/shard_map/ppermute | solution.py:21
  50.7 0.0 collective-permute-done.9.refs_1_
  50.7 0.9 %copy-done = bf16[1,2,2,128,128]{4,3,2,1,0:T(8,128)(2,1)S(1)} copy-done((bf16[1,2,2,128,128]{4,3,2,1,0:T(8,128)(2,1)S(1)}, bf16[1,2,2,128,128]{4,3,2,1,0:T(8,128)(2,1)}, u32[]{:S(2)}) %copy-start) | copy-done | bytes 131096
  51.6 0.8 %place_first.1.refs_3_ = bf16[8,2,2,128,128]{4,3,2,1,0:T(8,128)(2,1)} custom-call(s32[1]{0:T(128)} %bitcast.place_ref, bf16[1,2,2,128,128]{4,3,2,1,0:T(8,128)(2,1)S(1)} %copy-done, bf16[1,2,2,128,128]{4,3,2,1,0:T(8,128)(2,1)S(1)} %collective-permute-done.9.refs_1_, bf16[1,2,2,128,128]{4,3,2,1,0:T(8,128)(2,1)S(1)} %collective-permute-done.10.refs_2_, ...), custom_call_target="tpu_custom_call" | custom-call | tf_op jit(solution)/shard_map/place_first/pallas_call | solution.py:243
  52.4 7.6 %collective-permute-done.4.refs_1_ = bf16[4,1,2,2,128,128]{5,4,3,2,1,0:T(8,128)(2,1)S(1)} collective-permute-done((bf16[4,1,2,2,128,128]{5,4,3,2,1,0:T(8,128)(2,1)S(1)}, bf16[4,1,2,2,128,128]{5,4,3,2,1,0:T(8,128)(2,1)S(1)}, u32[]{:S(2)}, u32[]{:S(2)}) %collective-permute-start.4) | collective-permute-done | bytes 524320 | tf_op jit(solution)/shard_map/ppermute | solution.py:21
  60.1 2.4 %collective-permute-done.5.refs_2_ = bf16[4,1,2,2,128,128]{5,4,3,2,1,0:T(8,128)(2,1)S(1)} collective-permute-done((bf16[4,1,2,2,128,128]{5,4,3,2,1,0:T(8,128)(2,1)S(1)}, bf16[4,1,2,2,128,128]{5,4,3,2,1,0:T(8,128)(2,1)S(1)}, u32[]{:S(2)}, u32[]{:S(2)}) %collective-permute-start.5) | collective-permute-done | bytes 524320 | tf_op jit(solution)/shard_map/ppermute | solution.py:21
  62.5 1.7 %place_second.1 = bf16[8,2,2,128,128]{4,3,2,1,0:T(8,128)(2,1)} custom-call(s32[1]{0:T(128)} %bitcast.place_ref, s32[3]{0:T(128)} %bit_shifts_ref.3, f32[3]{0:T(128)} %occupation_ref.3, bf16[4,1,2,2,128,128]{5,4,3,2,1,0:T(8,128)(2,1)S(1)} %collective-permute-done.3.refs_0_, ...), custom_call_target="tpu_custom_call", output_to_operand_aliasing={{}: (6, {})} | custom-call | tf_op jit(solution)/shard_map/place_second/pallas_call | solution.py:276
  (9 shorter events, 0.0 us)
Async XLA Ops:
  2.9 23.0 %collective-permute-start.6 = (bf16[1,8,2,128,128]{4,3,2,1,0:T(8,128)(2,1)}, bf16[1,8,2,128,128]{4,3,2,1,0:T(8,128)(2,1)S(1)}, u32[]{:S(2)}, u32[]{:S(2)}) collective-permute-start(bf16[1,8,2,128,128]{4,3,2,1,0:T(8,128)(2,1)} %lesser.1), channel_id=1, source_target_pairs={{0,4},{4,0},{8,12},{12,8},{16,20},{20,16},{24,28},{28,24},{1,5},{5... | collective-permute-start | bytes 1572872 | tf_op jit(solution)/shard_map/ppermute | solution.py:21
  6.0 0.7 %copy-start.4 = (s32[8,3]{0,1:T(4,128)S(1)}, s32[8,3]{0,1:T(4,128)}, u32[]{:S(2)}) copy-start(s32[8,3]{0,1:T(4,128)} %param.10) | copy-start | bytes 292
  7.3 4.8 %copy-start.1 = (bf16[1,8,2,128,128]{4,3,2,1,0:T(8,128)(2,1)S(1)}, bf16[1,8,2,128,128]{4,3,2,1,0:T(8,128)(2,1)}, u32[]{:S(2)}) copy-start(bf16[1,8,2,128,128]{4,3,2,1,0:T(8,128)(2,1)} %lesser.1) | copy-start | bytes 1572868
  12.1 5.8 %collective-permute-start = (bf16[1,2,2,128,128]{4,3,2,1,0:T(8,128)(2,1)}, bf16[1,2,2,128,128]{4,3,2,1,0:T(8,128)(2,1)S(1)}, u32[]{:S(2)}, u32[]{:S(2)}) collective-permute-start(bf16[1,2,2,128,128]{4,3,2,1,0:T(8,128)(2,1)} %get-tuple-element.14), channel_id=1, source_target_pairs={{0,1},{1,0},{2,3},{3,2},{4,5},{5,4},{6,7},{7,6},{8,9},{9,8},{10,11... | collective-permute-start | bytes 393224 | tf_op jit(solution)/shard_map/ppermute | solution.py:21
  12.2 26.0 %collective-permute-start.7 = (bf16[1,8,2,128,128]{4,3,2,1,0:T(8,128)(2,1)S(1)}, bf16[1,8,2,128,128]{4,3,2,1,0:T(8,128)(2,1)S(1)}, u32[]{:S(2)}, u32[]{:S(2)}) collective-permute-start(bf16[1,8,2,128,128]{4,3,2,1,0:T(8,128)(2,1)S(1)} %copy-done.1), channel_id=1, source_target_pairs={{0,8},{4,12},{8,0},{12,4},{16,24},{20,28},{24,16},{28,20},{1,9},{5... | collective-permute-start | bytes 1572872 | tf_op jit(solution)/shard_map/ppermute | solution.py:21
  13.8 26.1 %collective-permute-start.8 = (bf16[1,8,2,128,128]{4,3,2,1,0:T(8,128)(2,1)S(1)}, bf16[1,8,2,128,128]{4,3,2,1,0:T(8,128)(2,1)}, u32[]{:S(2)}, u32[]{:S(2)}) collective-permute-start(bf16[1,8,2,128,128]{4,3,2,1,0:T(8,128)(2,1)S(1)} %copy-done.1), channel_id=1, source_target_pairs={{0,16},{4,20},{8,24},{12,28},{16,0},{20,4},{24,8},{28,12},{1,17},{... | collective-permute-start | bytes 1572872 | tf_op jit(solution)/shard_map/ppermute | solution.py:21
  16.4 6.3 %collective-permute-start.1 = (bf16[1,2,2,128,128]{4,3,2,1,0:T(8,128)(2,1)}, bf16[1,2,2,128,128]{4,3,2,1,0:T(8,128)(2,1)S(1)}, u32[]{:S(2)}, u32[]{:S(2)}) collective-permute-start(bf16[1,2,2,128,128]{4,3,2,1,0:T(8,128)(2,1)} %get-tuple-element.15), channel_id=1, source_target_pairs={{0,2},{1,3},{2,0},{3,1},{4,6},{5,7},{6,4},{7,5},{8,10},{9,11},{10,... | collective-permute-start | bytes 393224 | tf_op jit(solution)/shard_map/ppermute | solution.py:21
  17.9 6.0 %collective-permute-start.2 = (bf16[1,2,2,128,128]{4,3,2,1,0:T(8,128)(2,1)}, bf16[1,2,2,128,128]{4,3,2,1,0:T(8,128)(2,1)S(1)}, u32[]{:S(2)}, u32[]{:S(2)}) collective-permute-start(bf16[1,2,2,128,128]{4,3,2,1,0:T(8,128)(2,1)} %get-tuple-element.16), channel_id=1, source_target_pairs={{0,3},{1,2},{2,1},{3,0},{4,7},{5,6},{6,5},{7,4},{8,11},{9,10},{10,... | collective-permute-start | bytes 393224 | tf_op jit(solution)/shard_map/ppermute | solution.py:21
  24.9 27.5 %collective-permute-start.3 = (bf16[4,1,2,2,128,128]{5,4,3,2,1,0:T(8,128)(2,1)S(1)}, bf16[4,1,2,2,128,128]{5,4,3,2,1,0:T(8,128)(2,1)S(1)}, u32[]{:S(2)}, u32[]{:S(2)}) collective-permute-start(bf16[4,1,2,2,128,128]{5,4,3,2,1,0:T(8,128)(2,1)S(1)} %pad_maximum_fusion), channel_id=1, source_target_pairs={{0,4},{4,0},{8,12},{12,8},{16,20},{20,16},{24,28},{28,24},{1,5},{5... | collective-permute-start | bytes 1572872 | tf_op jit(solution)/shard_map/ppermute | solution.py:21
  25.5 34.6 %collective-permute-start.4 = (bf16[4,1,2,2,128,128]{5,4,3,2,1,0:T(8,128)(2,1)S(1)}, bf16[4,1,2,2,128,128]{5,4,3,2,1,0:T(8,128)(2,1)S(1)}, u32[]{:S(2)}, u32[]{:S(2)}) collective-permute-start(bf16[4,1,2,2,128,128]{5,4,3,2,1,0:T(8,128)(2,1)S(1)} %pad_maximum_fusion), channel_id=1, source_target_pairs={{0,8},{4,12},{8,0},{12,4},{16,24},{20,28},{24,16},{28,20},{1,9},{5... | collective-permute-start | bytes 1572872 | tf_op jit(solution)/shard_map/ppermute | solution.py:21
  25.9 14.0 %copy-start.2 = (bf16[1,8,2,128,128]{4,3,2,1,0:T(8,128)(2,1)}, bf16[1,8,2,128,128]{4,3,2,1,0:T(8,128)(2,1)S(1)}, u32[]{:S(2)}) copy-start(bf16[1,8,2,128,128]{4,3,2,1,0:T(8,128)(2,1)S(1)} %collective-permute-done.6.refs_0_) | copy-start | bytes 1572868
  25.9 36.5 %collective-permute-start.5 = (bf16[4,1,2,2,128,128]{5,4,3,2,1,0:T(8,128)(2,1)S(1)}, bf16[4,1,2,2,128,128]{5,4,3,2,1,0:T(8,128)(2,1)S(1)}, u32[]{:S(2)}, u32[]{:S(2)}) collective-permute-start(bf16[4,1,2,2,128,128]{5,4,3,2,1,0:T(8,128)(2,1)S(1)} %pad_maximum_fusion), channel_id=1, source_target_pairs={{0,16},{4,20},{8,24},{12,28},{16,0},{20,4},{24,8},{28,12},{1,17},{... | collective-permute-start | bytes 1572872 | tf_op jit(solution)/shard_map/ppermute | solution.py:21
  38.1 0.8 %copy-start.3 = (bf16[1,8,2,128,128]{4,3,2,1,0:T(8,128)(2,1)}, bf16[1,8,2,128,128]{4,3,2,1,0:T(8,128)(2,1)S(1)}, u32[]{:S(2)}) copy-start(bf16[1,8,2,128,128]{4,3,2,1,0:T(8,128)(2,1)S(1)} %collective-permute-done.7.refs_1_) | copy-start | bytes 1572868
  43.2 5.7 %collective-permute-start.10 = (bf16[1,2,2,128,128]{4,3,2,1,0:T(8,128)(2,1)}, bf16[1,2,2,128,128]{4,3,2,1,0:T(8,128)(2,1)S(1)}, u32[]{:S(2)}, u32[]{:S(2)}) collective-permute-start(bf16[1,2,2,128,128]{4,3,2,1,0:T(8,128)(2,1)} %get-tuple-element.19), channel_id=1, source_target_pairs={{0,2},{1,3},{2,0},{3,1},{4,6},{5,7},{6,4},{7,5},{8,10},{9,11},{10,... | collective-permute-start | bytes 393224 | tf_op jit(solution)/shard_map/ppermute | solution.py:21
  44.7 6.0 %collective-permute-start.11 = (bf16[1,2,2,128,128]{4,3,2,1,0:T(8,128)(2,1)}, bf16[1,2,2,128,128]{4,3,2,1,0:T(8,128)(2,1)S(1)}, u32[]{:S(2)}, u32[]{:S(2)}) collective-permute-start(bf16[1,2,2,128,128]{4,3,2,1,0:T(8,128)(2,1)} %get-tuple-element.20), channel_id=1, source_target_pairs={{0,3},{1,2},{2,1},{3,0},{4,7},{5,6},{6,5},{7,4},{8,11},{9,10},{10,... | collective-permute-start | bytes 393224 | tf_op jit(solution)/shard_map/ppermute | solution.py:21
  48.8 1.9 %collective-permute-start.9 = (bf16[1,2,2,128,128]{4,3,2,1,0:T(8,128)(2,1)}, bf16[1,2,2,128,128]{4,3,2,1,0:T(8,128)(2,1)S(1)}, u32[]{:S(2)}, u32[]{:S(2)}) collective-permute-start(bf16[1,2,2,128,128]{4,3,2,1,0:T(8,128)(2,1)} %get-tuple-element.18), channel_id=1, source_target_pairs={{0,1},{1,0},{2,3},{3,2},{4,5},{5,4},{6,7},{7,6},{8,9},{9,8},{10,11... | collective-permute-start | bytes 393224 | tf_op jit(solution)/shard_map/ppermute | solution.py:21
  50.7 0.9 %copy-start = (bf16[1,2,2,128,128]{4,3,2,1,0:T(8,128)(2,1)S(1)}, bf16[1,2,2,128,128]{4,3,2,1,0:T(8,128)(2,1)}, u32[]{:S(2)}) copy-start(bf16[1,2,2,128,128]{4,3,2,1,0:T(8,128)(2,1)} %get-tuple-element.17.refs_0_) | copy-start | bytes 393220
where the time goes:
time: 64.4 us; the launch traced here: 64.1 us
  waiting for transfers between devices  34.9 us (54%)
  Pallas kernels  13.5 us (21%)
  starting transfers between devices  11.7 us (18%)
  local copies, waits for them, and re-layouts  3.06 us (5%)
  other arithmetic  0.97 us (2%)
    ppermute x12, waiting for transfers between devices, flip(): return lax.ppermute(value, axis, pairs)  34.9 us
    ppermute x12, starting transfers between devices, flip(): return lax.ppermute(value, axis, pairs)  11.7 us
    pallas_call x2, Pallas kernels, coupled(): pl.pallas_call(kernel, out_shape=[jax.ShapeDtypeStruct((count, own, parts...  8.04 us
    unnamed x11, local copies, waits for them, and re-layouts  3.06 us
    pallas_call x1, Pallas kernels, lesser(): pl.pallas_call(functools.partial(lesser_kernel, first), out_shape=jax.Sha...  2.94 us
    pallas_call x1, Pallas kernels, place_second(): pl.pallas_call(functools.partial(weighted_kernel, taken, energies, first)...  1.66 us
  transfers between devices with their start and end apart: 12, of which 8 were waited for; matrix products, arithmetic and copies ran while one was open for 3% of the time, Pallas kernels for 14%

commit v1 on v0

v1 whole, which is shorter than its diff:
```python
import functools
import math

import jax
import jax.numpy as jnp
from jax import lax
from jax.experimental import pallas as pl
from jax.experimental.pallas import tpu as pltpu
from jax.sharding import PartitionSpec as P


SMEM = pl.BlockSpec(memory_space=pltpu.SMEM)
VMEM = pl.BlockSpec(memory_space=pltpu.VMEM)
ANY = pl.BlockSpec(memory_space=pl.ANY)
UNROLL = 8
GROUP = 4
RESIDENT_BYTES = 1600 * 1024


def flip(value, axis, mask):
    pairs = [(source, source ^ mask) for source in range(lax.axis_size(axis))]
    return lax.ppermute(value, axis, pairs)


def contract(left, right, dims):
    return lax.dot_general(
        left, right, (dims, ((), ())), preferred_element_type=jnp.float32
    )


def over_blocks(count, step):
    chunk = math.gcd(count, UNROLL)
    if count == chunk:
        for block in range(count):
            step(block)
        return

    @pl.loop(0, count // chunk)
    def _(outer):
        for inner in range(chunk):
            step(outer * chunk + inner)


def kept(shape):
    if math.prod(shape) * 2 > RESIDENT_BYTES // 2:
        return jax.ShapeDtypeStruct(shape, jnp.bfloat16)
    return pltpu.VMEM(shape, jnp.bfloat16)


def in_vmem(arrays):
    if sum(array.size * array.dtype.itemsize for array in arrays) > RESIDENT_BYTES:
        return arrays
    return [pltpu.with_memory_space_constraint(array, pltpu.VMEM) for array in arrays]


def start_loads(first, count, blocks, retarded_ref, sigma_ref, green, sigma, sems):
    loads = []
    for i, (e, b) in enumerate((e, b) for e in range(count) for b in blocks):
        pair = (
            pltpu.make_async_copy(retarded_ref.at[first + e, b], green.at[i], sems.at[0, i]),
            pltpu.make_async_copy(sigma_ref.at[first + e, b], sigma.at[i], sems.at[1, i]),
        )
        for copy in pair:
            copy.start()
        loads.append(pair)
    return loads


def lesser_items(loads, green, sigma):
    for start in range(0, len(loads), GROUP):
        group = range(start, min(start + GROUP, len(loads)))
        for i in group:
            for copy in loads[i]:
                copy.wait()
        for i in group:
            both = lesser_of(green[i, 0], green[i, 1], sigma[i, 0], sigma[i, 1])
            yield i, both.astype(jnp.bfloat16)


def lesser_of(real, imag, sigma_real, sigma_imag):
    left = jnp.concatenate([real, imag], axis=1)
    right = jnp.concatenate(
        [
            jnp.concatenate([sigma_real, sigma_imag], axis=1),
            jnp.concatenate([-sigma_imag, sigma_real], axis=1),
        ],
        axis=0,
    )
    product = contract(left, right, ((1,), (0,))).astype(jnp.bfloat16)
    flipped = jnp.concatenate(
        [
            jnp.concatenate([real, -imag], axis=1),
            jnp.concatenate([imag, real], axis=1),
        ],
        axis=0,
    )
    return contract(product, flipped, ((1,), (1,)))


def bend(coupling_ref, both, bent_ref, block):
    directions, size, _ = coupling_ref.shape
    stacked = coupling_ref[...].reshape(directions * size, size)
    bent = contract(stacked, both, ((1,), (0,))).astype(jnp.bfloat16)
    for direction in range(directions):
        rows = bent[direction * size : (direction + 1) * size]
        bent_ref[block, direction, 0] = rows[:, :size]
        bent_ref[block, direction, 1] = rows[:, size:]


def unbend(place_ref, neighbors_ref, coupling_ref, bent_ref, out_refs, energy):
    directions, size, _ = coupling_ref.shape
    wide = jnp.concatenate([coupling_ref[d] for d in range(directions)], axis=1)
    own = out_refs[0].shape[1]
    for distance, out_ref in enumerate(out_refs):
        for at in range(own):
            block = (place_ref[0] ^ distance) * own + at
            from_d = [neighbors_ref[block, d] for d in range(directions)]
            left = jnp.concatenate(
                [
                    jnp.concatenate(
                        [bent_ref[from_d[d], d, part] for d in range(directions)], axis=1
                    )
                    for part in range(2)
                ],
                axis=0,
            )
            total = contract(left, wide, ((1,), (1,))).astype(jnp.bfloat16)
            out_ref[energy, at, 0] = total[:size]
            out_ref[energy, at, 1] = total[size:]


def lesser_kernel(first, cut, retarded_ref, sigma_ref, lesser_ref, green, sigma, sems):
    count, blocks, _, size, _ = lesser_ref.shape
    loads = start_loads(
        first, count, range(cut, cut + blocks), retarded_ref, sigma_ref, green, sigma, sems
    )
    for i, both in lesser_items(loads, green, sigma):
        for part in range(2):
            lesser_ref[i // blocks, i % blocks, part] = both[:, part * size : (part + 1) * size]


def lesser_rest_kernel(first, *refs):
    retarded_ref, sigma_ref, begun_ref, rest_ref, whole_ref, green, sigma, sems = refs
    count, blocks, _, size, _ = rest_ref.shape
    cut = begun_ref.shape[1]
    loads = start_loads(
        first, count, range(cut, cut + blocks), retarded_ref, sigma_ref, green, sigma, sems
    )
    whole_ref[:, :cut] = begun_ref[...]
    for i, both in lesser_items(loads, green, sigma):
        for part in range(2):
            half = both[:, part * size : (part + 1) * size]
            rest_ref[i // blocks, i % blocks, part] = half
            whole_ref[i // blocks, cut + i % blocks, part] = half


def lesser_scratch(count, blocks, own):
    slots = pltpu.VMEM((count * blocks, *own), jnp.bfloat16)
    return [slots, slots, pltpu.SemaphoreType.DMA((2, count * blocks))]


def lesser_cost(count, blocks, size):
    return pl.CostEstimate(
        flops=count * blocks * 16 * size**3,
        bytes_accessed=count * blocks * 12 * size**2,
        transcendentals=0,
    )


def lesser_begin(retarded, sigma_in, first, count, cut):
    own = retarded.shape[2:]
    return pl.pallas_call(
        functools.partial(lesser_kernel, first, 0),
        out_shape=kept((count, cut, *own)),
        in_specs=[ANY, ANY],
        out_specs=VMEM,
        scratch_shapes=lesser_scratch(count, cut, own),
        cost_estimate=lesser_cost(count, cut, own[-1]),
        name="lesser_begin",
    )(retarded, sigma_in)


def lesser_rest(retarded, sigma_in, begun, first, count):
    blocks, *own = retarded.shape[1:]
    rest = blocks - begun.shape[1]
    return pl.pallas_call(
        functools.partial(lesser_rest_kernel, first),
        out_shape=[kept((count, rest, *own)), kept((count, blocks, *own))],
        in_specs=[ANY, ANY, VMEM],
        out_specs=[VMEM, VMEM],
        scratch_shapes=lesser_scratch(count, rest, own),
        cost_estimate=lesser_cost(count, rest, own[-1]),
        name="lesser_rest",
    )(retarded, sigma_in, *in_vmem([begun]))


def lesser_couple_kernel(first, place_ref, neighbors_ref, coupling_ref, *refs):
    retarded_ref, sigma_ref, *out_refs, bent_ref, green, sigma, sems = refs
    blocks = retarded_ref.shape[1]
    count = out_refs[0].shape[0]
    loads = start_loads(
        first, count, range(blocks), retarded_ref, sigma_ref, green, sigma, sems
    )
    for i, both in lesser_items(loads, green, sigma):
        bend(coupling_ref, both, bent_ref, i % blocks)
        if i % blocks == blocks - 1:
            unbend(place_ref, neighbors_ref, coupling_ref, bent_ref, out_refs, i // blocks)


def lesser_couple(place, neighbors, coupling, retarded, sigma_in, first, count, atoms):
    blocks, *own = retarded.shape[1:]
    directions, size, _ = coupling.shape
    return pl.pallas_call(
        functools.partial(lesser_couple_kernel, first),
        out_shape=[kept((count, blocks // atoms, *own))] * atoms,
        in_specs=[SMEM, SMEM, VMEM, ANY, ANY],
        out_specs=[VMEM] * atoms,
        scratch_shapes=[pltpu.VMEM((blocks, directions, *own), jnp.bfloat16)]
        + lesser_scratch(count, blocks, own),
        cost_estimate=pl.CostEstimate(
            flops=count * blocks * (16 + directions * 8) * size**3,
            bytes_accessed=count * blocks * 12 * size**2,
            transcendentals=0,
        ),
        name="lesser_couple",
    )(place, neighbors, coupling, retarded, sigma_in)


def sum_couple_kernel(
    widths, place_ref, bit_shifts_ref, occupation_ref, neighbors_ref, coupling_ref, *refs
):
    taken = sum(widths)
    arrived, out_refs, bent_ref = list(refs[:taken]), refs[taken:-1], refs[-1]
    terms = [[arrived.pop(0) for _ in range(width)] for width in widths]
    weights = weights_of(len(terms), place_ref, bit_shifts_ref, occupation_ref)
    span = bent_ref.shape[0] // max(widths)
    for piece in range(max(widths)):

        def one(at, piece=piece):
            parts = []
            for part in range(2):
                total = None
                for weight, term in zip(weights, terms):
                    block = at if len(term) > 1 else piece * span + at
                    value = term[piece % len(term)][0, block, part].astype(jnp.float32)
                    total = weight * value if total is None else total + weight * value
                parts.append(total.astype(jnp.bfloat16))
            bend(coupling_ref, jnp.concatenate(parts, axis=1), bent_ref, piece * span + at)

        over_blocks(span, one)
    unbend(place_ref, neighbors_ref, coupling_ref, bent_ref, out_refs, 0)


def sum_couple(scalars, coupling, terms, atoms):
    count, blocks, *own = terms[0][0].shape
    directions = coupling.shape[0]
    arrays = [array for term in terms for array in term]
    return pl.pallas_call(
        functools.partial(sum_couple_kernel, [len(term) for term in terms]),
        out_shape=[
            jax.ShapeDtypeStruct((count, blocks // atoms, *own), jnp.bfloat16)
            for _ in range(atoms)
        ],
        grid=(count,),
        in_specs=[SMEM] * len(scalars)
        + [VMEM]
        + [pl.BlockSpec((1, *array.shape[1:]), lambda e: (e, 0, 0, 0, 0)) for array in arrays],
        out_specs=[
            pl.BlockSpec((1, blocks // atoms, *own), lambda e: (e, 0, 0, 0, 0))
            for _ in range(atoms)
        ],
        scratch_shapes=[pltpu.VMEM((blocks, directions, *own), jnp.bfloat16)],
        cost_estimate=pl.CostEstimate(
            flops=count * blocks * directions * 8 * own[-1] ** 3,
            bytes_accessed=count * blocks * 12 * own[-1] ** 2,
            transcendentals=0,
        ),
        name="sum_couple",
    )(*scalars, coupling, *arrays)


def weights_of(bits, place_ref, bit_shifts_ref, occupation_ref):
    weights = []
    for bit in range(bits):
        weight = jnp.float32(0)
        for mode in range(bit_shifts_ref.shape[0]):
            weight += jnp.where(bit_shifts_ref[mode] == bit, occupation_ref[mode], 0.0)
        weights.append(weight)
    if bits > 1:
        odd = place_ref[1] == 1
        low, high = weights[-2:]
        weights[-2:] = [jnp.where(odd, low, high), jnp.where(odd, high, low)]
    return weights


def gather_kernel(distances, place_ref, *refs):
    pieces, out_ref, sems = refs[:distances], refs[distances], refs[distances + 1]
    count = pieces[0].shape[0]
    per = out_ref.shape[0] // distances
    copies = []
    for distance, piece in enumerate(pieces):
        rows = pl.ds((place_ref[0] ^ distance) * per, count)
        copies.append(pltpu.make_async_copy(piece, out_ref.at[rows], sems.at[distance]))
        copies[-1].start()
    for copy in copies:
        copy.wait()


def place_first(place, pieces, energies):
    own = pieces[0].shape[1:]
    return pl.pallas_call(
        functools.partial(gather_kernel, len(pieces)),
        out_shape=jax.ShapeDtypeStruct((len(pieces) * energies, *own), jnp.bfloat16),
        in_specs=[SMEM] + [VMEM] * len(pieces),
        out_specs=ANY,
        scratch_shapes=[pltpu.SemaphoreType.DMA((len(pieces),))],
        name="place_first",
    )(place, *in_vmem(pieces))


def weighted_kernel(
    taken, energies, first, place_ref, bit_shifts_ref, occupation_ref, *refs
):
    arrived, out_ref, result, sems = refs[:taken], *refs[taken + 1 :]
    weights = weights_of(taken, place_ref, bit_shifts_ref, occupation_ref)
    distances, count = arrived[0].shape[:2]
    stores = []
    for d in range(distances):
        for e in range(count):
            total = weights[0] * arrived[0][d, e].astype(jnp.float32)
            for bit in range(1, taken):
                total += weights[bit] * arrived[bit][d, e].astype(jnp.float32)
            result[d, e] = total.astype(jnp.bfloat16)
            row = (place_ref[0] ^ d) * energies + first + e
            store = pltpu.make_async_copy(result.at[d, e], out_ref.at[row], sems.at[d, e])
            store.start()
            stores.append(store)
    for store in stores:
        store.wait()


def place_second(place, bit_shifts, occupation, arrived, out, energies, first):
    taken = len(arrived)
    return pl.pallas_call(
        functools.partial(weighted_kernel, taken, energies, first),
        out_shape=jax.ShapeDtypeStruct(out.shape, out.dtype),
        in_specs=[SMEM] * 3 + [VMEM] * taken + [ANY],
        out_specs=ANY,
        scratch_shapes=[
            pltpu.VMEM(arrived[0].shape, jnp.bfloat16),
            pltpu.SemaphoreType.DMA(arrived[0].shape[:2]),
        ],
        input_output_aliases={3 + taken: 0},
        name="place_second",
    )(place, bit_shifts, occupation, *in_vmem(arrived), out)


def stack_kernel(distances, *refs):
    pieces, out_ref, sems = refs[:distances], refs[distances], refs[distances + 1]
    copies = []
    for distance, piece in enumerate(pieces):
        copies.append(pltpu.make_async_copy(piece, out_ref.at[distance], sems.at[distance]))
        copies[-1].start()
    for copy in copies:
        copy.wait()


def stack(pieces):
    return pl.pallas_call(
        functools.partial(stack_kernel, len(pieces)),
        out_shape=jax.ShapeDtypeStruct((len(pieces), *pieces[0].shape), jnp.bfloat16),
        in_specs=[VMEM] * len(pieces),
        out_specs=ANY,
        scratch_shapes=[pltpu.SemaphoreType.DMA((len(pieces),))],
        name="stack",
    )(*in_vmem(pieces))


def term_masks(count):
    bits = count.bit_length() - 1
    masks = [(2**bit, 2**bit) for bit in range(bits)]
    if bits > 1:
        low, high = 2 ** (bits - 2), 2 ** (bits - 1)
        masks[-2:] = [(low, high), (high, low)]
    return masks


def oddness(window, count):
    bits = count.bit_length() - 1
    return (window >> (bits - 1) ^ window >> (bits - 2)) & 1 if bits > 1 else window & 0


def exchange(value, term):
    count = lax.axis_size("win")
    masks = term_masks(count)[term]
    pairs = [(source, source ^ masks[oddness(source, count)]) for source in range(count)]
    return lax.ppermute(value, "win", pairs)


def on_device(retarded, sigma_in, bit_shifts, occupation, neighbors, coupling):
    energies, blocks = retarded.shape[:2]
    atoms = lax.axis_size("atom")
    windows = lax.axis_size("win")
    terms = len(term_masks(windows))
    half = energies // 2
    rest = energies - half
    cut = blocks // 2
    place = jnp.stack(
        [lax.axis_index("atom"), oddness(lax.axis_index("win"), windows)]
    ).astype(jnp.int32)
    begun = lesser_begin(retarded, sigma_in, 0, half, cut)
    arrived_begun = exchange(begun, terms - 2)
    ended, lesser_a = lesser_rest(retarded, sigma_in, begun, 0, half)
    arrived_ended = exchange(ended, terms - 2)
    arrived_a = {}
    for term in reversed(range(terms)):
        if term != terms - 2:
            arrived_a[term] = [exchange(lesser_a, term)]
    arrived_a[terms - 2] = [arrived_begun, arrived_ended]

    coupled_b = lesser_couple(place, neighbors, coupling, retarded, sigma_in, half, rest, atoms)
    exchanged_b = [coupled_b[0]]
    for distance in range(1, atoms):
        exchanged_b.append(flip(coupled_b[distance], "atom", distance))
    exchanged_b = stack(exchanged_b)
    arrived_b = {}
    for term in range(terms):
        arrived_b[term] = exchange(exchanged_b, term)

    coupled_a = sum_couple(
        (place, bit_shifts, occupation, neighbors),
        coupling,
        [arrived_a[term] for term in range(terms)],
        atoms,
    )
    exchanged_a = [coupled_a[0]]
    for distance in range(1, atoms):
        exchanged_a.append(flip(coupled_a[distance], "atom", distance))
    out = place_first(place, exchanged_a, energies)
    arrived_b = tuple(arrived_b[term] for term in range(terms))
    return place_second(place, bit_shifts, occupation, arrived_b, out, energies, half)


def solution(mesh):
    return jax.shard_map(
        on_device,
        mesh=mesh,
        in_specs=(
            P(("win", "atom"), None, None, None, None),
            P(("win", "atom"), None, None, None, None),
            P(),
            P(),
            P(),
            P(),
        ),
        out_specs=P("win", "atom", None, None, None),
        check_vma=False,
    )
```

time: 64.4 us -> 64.2 us (level)
  waiting for transfers between devices: 34.9 us -> 27.3 us
  starting transfers between devices: 11.7 us -> 16.3 us
  Pallas kernels: 13.5 us -> 15.7 us
  local copies, waits for them, and re-layouts: 3.06 us -> 3.83 us
    ppermute x12 -> x6, waiting for transfers between devices: 34.9 us -> 13 us  [flip(): return lax.ppermute(value, axis, pairs)]
    ppermute x0 -> x7, waiting for transfers between devices: none -> 14.2 us  [exchange(): return lax.ppermute(value, 'win', pairs)]
    ppermute x0 -> x7, starting transfers between devices: none -> 11.2 us  [exchange(): return lax.ppermute(value, 'win', pairs)]
    ppermute x12 -> x6, starting transfers between devices: 11.7 us -> 5.1 us  [flip(): return lax.ppermute(value, axis, pairs)]
    pallas_call x3 -> x5, Pallas kernels: 11 us -> 12.5 us  [the longest x1 5.25 us: lesser_couple(): pl.pallas_call(functools.partial(lesser_couple_kernel, first), out_shape=...]
    unnamed x11, local copies, waits for them, and re-layouts: 3.06 us -> 3.83 us
    pallas_call x1, Pallas kernels: 0.82 us -> 1.48 us  [place_first(): pl.pallas_call(functools.partial(gather_kernel, len(pieces)), out_shape=j...]
  transfers between devices with their start and end apart: 12 -> 13, of which waited for: 8 -> 7; matrix products, arithmetic and copies ran while one was open for 3% -> 0% of each run, Pallas kernels for 14% -> 14%
where the time goes in v1:
time: 64.2 us; the launch traced here: 63.8 us
  waiting for transfers between devices  27.3 us (43%)
  starting transfers between devices  16.3 us (25%)
  Pallas kernels  15.7 us (24%)
  local copies, waits for them, and re-layouts  3.83 us (6%)
  other arithmetic  0.65 us (1%)
    ppermute x7, waiting for transfers between devices, exchange(): return lax.ppermute(value, 'win', pairs)  14.2 us
    ppermute x6, waiting for transfers between devices, flip(): return lax.ppermute(value, axis, pairs)  13 us
    ppermute x7, starting transfers between devices, exchange(): return lax.ppermute(value, 'win', pairs)  11.2 us
    pallas_call x1, Pallas kernels, lesser_couple(): pl.pallas_call(functools.partial(lesser_couple_kernel, first), out_shape=...  5.25 us
    ppermute x6, starting transfers between devices, flip(): return lax.ppermute(value, axis, pairs)  5.1 us
    unnamed x11, local copies, waits for them, and re-layouts  3.83 us
    pallas_call x1, Pallas kernels, sum_couple(): pl.pallas_call(functools.partial(sum_couple_kernel, [len(term) for term i...  3.22 us
    pallas_call x1, Pallas kernels, place_second(): pl.pallas_call(functools.partial(weighted_kernel, taken, energies, first)...  1.67 us
  transfers between devices with their start and end apart: 13, of which 7 were waited for; matrix products, arithmetic and copies ran while one was open for 0% of the time, Pallas kernels for 14%

profile of v1, /device:TPU:0, one launch (start us, length us, event | category | flops | bytes accessed | tf_op | source)
XLA Modules:
  0.0 63.8 jit_solution(17057751784054630433)
XLA Ops:
  0.0 0.7 %copy-done.4 = s32[8,3]{0,1:T(4,128)S(1)} copy-done((s32[8,3]{0,1:T(4,128)S(1)}, s32[8,3]{0,1:T(4,128)}, u32[]{:S(2)}) %copy-start.4) | copy-done | bytes 120
  0.7 0.7 %copy.8.neighbors_ref = s32[8,3]{1,0:T(8,128)} copy(s32[8,3]{0,1:T(4,128)S(1)} %copy-done.4) | data formatting | bytes 192 | tf_op args[4]
  1.4 0.6 %pad_add_fusion.place_ref = s32[2]{0:T(128)} fusion(s32[1]{0:T(128)} %bitcast.1, s32[1]{0:T(128)} %bitcast), kind=kLoop, calls=%fused_computation | loop fusion | flops 2 | bytes 16 | tf_op jit(solution)/shard_map/stack | solution.py:408
  2.0 5.2 %lesser_couple.1 = (bf16[1,2,2,128,128]{4,3,2,1,0:T(8,128)(2,1)S(1)}, bf16[1,2,2,128,128]{4,3,2,1,0:T(8,128)(2,1)S(1)}, bf16[1,2,2,128,128]{4,3,2,1,0:T(8,128)(2,1)S(1)}, bf16[1,2,2,128,128]{4,3,2,1,0:T(8,128)(2,1)S(1)}) custom-call(s32[2]{0:T(128)} %pad_add_fusion.place_ref, s32[8,3]{1,0:T(8,128)} %copy.8.neighbors_ref, bf16[3,128,128]{2,1,0:T(8,128)(2,1)} %coupling_ref.3, ...), custom_call_target="tpu_custom_call" | custom-call | flops 671088640 | bytes 1572864 | tf_op jit(solution)/shard_map/lesser_couple/pallas_call | solution.py:213
  7.3 0.6 collective-permute-start
  7.8 1.6 %lesser_begin.1.refs_2_ = bf16[1,4,2,128,128]{4,3,2,1,0:T(8,128)(2,1)S(1)} custom-call(bf16[2,8,2,128,128]{4,3,2,1,0:T(8,128)(2,1)} %refs_0_.3, bf16[2,8,2,128,128]{4,3,2,1,0:T(8,128)(2,1)} %refs_1_.3), custom_call_target="tpu_custom_call" | custom-call | flops 134217728 | bytes 786432 | tf_op jit(solution)/shard_map/lesser_begin/pallas_call | solution.py:172
  9.4 1.6 %lesser_rest.1 = (bf16[1,4,2,128,128]{4,3,2,1,0:T(8,128)(2,1)S(1)}, bf16[1,8,2,128,128]{4,3,2,1,0:T(8,128)(2,1)S(1)}) custom-call(bf16[2,8,2,128,128]{4,3,2,1,0:T(8,128)(2,1)} %refs_0_.3, bf16[2,8,2,128,128]{4,3,2,1,0:T(8,128)(2,1)} %refs_1_.3, bf16[1,4,2,128,128]{4,3,2,1,0:T(8,128)(2,1)S(1)} %lesser_begin.1.refs_2_), custom_call_target="tpu_custom_call" | custom-call | flops 134217728 | bytes 786432 | tf_op jit(solution)/shard_map/lesser_rest/pallas_call | solution.py:186
  11.1 3.6 %collective-permute-start.9 = (bf16[1,8,2,128,128]{4,3,2,1,0:T(8,128)(2,1)S(1)}, bf16[1,8,2,128,128]{4,3,2,1,0:T(8,128)(2,1)S(1)}, u32[]{:S(2)}, u32[]{:S(2)}) collective-permute-start(bf16[1,8,2,128,128]{4,3,2,1,0:T(8,128)(2,1)S(1)} %get-tuple-element.19), channel_id=1, source_target_pairs={{0,16},{4,20},{8,0},{12,4},{16,24},{20,28},{24,8},{28,12},{1,17},{... | collective-permute-start | bytes 1572872 | tf_op jit(solution)/shard_map/ppermute | solution.py:397
  14.7 1.5 %collective-permute-start.6 = (bf16[1,8,2,128,128]{4,3,2,1,0:T(8,128)(2,1)S(1)}, bf16[1,8,2,128,128]{4,3,2,1,0:T(8,128)(2,1)S(1)}, u32[]{:S(2)}, u32[]{:S(2)}) collective-permute-start(bf16[1,8,2,128,128]{4,3,2,1,0:T(8,128)(2,1)S(1)} %get-tuple-element.19), channel_id=1, source_target_pairs={{0,4},{4,0},{8,12},{12,8},{16,20},{20,16},{24,28},{28,24},{1,5},{5... | collective-permute-start | bytes 1572872 | tf_op jit(solution)/shard_map/ppermute | solution.py:397
  16.2 1.5 %collective-permute-start.1 = (bf16[1,2,2,128,128]{4,3,2,1,0:T(8,128)(2,1)S(1)}, bf16[1,2,2,128,128]{4,3,2,1,0:T(8,128)(2,1)S(1)}, u32[]{:S(2)}, u32[]{:S(2)}) collective-permute-start(bf16[1,2,2,128,128]{4,3,2,1,0:T(8,128)(2,1)S(1)} %get-tuple-element.17), channel_id=1, source_target_pairs={{0,2},{1,3},{2,0},{3,1},{4,6},{5,7},{6,4},{7,5},{8,10},{9,11},{10,... | collective-permute-start | bytes 393224 | tf_op jit(solution)/shard_map/ppermute | solution.py:22
  17.7 1.9 %collective-permute-start.8 = (bf16[1,4,2,128,128]{4,3,2,1,0:T(8,128)(2,1)S(1)}, bf16[1,4,2,128,128]{4,3,2,1,0:T(8,128)(2,1)}, u32[]{:S(2)}, u32[]{:S(2)}) collective-permute-start(bf16[1,4,2,128,128]{4,3,2,1,0:T(8,128)(2,1)S(1)} %get-tuple-element.20), channel_id=1, source_target_pairs={{0,8},{4,12},{8,24},{12,28},{16,0},{20,4},{24,16},{28,20},{1,9},{5... | collective-permute-start | bytes 786440 | tf_op jit(solution)/shard_map/ppermute | solution.py:397
  19.6 1.9 %collective-permute-done.1.refs_2_ = bf16[1,2,2,128,128]{4,3,2,1,0:T(8,128)(2,1)S(1)} collective-permute-done((bf16[1,2,2,128,128]{4,3,2,1,0:T(8,128)(2,1)S(1)}, bf16[1,2,2,128,128]{4,3,2,1,0:T(8,128)(2,1)S(1)}, u32[]{:S(2)}, u32[]{:S(2)}) %collective-permute-start.1) | collective-permute-done | bytes 131104 | tf_op jit(solution)/shard_map/ppermute | solution.py:22
  21.5 0.2 collective-permute-start.2
  21.7 5.5 %collective-permute-done.2.refs_3_ = bf16[1,2,2,128,128]{4,3,2,1,0:T(8,128)(2,1)S(1)} collective-permute-done((bf16[1,2,2,128,128]{4,3,2,1,0:T(8,128)(2,1)S(1)}, bf16[1,2,2,128,128]{4,3,2,1,0:T(8,128)(2,1)S(1)}, u32[]{:S(2)}, u32[]{:S(2)}) %collective-permute-start.2) | collective-permute-done | bytes 131104 | tf_op jit(solution)/shard_map/ppermute | solution.py:22
  27.3 0.8 %stack.13 = bf16[4,1,2,2,128,128]{5,4,3,2,1,0:T(8,128)(2,1)} custom-call(bf16[1,2,2,128,128]{4,3,2,1,0:T(8,128)(2,1)S(1)} %get-tuple-element.15.refs_0_, bf16[1,2,2,128,128]{4,3,2,1,0:T(8,128)(2,1)S(1)} %collective-permute-done.refs_1_, bf16[1,2,2,128,128]{4,3,2,1,0:T(8,128)(2,1)S(1)} %collective-permute-done.1.refs_2_, ...), custom_call_target="tpu_custom_call" | custom-call | tf_op jit(solution)/shard_map/stack/pallas_call | solution.py:369
  28.1 1.6 %collective-permute-start.5 = (bf16[4,1,2,2,128,128]{5,4,3,2,1,0:T(8,128)(2,1)}, bf16[4,1,2,2,128,128]{5,4,3,2,1,0:T(8,128)(2,1)S(1)}, u32[]{:S(2)}, u32[]{:S(2)}) collective-permute-start(bf16[4,1,2,2,128,128]{5,4,3,2,1,0:T(8,128)(2,1)} %stack.13), channel_id=1, source_target_pairs={{0,16},{4,20},{8,0},{12,4},{16,24},{20,28},{24,8},{28,12},{1,17},{... | collective-permute-start | bytes 1572872 | tf_op jit(solution)/shard_map/ppermute | solution.py:397
  29.7 4.4 %collective-permute-done.7.refs_1_ = bf16[1,4,2,128,128]{4,3,2,1,0:T(8,128)(2,1)S(1)} collective-permute-done((bf16[1,4,2,128,128]{4,3,2,1,0:T(8,128)(2,1)S(1)}, bf16[1,4,2,128,128]{4,3,2,1,0:T(8,128)(2,1)S(1)}, u32[]{:S(2)}, u32[]{:S(2)}) %collective-permute-start.7) | collective-permute-done | bytes 262176 | tf_op jit(solution)/shard_map/ppermute | solution.py:397
  34.2 1.0 %collective-permute-start.4 = (bf16[4,1,2,2,128,128]{5,4,3,2,1,0:T(8,128)(2,1)}, bf16[4,1,2,2,128,128]{5,4,3,2,1,0:T(8,128)(2,1)S(1)}, u32[]{:S(2)}, u32[]{:S(2)}) collective-permute-start(bf16[4,1,2,2,128,128]{5,4,3,2,1,0:T(8,128)(2,1)} %stack.13), channel_id=1, source_target_pairs={{0,8},{4,12},{8,24},{12,28},{16,0},{20,4},{24,16},{28,20},{1,9},{5... | collective-permute-start | bytes 1572872 | tf_op jit(solution)/shard_map/ppermute | solution.py:397
  35.2 5.1 %collective-permute-done.8.refs_2_ = bf16[1,4,2,128,128]{4,3,2,1,0:T(8,128)(2,1)} collective-permute-done((bf16[1,4,2,128,128]{4,3,2,1,0:T(8,128)(2,1)S(1)}, bf16[1,4,2,128,128]{4,3,2,1,0:T(8,128)(2,1)}, u32[]{:S(2)}, u32[]{:S(2)}) %collective-permute-start.8) | collective-permute-done | bytes 262176 | tf_op jit(solution)/shard_map/ppermute | solution.py:397
  40.3 1.5 %collective-permute-start.3 = (bf16[4,1,2,2,128,128]{5,4,3,2,1,0:T(8,128)(2,1)}, bf16[4,1,2,2,128,128]{5,4,3,2,1,0:T(8,128)(2,1)S(1)}, u32[]{:S(2)}, u32[]{:S(2)}) collective-permute-start(bf16[4,1,2,2,128,128]{5,4,3,2,1,0:T(8,128)(2,1)} %stack.13), channel_id=1, source_target_pairs={{0,4},{4,0},{8,12},{12,8},{16,20},{20,16},{24,28},{28,24},{1,5},{5... | collective-permute-start | bytes 1572872 | tf_op jit(solution)/shard_map/ppermute | solution.py:397
  41.8 0.0 collective-permute-done.9.refs_3_
  41.8 0.8 %copy-done.1 = bf16[1,8,2,128,128]{4,3,2,1,0:T(8,128)(2,1)} copy-done((bf16[1,8,2,128,128]{4,3,2,1,0:T(8,128)(2,1)}, bf16[1,8,2,128,128]{4,3,2,1,0:T(8,128)(2,1)S(1)}, u32[]{:S(2)}) %copy-start.1) | copy-done | bytes 524312
  42.6 0.8 %copy-done.2 = bf16[1,8,2,128,128]{4,3,2,1,0:T(8,128)(2,1)} copy-done((bf16[1,8,2,128,128]{4,3,2,1,0:T(8,128)(2,1)}, bf16[1,8,2,128,128]{4,3,2,1,0:T(8,128)(2,1)S(1)}, u32[]{:S(2)}) %copy-start.2) | copy-done | bytes 524312
  43.4 3.2 %sum_couple.1 = (bf16[1,2,2,128,128]{4,3,2,1,0:T(8,128)(2,1)}, bf16[1,2,2,128,128]{4,3,2,1,0:T(8,128)(2,1)}, bf16[1,2,2,128,128]{4,3,2,1,0:T(8,128)(2,1)}, bf16[1,2,2,128,128]{4,3,2,1,0:T(8,128)(2,1)}) custom-call(s32[2]{0:T(128)} %pad_add_fusion.place_ref, s32[3]{0:T(128)} %bit_shifts_ref.3, f32[3]{0:T(128)} %occupation_ref.3, s32[8,3]{1,0:T(8,128)} %copy.8.neighbors_ref, ...), custom_call_target="tpu_custom_call" | custom-call | flops 402653184 | bytes 1572864 | tf_op jit(solution)/shard_map/sum_couple/pallas_call | solution.py:258
  46.6 1.6 %collective-permute-start.11 = (bf16[1,2,2,128,128]{4,3,2,1,0:T(8,128)(2,1)}, bf16[1,2,2,128,128]{4,3,2,1,0:T(8,128)(2,1)S(1)}, u32[]{:S(2)}, u32[]{:S(2)}) collective-permute-start(bf16[1,2,2,128,128]{4,3,2,1,0:T(8,128)(2,1)} %get-tuple-element.23), channel_id=1, source_target_pairs={{0,2},{1,3},{2,0},{3,1},{4,6},{5,7},{6,4},{7,5},{8,10},{9,11},{10,... | collective-permute-start | bytes 393224 | tf_op jit(solution)/shard_map/ppermute | solution.py:22
  48.2 1.3 %collective-permute-start.12 = (bf16[1,2,2,128,128]{4,3,2,1,0:T(8,128)(2,1)}, bf16[1,2,2,128,128]{4,3,2,1,0:T(8,128)(2,1)S(1)}, u32[]{:S(2)}, u32[]{:S(2)}) collective-permute-start(bf16[1,2,2,128,128]{4,3,2,1,0:T(8,128)(2,1)} %get-tuple-element.24), channel_id=1, source_target_pairs={{0,3},{1,2},{2,1},{3,0},{4,7},{5,6},{6,5},{7,4},{8,11},{9,10},{10,... | collective-permute-start | bytes 393224 | tf_op jit(solution)/shard_map/ppermute | solution.py:22
  49.5 3.8 %collective-permute-done.11.refs_2_ = bf16[1,2,2,128,128]{4,3,2,1,0:T(8,128)(2,1)S(1)} collective-permute-done((bf16[1,2,2,128,128]{4,3,2,1,0:T(8,128)(2,1)}, bf16[1,2,2,128,128]{4,3,2,1,0:T(8,128)(2,1)S(1)}, u32[]{:S(2)}, u32[]{:S(2)}) %collective-permute-start.11) | collective-permute-done | bytes 131104 | tf_op jit(solution)/shard_map/ppermute | solution.py:22
  53.2 1.8 %collective-permute-done.12.refs_3_ = bf16[1,2,2,128,128]{4,3,2,1,0:T(8,128)(2,1)S(1)} collective-permute-done((bf16[1,2,2,128,128]{4,3,2,1,0:T(8,128)(2,1)}, bf16[1,2,2,128,128]{4,3,2,1,0:T(8,128)(2,1)S(1)}, u32[]{:S(2)}, u32[]{:S(2)}) %collective-permute-start.12) | collective-permute-done | bytes 131104 | tf_op jit(solution)/shard_map/ppermute | solution.py:22
  55.0 0.9 %copy-done = bf16[1,2,2,128,128]{4,3,2,1,0:T(8,128)(2,1)S(1)} copy-done((bf16[1,2,2,128,128]{4,3,2,1,0:T(8,128)(2,1)S(1)}, bf16[1,2,2,128,128]{4,3,2,1,0:T(8,128)(2,1)}, u32[]{:S(2)}) %copy-start) | copy-done | bytes 131096
  56.0 1.5 %place_first.1.refs_3_ = bf16[8,2,2,128,128]{4,3,2,1,0:T(8,128)(2,1)} custom-call(s32[2]{0:T(128)} %pad_add_fusion.place_ref, bf16[1,2,2,128,128]{4,3,2,1,0:T(8,128)(2,1)S(1)} %copy-done, bf16[1,2,2,128,128]{4,3,2,1,0:T(8,128)(2,1)S(1)} %collective-permute-done.10.refs_1_, bf16[1,2,2,128,128]{4,3,2,1,0:T(8,128)(2,1)S(1)} %collective-permute-done.11.refs_2_, ...), custom_call_target="tpu_custom_call" | custom-call | tf_op jit(solution)/shard_map/place_first/pallas_call | solution.py:311
  57.5 4.6 %collective-permute-done.4.refs_1_ = bf16[4,1,2,2,128,128]{5,4,3,2,1,0:T(8,128)(2,1)S(1)} collective-permute-done((bf16[4,1,2,2,128,128]{5,4,3,2,1,0:T(8,128)(2,1)}, bf16[4,1,2,2,128,128]{5,4,3,2,1,0:T(8,128)(2,1)S(1)}, u32[]{:S(2)}, u32[]{:S(2)}) %collective-permute-start.4) | collective-permute-done | bytes 524320 | tf_op jit(solution)/shard_map/ppermute | solution.py:397
  62.1 1.7 %place_second.1 = bf16[8,2,2,128,128]{4,3,2,1,0:T(8,128)(2,1)} custom-call(s32[2]{0:T(128)} %pad_add_fusion.place_ref, s32[3]{0:T(128)} %bit_shifts_ref.3, f32[3]{0:T(128)} %occupation_ref.3, bf16[4,1,2,2,128,128]{5,4,3,2,1,0:T(8,128)(2,1)S(1)} %collective-permute-done.3.refs_0_, ...), custom_call_target="tpu_custom_call", output_to_operand_aliasing={{}: (6, {})} | custom-call | tf_op jit(solution)/shard_map/place_second/pallas_call | solution.py:344
  (13 shorter events, 0.0 us)
Async XLA Ops:
  0.0 0.7 %copy-start.4 = (s32[8,3]{0,1:T(4,128)S(1)}, s32[8,3]{0,1:T(4,128)}, u32[]{:S(2)}) copy-start(s32[8,3]{0,1:T(4,128)} %param.10) | copy-start | bytes 292
  7.3 10.5 %collective-permute-start = (bf16[1,2,2,128,128]{4,3,2,1,0:T(8,128)(2,1)S(1)}, bf16[1,2,2,128,128]{4,3,2,1,0:T(8,128)(2,1)S(1)}, u32[]{:S(2)}, u32[]{:S(2)}) collective-permute-start(bf16[1,2,2,128,128]{4,3,2,1,0:T(8,128)(2,1)S(1)} %get-tuple-element.16), channel_id=1, source_target_pairs={{0,1},{1,0},{2,3},{3,2},{4,5},{5,4},{6,7},{7,6},{8,9},{9,8},{10,11... | collective-permute-start | bytes 393224 | tf_op jit(solution)/shard_map/ppermute | solution.py:22
  11.1 30.7 %collective-permute-start.9 = (bf16[1,8,2,128,128]{4,3,2,1,0:T(8,128)(2,1)S(1)}, bf16[1,8,2,128,128]{4,3,2,1,0:T(8,128)(2,1)S(1)}, u32[]{:S(2)}, u32[]{:S(2)}) collective-permute-start(bf16[1,8,2,128,128]{4,3,2,1,0:T(8,128)(2,1)S(1)} %get-tuple-element.19), channel_id=1, source_target_pairs={{0,16},{4,20},{8,0},{12,4},{16,24},{20,28},{24,8},{28,12},{1,17},{... | collective-permute-start | bytes 1572872 | tf_op jit(solution)/shard_map/ppermute | solution.py:397
  14.7 27.1 %collective-permute-start.6 = (bf16[1,8,2,128,128]{4,3,2,1,0:T(8,128)(2,1)S(1)}, bf16[1,8,2,128,128]{4,3,2,1,0:T(8,128)(2,1)S(1)}, u32[]{:S(2)}, u32[]{:S(2)}) collective-permute-start(bf16[1,8,2,128,128]{4,3,2,1,0:T(8,128)(2,1)S(1)} %get-tuple-element.19), channel_id=1, source_target_pairs={{0,4},{4,0},{8,12},{12,8},{16,20},{20,16},{24,28},{28,24},{1,5},{5... | collective-permute-start | bytes 1572872 | tf_op jit(solution)/shard_map/ppermute | solution.py:397
  16.2 5.3 %collective-permute-start.1 = (bf16[1,2,2,128,128]{4,3,2,1,0:T(8,128)(2,1)S(1)}, bf16[1,2,2,128,128]{4,3,2,1,0:T(8,128)(2,1)S(1)}, u32[]{:S(2)}, u32[]{:S(2)}) collective-permute-start(bf16[1,2,2,128,128]{4,3,2,1,0:T(8,128)(2,1)S(1)} %get-tuple-element.17), channel_id=1, source_target_pairs={{0,2},{1,3},{2,0},{3,1},{4,6},{5,7},{6,4},{7,5},{8,10},{9,11},{10,... | collective-permute-start | bytes 393224 | tf_op jit(solution)/shard_map/ppermute | solution.py:22
  17.7 16.4 %collective-permute-start.7 = (bf16[1,4,2,128,128]{4,3,2,1,0:T(8,128)(2,1)S(1)}, bf16[1,4,2,128,128]{4,3,2,1,0:T(8,128)(2,1)S(1)}, u32[]{:S(2)}, u32[]{:S(2)}) collective-permute-start(bf16[1,4,2,128,128]{4,3,2,1,0:T(8,128)(2,1)S(1)} %lesser_begin.1.refs_2_), channel_id=1, source_target_pairs={{0,8},{4,12},{8,24},{12,28},{16,0},{20,4},{24,16},{28,20},{1,9},{5... | collective-permute-start | bytes 786440 | tf_op jit(solution)/shard_map/ppermute | solution.py:397
  17.7 22.6 %collective-permute-start.8 = (bf16[1,4,2,128,128]{4,3,2,1,0:T(8,128)(2,1)S(1)}, bf16[1,4,2,128,128]{4,3,2,1,0:T(8,128)(2,1)}, u32[]{:S(2)}, u32[]{:S(2)}) collective-permute-start(bf16[1,4,2,128,128]{4,3,2,1,0:T(8,128)(2,1)S(1)} %get-tuple-element.20), channel_id=1, source_target_pairs={{0,8},{4,12},{8,24},{12,28},{16,0},{20,4},{24,16},{28,20},{1,9},{5... | collective-permute-start | bytes 786440 | tf_op jit(solution)/shard_map/ppermute | solution.py:397
  21.5 5.7 %collective-permute-start.2 = (bf16[1,2,2,128,128]{4,3,2,1,0:T(8,128)(2,1)S(1)}, bf16[1,2,2,128,128]{4,3,2,1,0:T(8,128)(2,1)S(1)}, u32[]{:S(2)}, u32[]{:S(2)}) collective-permute-start(bf16[1,2,2,128,128]{4,3,2,1,0:T(8,128)(2,1)S(1)} %get-tuple-element.18), channel_id=1, source_target_pairs={{0,3},{1,2},{2,1},{3,0},{4,7},{5,6},{6,5},{7,4},{8,11},{9,10},{10,... | collective-permute-start | bytes 393224 | tf_op jit(solution)/shard_map/ppermute | solution.py:22
  28.1 29.4 %collective-permute-start.5 = (bf16[4,1,2,2,128,128]{5,4,3,2,1,0:T(8,128)(2,1)}, bf16[4,1,2,2,128,128]{5,4,3,2,1,0:T(8,128)(2,1)S(1)}, u32[]{:S(2)}, u32[]{:S(2)}) collective-permute-start(bf16[4,1,2,2,128,128]{5,4,3,2,1,0:T(8,128)(2,1)} %stack.13), channel_id=1, source_target_pairs={{0,16},{4,20},{8,0},{12,4},{16,24},{20,28},{24,8},{28,12},{1,17},{... | collective-permute-start | bytes 1572872 | tf_op jit(solution)/shard_map/ppermute | solution.py:397
  34.2 7.7 %copy-start.3 = (bf16[1,4,2,128,128]{4,3,2,1,0:T(8,128)(2,1)}, bf16[1,4,2,128,128]{4,3,2,1,0:T(8,128)(2,1)S(1)}, u32[]{:S(2)}) copy-start(bf16[1,4,2,128,128]{4,3,2,1,0:T(8,128)(2,1)S(1)} %collective-permute-done.7.refs_1_) | copy-start | bytes 786436
  34.2 27.9 %collective-permute-start.4 = (bf16[4,1,2,2,128,128]{5,4,3,2,1,0:T(8,128)(2,1)}, bf16[4,1,2,2,128,128]{5,4,3,2,1,0:T(8,128)(2,1)S(1)}, u32[]{:S(2)}, u32[]{:S(2)}) collective-permute-start(bf16[4,1,2,2,128,128]{5,4,3,2,1,0:T(8,128)(2,1)} %stack.13), channel_id=1, source_target_pairs={{0,8},{4,12},{8,24},{12,28},{16,0},{20,4},{24,16},{28,20},{1,9},{5... | collective-permute-start | bytes 1572872 | tf_op jit(solution)/shard_map/ppermute | solution.py:397
  40.3 21.8 %collective-permute-start.3 = (bf16[4,1,2,2,128,128]{5,4,3,2,1,0:T(8,128)(2,1)}, bf16[4,1,2,2,128,128]{5,4,3,2,1,0:T(8,128)(2,1)S(1)}, u32[]{:S(2)}, u32[]{:S(2)}) collective-permute-start(bf16[4,1,2,2,128,128]{5,4,3,2,1,0:T(8,128)(2,1)} %stack.13), channel_id=1, source_target_pairs={{0,4},{4,0},{8,12},{12,8},{16,20},{20,16},{24,28},{28,24},{1,5},{5... | collective-permute-start | bytes 1572872 | tf_op jit(solution)/shard_map/ppermute | solution.py:397
  41.8 0.8 %copy-start.1 = (bf16[1,8,2,128,128]{4,3,2,1,0:T(8,128)(2,1)}, bf16[1,8,2,128,128]{4,3,2,1,0:T(8,128)(2,1)S(1)}, u32[]{:S(2)}) copy-start(bf16[1,8,2,128,128]{4,3,2,1,0:T(8,128)(2,1)S(1)} %collective-permute-done.9.refs_3_) | copy-start | bytes 1572868
  42.6 0.8 %copy-start.2 = (bf16[1,8,2,128,128]{4,3,2,1,0:T(8,128)(2,1)}, bf16[1,8,2,128,128]{4,3,2,1,0:T(8,128)(2,1)S(1)}, u32[]{:S(2)}) copy-start(bf16[1,8,2,128,128]{4,3,2,1,0:T(8,128)(2,1)S(1)} %collective-permute-done.6.refs_0_) | copy-start | bytes 1572868
  46.6 1.6 %collective-permute-start.10 = (bf16[1,2,2,128,128]{4,3,2,1,0:T(8,128)(2,1)}, bf16[1,2,2,128,128]{4,3,2,1,0:T(8,128)(2,1)S(1)}, u32[]{:S(2)}, u32[]{:S(2)}) collective-permute-start(bf16[1,2,2,128,128]{4,3,2,1,0:T(8,128)(2,1)} %get-tuple-element.22), channel_id=1, source_target_pairs={{0,1},{1,0},{2,3},{3,2},{4,5},{5,4},{6,7},{7,6},{8,9},{9,8},{10,11... | collective-permute-start | bytes 393224 | tf_op jit(solution)/shard_map/ppermute | solution.py:22
  46.6 6.6 %collective-permute-start.11 = (bf16[1,2,2,128,128]{4,3,2,1,0:T(8,128)(2,1)}, bf16[1,2,2,128,128]{4,3,2,1,0:T(8,128)(2,1)S(1)}, u32[]{:S(2)}, u32[]{:S(2)}) collective-permute-start(bf16[1,2,2,128,128]{4,3,2,1,0:T(8,128)(2,1)} %get-tuple-element.23), channel_id=1, source_target_pairs={{0,2},{1,3},{2,0},{3,1},{4,6},{5,7},{6,4},{7,5},{8,10},{9,11},{10,... | collective-permute-start | bytes 393224 | tf_op jit(solution)/shard_map/ppermute | solution.py:22
  48.2 6.9 %collective-permute-start.12 = (bf16[1,2,2,128,128]{4,3,2,1,0:T(8,128)(2,1)}, bf16[1,2,2,128,128]{4,3,2,1,0:T(8,128)(2,1)S(1)}, u32[]{:S(2)}, u32[]{:S(2)}) collective-permute-start(bf16[1,2,2,128,128]{4,3,2,1,0:T(8,128)(2,1)} %get-tuple-element.24), channel_id=1, source_target_pairs={{0,3},{1,2},{2,1},{3,0},{4,7},{5,6},{6,5},{7,4},{8,11},{9,10},{10,... | collective-permute-start | bytes 393224 | tf_op jit(solution)/shard_map/ppermute | solution.py:22
  55.0 0.9 %copy-start = (bf16[1,2,2,128,128]{4,3,2,1,0:T(8,128)(2,1)S(1)}, bf16[1,2,2,128,128]{4,3,2,1,0:T(8,128)(2,1)}, u32[]{:S(2)}) copy-start(bf16[1,2,2,128,128]{4,3,2,1,0:T(8,128)(2,1)} %get-tuple-element.21.refs_0_) | copy-start | bytes 393220

commit v2 on v1

--- a/solution.py
+++ b/solution.py
@@ -66,15 +66,13 @@
     return loads
 
 
-def lesser_items(loads, green, sigma):
-    for start in range(0, len(loads), GROUP):
-        group = range(start, min(start + GROUP, len(loads)))
-        for i in group:
-            for copy in loads[i]:
-                copy.wait()
-        for i in group:
-            both = lesser_of(green[i, 0], green[i, 1], sigma[i, 0], sigma[i, 1])
-            yield i, both.astype(jnp.bfloat16)
+def lesser_items(loads, green, sigma, items):
+    for i in items:
+        for copy in loads[i]:
+            copy.wait()
+    for i in items:
+        both = lesser_of(green[i, 0], green[i, 1], sigma[i, 0], sigma[i, 1])
+        yield i, both.astype(jnp.bfloat16)
 
 
 def lesser_of(real, imag, sigma_real, sigma_imag):
@@ -114,11 +112,11 @@
     for distance, out_ref in enumerate(out_refs):
         for at in range(own):
             block = (place_ref[0] ^ distance) * own + at
-            from_d = [neighbors_ref[block, d] for d in range(directions)]
+            source = [neighbors_ref[d, block] for d in range(directions)]
             left = jnp.concatenate(
                 [
                     jnp.concatenate(
-                        [bent_ref[from_d[d], d, part] for d in range(directions)], axis=1
+                        [bent_ref[source[d], d, part] for d in range(directions)], axis=1
                     )
                     for part in range(2)
                 ],
@@ -134,7 +132,7 @@
     loads = start_loads(
         first, count, range(cut, cut + blocks), retarded_ref, sigma_ref, green, sigma, sems
     )
-    for i, both in lesser_items(loads, green, sigma):
+    for i, both in lesser_items(loads, green, sigma, range(len(loads))):
         for part in range(2):
             lesser_ref[i // blocks, i % blocks, part] = both[:, part * size : (part + 1) * size]
 
@@ -147,7 +145,7 @@
         first, count, range(cut, cut + blocks), retarded_ref, sigma_ref, green, sigma, sems
     )
     whole_ref[:, :cut] = begun_ref[...]
-    for i, both in lesser_items(loads, green, sigma):
+    for i, both in lesser_items(loads, green, sigma, range(len(loads))):
         for part in range(2):
             half = both[:, part * size : (part + 1) * size]
             rest_ref[i // blocks, i % blocks, part] = half
@@ -195,16 +193,20 @@
 
 
 def lesser_couple_kernel(first, place_ref, neighbors_ref, coupling_ref, *refs):
-    retarded_ref, sigma_ref, *out_refs, bent_ref, green, sigma, sems = refs
+    retarded_ref, sigma_ref, *out_refs, bent_ref, made, green, sigma, sems = refs
     blocks = retarded_ref.shape[1]
     count = out_refs[0].shape[0]
     loads = start_loads(
         first, count, range(blocks), retarded_ref, sigma_ref, green, sigma, sems
     )
-    for i, both in lesser_items(loads, green, sigma):
-        bend(coupling_ref, both, bent_ref, i % blocks)
-        if i % blocks == blocks - 1:
-            unbend(place_ref, neighbors_ref, coupling_ref, bent_ref, out_refs, i // blocks)
+    for start in range(0, len(loads), GROUP):
+        group = range(start, min(start + GROUP, len(loads)))
+        for i, both in lesser_items(loads, green, sigma, group):
+            made[i % GROUP] = both
+        for i in group:
+            bend(coupling_ref, made[i % GROUP], bent_ref, i % blocks)
+            if i % blocks == blocks - 1:
+                unbend(place_ref, neighbors_ref, coupling_ref, bent_ref, out_refs, i // blocks)
 
 
 def lesser_couple(place, neighbors, coupling, retarded, sigma_in, first, count, atoms):
@@ -215,7 +217,10 @@
         out_shape=[kept((count, blocks // atoms, *own))] * atoms,
         in_specs=[SMEM, SMEM, VMEM, ANY, ANY],
         out_specs=[VMEM] * atoms,
-        scratch_shapes=[pltpu.VMEM((blocks, directions, *own), jnp.bfloat16)]
+        scratch_shapes=[
+            pltpu.VMEM((blocks, directions, *own), jnp.bfloat16),
+            pltpu.VMEM((GROUP, size, own[0] * size), jnp.bfloat16),
+        ]
         + lesser_scratch(count, blocks, own),
         cost_estimate=pl.CostEstimate(
             flops=count * blocks * (16 + directions * 8) * size**3,
@@ -227,12 +232,12 @@
 
 
 def sum_couple_kernel(
-    widths, place_ref, bit_shifts_ref, occupation_ref, neighbors_ref, coupling_ref, *refs
+    widths, place_ref, odd_ref, bit_shifts_ref, occupation_ref, neighbors_ref, coupling_ref, *refs
 ):
     taken = sum(widths)
     arrived, out_refs, bent_ref = list(refs[:taken]), refs[taken:-1], refs[-1]
     terms = [[arrived.pop(0) for _ in range(width)] for width in widths]
-    weights = weights_of(len(terms), place_ref, bit_shifts_ref, occupation_ref)
+    weights = weights_of(len(terms), odd_ref, bit_shifts_ref, occupation_ref)
     span = bent_ref.shape[0] // max(widths)
     for piece in range(max(widths)):
 
@@ -279,7 +284,7 @@
     )(*scalars, coupling, *arrays)
 
 
-def weights_of(bits, place_ref, bit_shifts_ref, occupation_ref):
+def weights_of(bits, odd_ref, bit_shifts_ref, occupation_ref):
     weights = []
     for bit in range(bits):
         weight = jnp.float32(0)
@@ -287,7 +292,7 @@
             weight += jnp.where(bit_shifts_ref[mode] == bit, occupation_ref[mode], 0.0)
         weights.append(weight)
     if bits > 1:
-        odd = place_ref[1] == 1
+        odd = odd_ref[0] == 1
         low, high = weights[-2:]
         weights[-2:] = [jnp.where(odd, low, high), jnp.where(odd, high, low)]
     return weights
@@ -318,18 +323,18 @@
     )(place, *in_vmem(pieces))
 
 
-def weighted_kernel(
-    taken, energies, first, place_ref, bit_shifts_ref, occupation_ref, *refs
+def last_kernel(
+    terms, energies, first, place_ref, odd_ref, bit_shifts_ref, occupation_ref, *refs
 ):
-    arrived, out_ref, result, sems = refs[:taken], *refs[taken + 1 :]
-    weights = weights_of(taken, place_ref, bit_shifts_ref, occupation_ref)
-    distances, count = arrived[0].shape[:2]
+    arrived, (_, out_ref, result, sems) = refs[:terms], refs[terms:]
+    weights = weights_of(terms, odd_ref, bit_shifts_ref, occupation_ref)
+    distances, count = result.shape[:2]
     stores = []
     for d in range(distances):
         for e in range(count):
             total = weights[0] * arrived[0][d, e].astype(jnp.float32)
-            for bit in range(1, taken):
-                total += weights[bit] * arrived[bit][d, e].astype(jnp.float32)
+            for weight, term in zip(weights[1:], arrived[1:]):
+                total += weight * term[d, e].astype(jnp.float32)
             result[d, e] = total.astype(jnp.bfloat16)
             row = (place_ref[0] ^ d) * energies + first + e
             store = pltpu.make_async_copy(result.at[d, e], out_ref.at[row], sems.at[d, e])
@@ -339,20 +344,20 @@
         store.wait()
 
 
-def place_second(place, bit_shifts, occupation, arrived, out, energies, first):
-    taken = len(arrived)
-    return pl.pallas_call(
-        functools.partial(weighted_kernel, taken, energies, first),
+def place_second(scalars, arrived, out, energies, first):
+    shape, terms = arrived[0].shape, len(arrived)
+    return pl.pallas_call(
+        functools.partial(last_kernel, terms, energies, first),
         out_shape=jax.ShapeDtypeStruct(out.shape, out.dtype),
-        in_specs=[SMEM] * 3 + [VMEM] * taken + [ANY],
+        in_specs=[SMEM] * len(scalars) + [VMEM] * terms + [ANY],
         out_specs=ANY,
         scratch_shapes=[
-            pltpu.VMEM(arrived[0].shape, jnp.bfloat16),
-            pltpu.SemaphoreType.DMA(arrived[0].shape[:2]),
+            pltpu.VMEM(shape, jnp.bfloat16),
+            pltpu.SemaphoreType.DMA(shape[:2]),
         ],
-        input_output_aliases={3 + taken: 0},
+        input_output_aliases={len(scalars) + terms: 0},
         name="place_second",
-    )(place, bit_shifts, occupation, *in_vmem(arrived), out)
+    )(*scalars, *in_vmem(arrived), out)
 
 
 def stack_kernel(distances, *refs):
@@ -405,9 +410,9 @@
     half = energies // 2
     rest = energies - half
     cut = blocks // 2
-    place = jnp.stack(
-        [lax.axis_index("atom"), oddness(lax.axis_index("win"), windows)]
-    ).astype(jnp.int32)
+    place = lax.axis_index("atom").astype(jnp.int32).reshape(1)
+    odd = oddness(lax.axis_index("win"), windows).astype(jnp.int32).reshape(1)
+    table = neighbors.T
     begun = lesser_begin(retarded, sigma_in, 0, half, cut)
     arrived_begun = exchange(begun, terms - 2)
     ended, lesser_a = lesser_rest(retarded, sigma_in, begun, 0, half)
@@ -418,7 +423,9 @@
             arrived_a[term] = [exchange(lesser_a, term)]
     arrived_a[terms - 2] = [arrived_begun, arrived_ended]
 
-    coupled_b = lesser_couple(place, neighbors, coupling, retarded, sigma_in, half, rest, atoms)
+    coupled_b = lesser_couple(
+        place, table, coupling, retarded, sigma_in, half, rest, atoms
+    )
     exchanged_b = [coupled_b[0]]
     for distance in range(1, atoms):
         exchanged_b.append(flip(coupled_b[distance], "atom", distance))
@@ -428,7 +435,7 @@
         arrived_b[term] = exchange(exchanged_b, term)
 
     coupled_a = sum_couple(
-        (place, bit_shifts, occupation, neighbors),
+        (place, odd, bit_shifts, occupation, table),
         coupling,
         [arrived_a[term] for term in range(terms)],
         atoms,
@@ -437,8 +444,9 @@
     for distance in range(1, atoms):
         exchanged_a.append(flip(coupled_a[distance], "atom", distance))
     out = place_first(place, exchanged_a, energies)
-    arrived_b = tuple(arrived_b[term] for term in range(terms))
-    return place_second(place, bit_shifts, occupation, arrived_b, out, energies, half)
+    arrived_b = [arrived_b[term] for term in range(terms)]
+    scalars = (place, odd, bit_shifts, occupation)
+    return place_second(scalars, arrived_b, out, energies, half)
 
 
 def solution(mesh):

time: 64.2 us -> 61 us (0.950)
  local copies, waits for them, and re-layouts: 3.83 us -> 1.68 us
  Pallas kernels: 15.7 us -> 13.9 us
  waiting for transfers between devices: 27.3 us -> 28.6 us
  other arithmetic: 0.65 us -> 0 us
    unnamed x11 -> x8, local copies, waits for them, and re-layouts: 3.83 us -> 1.68 us
    ppermute x7, waiting for transfers between devices: 14.2 us -> 15.6 us  [exchange(): return lax.ppermute(value, 'win', pairs)]
    pallas_call x1, Pallas kernels: 5.25 us -> 4.15 us  [lesser_couple(): pl.pallas_call(functools.partial(lesser_couple_kernel, first), out_shape=...]
    pallas_call x1, Pallas kernels: 1.48 us -> 0.82 us  [place_first(): pl.pallas_call(functools.partial(gather_kernel, len(pieces)), out_shape=j...]
    another operation x1 -> x0, other arithmetic: 0.65 us -> none  [on_device(): jnp.stack([lax.axis_index('atom'), oddness(lax.axis_index('win'), windows)])]
  transfers between devices with their start and end apart: 13 -> 13, of which waited for: 7 -> 7; matrix products, arithmetic and copies ran while one was open for 0% -> 0% of each run, Pallas kernels for 14% -> 13%
where the time goes in v2:
time: 61 us; the launch traced here: 60.7 us
  waiting for transfers between devices  28.6 us (47%)
  starting transfers between devices  16.4 us (27%)
  Pallas kernels  13.9 us (23%)
  local copies, waits for them, and re-layouts  1.68 us (3%)
    ppermute x7, waiting for transfers between devices, exchange(): return lax.ppermute(value, 'win', pairs)  15.6 us
    ppermute x6, waiting for transfers between devices, flip(): return lax.ppermute(value, axis, pairs)  13 us
    ppermute x7, starting transfers between devices, exchange(): return lax.ppermute(value, 'win', pairs)  11.2 us
    ppermute x6, starting transfers between devices, flip(): return lax.ppermute(value, axis, pairs)  5.19 us
    pallas_call x1, Pallas kernels, lesser_couple(): pl.pallas_call(functools.partial(lesser_couple_kernel, first), out_shape=...  4.15 us
    pallas_call x1, Pallas kernels, sum_couple(): pl.pallas_call(functools.partial(sum_couple_kernel, [len(term) for term i...  3.23 us
    unnamed x8, local copies, waits for them, and re-layouts  1.68 us
    pallas_call x1, Pallas kernels, place_second(): pl.pallas_call(functools.partial(last_kernel, terms, energies, first), ou...  1.66 us
  transfers between devices with their start and end apart: 13, of which 7 were waited for; matrix products, arithmetic and copies ran while one was open for 0% of the time, Pallas kernels for 13%

profile of v2, /device:TPU:0, one launch (start us, length us, event | category | flops | bytes accessed | tf_op | source)
XLA Modules:
  0.0 60.7 jit_solution(12555219547573202837)
XLA Ops:
  0.0 4.1 %lesser_couple.1 = (bf16[1,2,2,128,128]{4,3,2,1,0:T(8,128)(2,1)S(1)}, bf16[1,2,2,128,128]{4,3,2,1,0:T(8,128)(2,1)S(1)}, bf16[1,2,2,128,128]{4,3,2,1,0:T(8,128)(2,1)S(1)}, bf16[1,2,2,128,128]{4,3,2,1,0:T(8,128)(2,1)S(1)}) custom-call(s32[1]{0:T(128)} %bitcast.place_ref, s32[3,8]{1,0:T(4,128)} %bitcast.3, bf16[3,128,128]{2,1,0:T(8,128)(2,1)} %coupling_ref.3, ...), custom_call_target="tpu_custom_call" | custom-call | flops 671088640 | bytes 1572864 | tf_op jit(solution)/shard_map/lesser_couple/pallas_call | solution.py:215
  4.2 0.6 collective-permute-start
  4.7 1.6 %lesser_begin.1.refs_2_ = bf16[1,4,2,128,128]{4,3,2,1,0:T(8,128)(2,1)S(1)} custom-call(bf16[2,8,2,128,128]{4,3,2,1,0:T(8,128)(2,1)} %refs_0_.3, bf16[2,8,2,128,128]{4,3,2,1,0:T(8,128)(2,1)} %refs_1_.3), custom_call_target="tpu_custom_call" | custom-call | flops 134217728 | bytes 786432 | tf_op jit(solution)/shard_map/lesser_begin/pallas_call | solution.py:170
  6.3 1.6 %lesser_rest.1 = (bf16[1,4,2,128,128]{4,3,2,1,0:T(8,128)(2,1)S(1)}, bf16[1,8,2,128,128]{4,3,2,1,0:T(8,128)(2,1)S(1)}) custom-call(bf16[2,8,2,128,128]{4,3,2,1,0:T(8,128)(2,1)} %refs_0_.3, bf16[2,8,2,128,128]{4,3,2,1,0:T(8,128)(2,1)} %refs_1_.3, bf16[1,4,2,128,128]{4,3,2,1,0:T(8,128)(2,1)S(1)} %lesser_begin.1.refs_2_), custom_call_target="tpu_custom_call" | custom-call | flops 134217728 | bytes 786432 | tf_op jit(solution)/shard_map/lesser_rest/pallas_call | solution.py:184
  8.0 3.6 %collective-permute-start.9 = (bf16[1,8,2,128,128]{4,3,2,1,0:T(8,128)(2,1)S(1)}, bf16[1,8,2,128,128]{4,3,2,1,0:T(8,128)(2,1)S(1)}, u32[]{:S(2)}, u32[]{:S(2)}) collective-permute-start(bf16[1,8,2,128,128]{4,3,2,1,0:T(8,128)(2,1)S(1)} %get-tuple-element.19), channel_id=1, source_target_pairs={{0,16},{4,20},{8,0},{12,4},{16,24},{20,28},{24,8},{28,12},{1,17},{... | collective-permute-start | bytes 1572872 | tf_op jit(solution)/shard_map/ppermute | solution.py:402
  11.6 1.5 %collective-permute-start.6 = (bf16[1,8,2,128,128]{4,3,2,1,0:T(8,128)(2,1)S(1)}, bf16[1,8,2,128,128]{4,3,2,1,0:T(8,128)(2,1)}, u32[]{:S(2)}, u32[]{:S(2)}) collective-permute-start(bf16[1,8,2,128,128]{4,3,2,1,0:T(8,128)(2,1)S(1)} %get-tuple-element.19), channel_id=1, source_target_pairs={{0,4},{4,0},{8,12},{12,8},{16,20},{20,16},{24,28},{28,24},{1,5},{5... | collective-permute-start | bytes 1572872 | tf_op jit(solution)/shard_map/ppermute | solution.py:402
  13.1 1.5 %collective-permute-start.1 = (bf16[1,2,2,128,128]{4,3,2,1,0:T(8,128)(2,1)S(1)}, bf16[1,2,2,128,128]{4,3,2,1,0:T(8,128)(2,1)S(1)}, u32[]{:S(2)}, u32[]{:S(2)}) collective-permute-start(bf16[1,2,2,128,128]{4,3,2,1,0:T(8,128)(2,1)S(1)} %get-tuple-element.17), channel_id=1, source_target_pairs={{0,2},{1,3},{2,0},{3,1},{4,6},{5,7},{6,4},{7,5},{8,10},{9,11},{10,... | collective-permute-start | bytes 393224 | tf_op jit(solution)/shard_map/ppermute | solution.py:22
  14.6 0.0 collective-permute-start.7
  14.6 1.9 %collective-permute-start.8 = (bf16[1,4,2,128,128]{4,3,2,1,0:T(8,128)(2,1)S(1)}, bf16[1,4,2,128,128]{4,3,2,1,0:T(8,128)(2,1)S(1)}, u32[]{:S(2)}, u32[]{:S(2)}) collective-permute-start(bf16[1,4,2,128,128]{4,3,2,1,0:T(8,128)(2,1)S(1)} %get-tuple-element.20), channel_id=1, source_target_pairs={{0,8},{4,12},{8,24},{12,28},{16,0},{20,4},{24,16},{28,20},{1,9},{5... | collective-permute-start | bytes 786440 | tf_op jit(solution)/shard_map/ppermute | solution.py:402
  16.5 1.9 %collective-permute-done.1.refs_2_ = bf16[1,2,2,128,128]{4,3,2,1,0:T(8,128)(2,1)S(1)} collective-permute-done((bf16[1,2,2,128,128]{4,3,2,1,0:T(8,128)(2,1)S(1)}, bf16[1,2,2,128,128]{4,3,2,1,0:T(8,128)(2,1)S(1)}, u32[]{:S(2)}, u32[]{:S(2)}) %collective-permute-start.1) | collective-permute-done | bytes 131104 | tf_op jit(solution)/shard_map/ppermute | solution.py:22
  18.4 0.3 collective-permute-start.2
  18.7 5.4 %collective-permute-done.2.refs_3_ = bf16[1,2,2,128,128]{4,3,2,1,0:T(8,128)(2,1)S(1)} collective-permute-done((bf16[1,2,2,128,128]{4,3,2,1,0:T(8,128)(2,1)S(1)}, bf16[1,2,2,128,128]{4,3,2,1,0:T(8,128)(2,1)S(1)}, u32[]{:S(2)}, u32[]{:S(2)}) %collective-permute-start.2) | collective-permute-done | bytes 131104 | tf_op jit(solution)/shard_map/ppermute | solution.py:22
  24.1 0.8 %stack.1 = bf16[4,1,2,2,128,128]{5,4,3,2,1,0:T(8,128)(2,1)} custom-call(bf16[1,2,2,128,128]{4,3,2,1,0:T(8,128)(2,1)S(1)} %get-tuple-element.15.refs_0_, bf16[1,2,2,128,128]{4,3,2,1,0:T(8,128)(2,1)S(1)} %collective-permute-done.refs_1_, bf16[1,2,2,128,128]{4,3,2,1,0:T(8,128)(2,1)S(1)} %collective-permute-done.1.refs_2_, ...), custom_call_target="tpu_custom_call" | custom-call | tf_op jit(solution)/shard_map/stack/pallas_call | solution.py:374
  25.0 1.6 %collective-permute-start.5 = (bf16[4,1,2,2,128,128]{5,4,3,2,1,0:T(8,128)(2,1)}, bf16[4,1,2,2,128,128]{5,4,3,2,1,0:T(8,128)(2,1)S(1)}, u32[]{:S(2)}, u32[]{:S(2)}) collective-permute-start(bf16[4,1,2,2,128,128]{5,4,3,2,1,0:T(8,128)(2,1)} %stack.1), channel_id=1, source_target_pairs={{0,16},{4,20},{8,0},{12,4},{16,24},{20,28},{24,8},{28,12},{1,17},{... | collective-permute-start | bytes 1572872 | tf_op jit(solution)/shard_map/ppermute | solution.py:402
  26.6 4.4 %collective-permute-done.7.refs_1_ = bf16[1,4,2,128,128]{4,3,2,1,0:T(8,128)(2,1)S(1)} collective-permute-done((bf16[1,4,2,128,128]{4,3,2,1,0:T(8,128)(2,1)S(1)}, bf16[1,4,2,128,128]{4,3,2,1,0:T(8,128)(2,1)S(1)}, u32[]{:S(2)}, u32[]{:S(2)}) %collective-permute-start.7) | collective-permute-done | bytes 262176 | tf_op jit(solution)/shard_map/ppermute | solution.py:402
  31.1 1.0 %collective-permute-start.4 = (bf16[4,1,2,2,128,128]{5,4,3,2,1,0:T(8,128)(2,1)}, bf16[4,1,2,2,128,128]{5,4,3,2,1,0:T(8,128)(2,1)S(1)}, u32[]{:S(2)}, u32[]{:S(2)}) collective-permute-start(bf16[4,1,2,2,128,128]{5,4,3,2,1,0:T(8,128)(2,1)} %stack.1), channel_id=1, source_target_pairs={{0,8},{4,12},{8,24},{12,28},{16,0},{20,4},{24,16},{28,20},{1,9},{5... | collective-permute-start | bytes 1572872 | tf_op jit(solution)/shard_map/ppermute | solution.py:402
  32.1 5.0 %collective-permute-done.8.refs_2_ = bf16[1,4,2,128,128]{4,3,2,1,0:T(8,128)(2,1)S(1)} collective-permute-done((bf16[1,4,2,128,128]{4,3,2,1,0:T(8,128)(2,1)S(1)}, bf16[1,4,2,128,128]{4,3,2,1,0:T(8,128)(2,1)S(1)}, u32[]{:S(2)}, u32[]{:S(2)}) %collective-permute-start.8) | collective-permute-done | bytes 262176 | tf_op jit(solution)/shard_map/ppermute | solution.py:402
  37.1 1.5 %collective-permute-start.3 = (bf16[4,1,2,2,128,128]{5,4,3,2,1,0:T(8,128)(2,1)}, bf16[4,1,2,2,128,128]{5,4,3,2,1,0:T(8,128)(2,1)S(1)}, u32[]{:S(2)}, u32[]{:S(2)}) collective-permute-start(bf16[4,1,2,2,128,128]{5,4,3,2,1,0:T(8,128)(2,1)} %stack.1), channel_id=1, source_target_pairs={{0,4},{4,0},{8,12},{12,8},{16,20},{20,16},{24,28},{28,24},{1,5},{5... | collective-permute-start | bytes 1572872 | tf_op jit(solution)/shard_map/ppermute | solution.py:402
  38.6 0.0 collective-permute-done.6.refs_0_
  38.6 0.8 %copy-done.1 = bf16[1,8,2,128,128]{4,3,2,1,0:T(8,128)(2,1)} copy-done((bf16[1,8,2,128,128]{4,3,2,1,0:T(8,128)(2,1)}, bf16[1,8,2,128,128]{4,3,2,1,0:T(8,128)(2,1)S(1)}, u32[]{:S(2)}) %copy-start.1) | copy-done | bytes 524312
  39.4 3.2 %sum_couple.1 = (bf16[1,2,2,128,128]{4,3,2,1,0:T(8,128)(2,1)}, bf16[1,2,2,128,128]{4,3,2,1,0:T(8,128)(2,1)}, bf16[1,2,2,128,128]{4,3,2,1,0:T(8,128)(2,1)}, bf16[1,2,2,128,128]{4,3,2,1,0:T(8,128)(2,1)}) custom-call(s32[1]{0:T(128)} %bitcast.place_ref, s32[1]{0:T(128)} %bitcast.1.odd_ref, s32[3]{0:T(128)} %bit_shifts_ref.3, f32[3]{0:T(128)} %occupation_ref.3, ...), custom_call_target="tpu_custom_call" | custom-call | flops 402653184 | bytes 1572864 | tf_op jit(solution)/shard_map/sum_couple/pallas_call | solution.py:263
  42.6 0.0 collective-permute-start.10
  42.6 1.5 %collective-permute-start.11 = (bf16[1,2,2,128,128]{4,3,2,1,0:T(8,128)(2,1)}, bf16[1,2,2,128,128]{4,3,2,1,0:T(8,128)(2,1)S(1)}, u32[]{:S(2)}, u32[]{:S(2)}) collective-permute-start(bf16[1,2,2,128,128]{4,3,2,1,0:T(8,128)(2,1)} %get-tuple-element.23), channel_id=1, source_target_pairs={{0,2},{1,3},{2,0},{3,1},{4,6},{5,7},{6,4},{7,5},{8,10},{9,11},{10,... | collective-permute-start | bytes 393224 | tf_op jit(solution)/shard_map/ppermute | solution.py:22
  44.2 0.0 collective-permute-done.10.refs_1_
  44.2 1.3 %collective-permute-start.12 = (bf16[1,2,2,128,128]{4,3,2,1,0:T(8,128)(2,1)}, bf16[1,2,2,128,128]{4,3,2,1,0:T(8,128)(2,1)S(1)}, u32[]{:S(2)}, u32[]{:S(2)}) collective-permute-start(bf16[1,2,2,128,128]{4,3,2,1,0:T(8,128)(2,1)} %get-tuple-element.24), channel_id=1, source_target_pairs={{0,3},{1,2},{2,1},{3,0},{4,7},{5,6},{6,5},{7,4},{8,11},{9,10},{10,... | collective-permute-start | bytes 393224 | tf_op jit(solution)/shard_map/ppermute | solution.py:22
  45.5 3.8 %collective-permute-done.11.refs_2_ = bf16[1,2,2,128,128]{4,3,2,1,0:T(8,128)(2,1)S(1)} collective-permute-done((bf16[1,2,2,128,128]{4,3,2,1,0:T(8,128)(2,1)}, bf16[1,2,2,128,128]{4,3,2,1,0:T(8,128)(2,1)S(1)}, u32[]{:S(2)}, u32[]{:S(2)}) %collective-permute-start.11) | collective-permute-done | bytes 131104 | tf_op jit(solution)/shard_map/ppermute | solution.py:22
  49.2 1.9 %collective-permute-done.12.refs_3_ = bf16[1,2,2,128,128]{4,3,2,1,0:T(8,128)(2,1)S(1)} collective-permute-done((bf16[1,2,2,128,128]{4,3,2,1,0:T(8,128)(2,1)}, bf16[1,2,2,128,128]{4,3,2,1,0:T(8,128)(2,1)S(1)}, u32[]{:S(2)}, u32[]{:S(2)}) %collective-permute-start.12) | collective-permute-done | bytes 131104 | tf_op jit(solution)/shard_map/ppermute | solution.py:22
  51.1 0.9 %copy-done = bf16[1,2,2,128,128]{4,3,2,1,0:T(8,128)(2,1)S(1)} copy-done((bf16[1,2,2,128,128]{4,3,2,1,0:T(8,128)(2,1)S(1)}, bf16[1,2,2,128,128]{4,3,2,1,0:T(8,128)(2,1)}, u32[]{:S(2)}) %copy-start) | copy-done | bytes 131096
  52.0 0.8 %place_first.1.refs_3_ = bf16[8,2,2,128,128]{4,3,2,1,0:T(8,128)(2,1)} custom-call(s32[1]{0:T(128)} %bitcast.place_ref, bf16[1,2,2,128,128]{4,3,2,1,0:T(8,128)(2,1)S(1)} %copy-done, bf16[1,2,2,128,128]{4,3,2,1,0:T(8,128)(2,1)S(1)} %collective-permute-done.10.refs_1_, bf16[1,2,2,128,128]{4,3,2,1,0:T(8,128)(2,1)S(1)} %collective-permute-done.11.refs_2_, ...), custom_call_target="tpu_custom_call" | custom-call | tf_op jit(solution)/shard_map/place_first/pallas_call | solution.py:316
  52.8 6.2 %collective-permute-done.4.refs_1_ = bf16[4,1,2,2,128,128]{5,4,3,2,1,0:T(8,128)(2,1)S(1)} collective-permute-done((bf16[4,1,2,2,128,128]{5,4,3,2,1,0:T(8,128)(2,1)}, bf16[4,1,2,2,128,128]{5,4,3,2,1,0:T(8,128)(2,1)S(1)}, u32[]{:S(2)}, u32[]{:S(2)}) %collective-permute-start.4) | collective-permute-done | bytes 524320 | tf_op jit(solution)/shard_map/ppermute | solution.py:402
  59.0 0.0 collective-permute-done.3.refs_0_
  59.0 1.7 %place_second.1 = bf16[8,2,2,128,128]{4,3,2,1,0:T(8,128)(2,1)} custom-call(s32[1]{0:T(128)} %bitcast.place_ref, s32[1]{0:T(128)} %bitcast.1.odd_ref, s32[3]{0:T(128)} %bit_shifts_ref.3, f32[3]{0:T(128)} %occupation_ref.3, bf16[4,1,2,2,128,128]{5,4,3,2,1,0:T(8,128)(2,1)S(1)} %collective-permute-done.3.refs_0_, ...), custom_call_target="tpu_custom_call", output_to_operand_aliasing={{}: (7, {})} | custom-call | tf_op jit(solution)/shard_map/place_second/pallas_call | solution.py:349
  (9 shorter events, 0.0 us)
Async XLA Ops:
  4.2 10.5 %collective-permute-start = (bf16[1,2,2,128,128]{4,3,2,1,0:T(8,128)(2,1)S(1)}, bf16[1,2,2,128,128]{4,3,2,1,0:T(8,128)(2,1)S(1)}, u32[]{:S(2)}, u32[]{:S(2)}) collective-permute-start(bf16[1,2,2,128,128]{4,3,2,1,0:T(8,128)(2,1)S(1)} %get-tuple-element.16), channel_id=1, source_target_pairs={{0,1},{1,0},{2,3},{3,2},{4,5},{5,4},{6,7},{7,6},{8,9},{9,8},{10,11... | collective-permute-start | bytes 393224 | tf_op jit(solution)/shard_map/ppermute | solution.py:22
  8.0 30.6 %collective-permute-start.9 = (bf16[1,8,2,128,128]{4,3,2,1,0:T(8,128)(2,1)S(1)}, bf16[1,8,2,128,128]{4,3,2,1,0:T(8,128)(2,1)S(1)}, u32[]{:S(2)}, u32[]{:S(2)}) collective-permute-start(bf16[1,8,2,128,128]{4,3,2,1,0:T(8,128)(2,1)S(1)} %get-tuple-element.19), channel_id=1, source_target_pairs={{0,16},{4,20},{8,0},{12,4},{16,24},{20,28},{24,8},{28,12},{1,17},{... | collective-permute-start | bytes 1572872 | tf_op jit(solution)/shard_map/ppermute | solution.py:402
  11.6 27.0 %collective-permute-start.6 = (bf16[1,8,2,128,128]{4,3,2,1,0:T(8,128)(2,1)S(1)}, bf16[1,8,2,128,128]{4,3,2,1,0:T(8,128)(2,1)}, u32[]{:S(2)}, u32[]{:S(2)}) collective-permute-start(bf16[1,8,2,128,128]{4,3,2,1,0:T(8,128)(2,1)S(1)} %get-tuple-element.19), channel_id=1, source_target_pairs={{0,4},{4,0},{8,12},{12,8},{16,20},{20,16},{24,28},{28,24},{1,5},{5... | collective-permute-start | bytes 1572872 | tf_op jit(solution)/shard_map/ppermute | solution.py:402
  13.1 5.3 %collective-permute-start.1 = (bf16[1,2,2,128,128]{4,3,2,1,0:T(8,128)(2,1)S(1)}, bf16[1,2,2,128,128]{4,3,2,1,0:T(8,128)(2,1)S(1)}, u32[]{:S(2)}, u32[]{:S(2)}) collective-permute-start(bf16[1,2,2,128,128]{4,3,2,1,0:T(8,128)(2,1)S(1)} %get-tuple-element.17), channel_id=1, source_target_pairs={{0,2},{1,3},{2,0},{3,1},{4,6},{5,7},{6,4},{7,5},{8,10},{9,11},{10,... | collective-permute-start | bytes 393224 | tf_op jit(solution)/shard_map/ppermute | solution.py:22
  14.6 16.4 %collective-permute-start.7 = (bf16[1,4,2,128,128]{4,3,2,1,0:T(8,128)(2,1)S(1)}, bf16[1,4,2,128,128]{4,3,2,1,0:T(8,128)(2,1)S(1)}, u32[]{:S(2)}, u32[]{:S(2)}) collective-permute-start(bf16[1,4,2,128,128]{4,3,2,1,0:T(8,128)(2,1)S(1)} %lesser_begin.1.refs_2_), channel_id=1, source_target_pairs={{0,8},{4,12},{8,24},{12,28},{16,0},{20,4},{24,16},{28,20},{1,9},{5... | collective-permute-start | bytes 786440 | tf_op jit(solution)/shard_map/ppermute | solution.py:402
  14.6 22.5 %collective-permute-start.8 = (bf16[1,4,2,128,128]{4,3,2,1,0:T(8,128)(2,1)S(1)}, bf16[1,4,2,128,128]{4,3,2,1,0:T(8,128)(2,1)S(1)}, u32[]{:S(2)}, u32[]{:S(2)}) collective-permute-start(bf16[1,4,2,128,128]{4,3,2,1,0:T(8,128)(2,1)S(1)} %get-tuple-element.20), channel_id=1, source_target_pairs={{0,8},{4,12},{8,24},{12,28},{16,0},{20,4},{24,16},{28,20},{1,9},{5... | collective-permute-start | bytes 786440 | tf_op jit(solution)/shard_map/ppermute | solution.py:402
  18.4 5.7 %collective-permute-start.2 = (bf16[1,2,2,128,128]{4,3,2,1,0:T(8,128)(2,1)S(1)}, bf16[1,2,2,128,128]{4,3,2,1,0:T(8,128)(2,1)S(1)}, u32[]{:S(2)}, u32[]{:S(2)}) collective-permute-start(bf16[1,2,2,128,128]{4,3,2,1,0:T(8,128)(2,1)S(1)} %get-tuple-element.18), channel_id=1, source_target_pairs={{0,3},{1,2},{2,1},{3,0},{4,7},{5,6},{6,5},{7,4},{8,11},{9,10},{10,... | collective-permute-start | bytes 393224 | tf_op jit(solution)/shard_map/ppermute | solution.py:22
  25.0 27.8 %collective-permute-start.5 = (bf16[4,1,2,2,128,128]{5,4,3,2,1,0:T(8,128)(2,1)}, bf16[4,1,2,2,128,128]{5,4,3,2,1,0:T(8,128)(2,1)S(1)}, u32[]{:S(2)}, u32[]{:S(2)}) collective-permute-start(bf16[4,1,2,2,128,128]{5,4,3,2,1,0:T(8,128)(2,1)} %stack.1), channel_id=1, source_target_pairs={{0,16},{4,20},{8,0},{12,4},{16,24},{20,28},{24,8},{28,12},{1,17},{... | collective-permute-start | bytes 1572872 | tf_op jit(solution)/shard_map/ppermute | solution.py:402
  31.1 7.6 %copy-start.2 = (bf16[1,4,2,128,128]{4,3,2,1,0:T(8,128)(2,1)}, bf16[1,4,2,128,128]{4,3,2,1,0:T(8,128)(2,1)S(1)}, u32[]{:S(2)}) copy-start(bf16[1,4,2,128,128]{4,3,2,1,0:T(8,128)(2,1)S(1)} %collective-permute-done.7.refs_1_) | copy-start | bytes 786436
  31.1 27.9 %collective-permute-start.4 = (bf16[4,1,2,2,128,128]{5,4,3,2,1,0:T(8,128)(2,1)}, bf16[4,1,2,2,128,128]{5,4,3,2,1,0:T(8,128)(2,1)S(1)}, u32[]{:S(2)}, u32[]{:S(2)}) collective-permute-start(bf16[4,1,2,2,128,128]{5,4,3,2,1,0:T(8,128)(2,1)} %stack.1), channel_id=1, source_target_pairs={{0,8},{4,12},{8,24},{12,28},{16,0},{20,4},{24,16},{28,20},{1,9},{5... | collective-permute-start | bytes 1572872 | tf_op jit(solution)/shard_map/ppermute | solution.py:402
  37.1 1.5 %copy-start.3 = (bf16[1,4,2,128,128]{4,3,2,1,0:T(8,128)(2,1)}, bf16[1,4,2,128,128]{4,3,2,1,0:T(8,128)(2,1)S(1)}, u32[]{:S(2)}) copy-start(bf16[1,4,2,128,128]{4,3,2,1,0:T(8,128)(2,1)S(1)} %collective-permute-done.8.refs_2_) | copy-start | bytes 786436
  37.1 21.9 %collective-permute-start.3 = (bf16[4,1,2,2,128,128]{5,4,3,2,1,0:T(8,128)(2,1)}, bf16[4,1,2,2,128,128]{5,4,3,2,1,0:T(8,128)(2,1)S(1)}, u32[]{:S(2)}, u32[]{:S(2)}) collective-permute-start(bf16[4,1,2,2,128,128]{5,4,3,2,1,0:T(8,128)(2,1)} %stack.1), channel_id=1, source_target_pairs={{0,4},{4,0},{8,12},{12,8},{16,20},{20,16},{24,28},{28,24},{1,5},{5... | collective-permute-start | bytes 1572872 | tf_op jit(solution)/shard_map/ppermute | solution.py:402
  38.6 0.8 %copy-start.1 = (bf16[1,8,2,128,128]{4,3,2,1,0:T(8,128)(2,1)}, bf16[1,8,2,128,128]{4,3,2,1,0:T(8,128)(2,1)S(1)}, u32[]{:S(2)}) copy-start(bf16[1,8,2,128,128]{4,3,2,1,0:T(8,128)(2,1)S(1)} %collective-permute-done.9.refs_3_) | copy-start | bytes 1572868
  42.6 1.6 %collective-permute-start.10 = (bf16[1,2,2,128,128]{4,3,2,1,0:T(8,128)(2,1)}, bf16[1,2,2,128,128]{4,3,2,1,0:T(8,128)(2,1)S(1)}, u32[]{:S(2)}, u32[]{:S(2)}) collective-permute-start(bf16[1,2,2,128,128]{4,3,2,1,0:T(8,128)(2,1)} %get-tuple-element.22), channel_id=1, source_target_pairs={{0,1},{1,0},{2,3},{3,2},{4,5},{5,4},{6,7},{7,6},{8,9},{9,8},{10,11... | collective-permute-start | bytes 393224 | tf_op jit(solution)/shard_map/ppermute | solution.py:22
  42.6 6.6 %collective-permute-start.11 = (bf16[1,2,2,128,128]{4,3,2,1,0:T(8,128)(2,1)}, bf16[1,2,2,128,128]{4,3,2,1,0:T(8,128)(2,1)S(1)}, u32[]{:S(2)}, u32[]{:S(2)}) collective-permute-start(bf16[1,2,2,128,128]{4,3,2,1,0:T(8,128)(2,1)} %get-tuple-element.23), channel_id=1, source_target_pairs={{0,2},{1,3},{2,0},{3,1},{4,6},{5,7},{6,4},{7,5},{8,10},{9,11},{10,... | collective-permute-start | bytes 393224 | tf_op jit(solution)/shard_map/ppermute | solution.py:22
  44.2 6.9 %collective-permute-start.12 = (bf16[1,2,2,128,128]{4,3,2,1,0:T(8,128)(2,1)}, bf16[1,2,2,128,128]{4,3,2,1,0:T(8,128)(2,1)S(1)}, u32[]{:S(2)}, u32[]{:S(2)}) collective-permute-start(bf16[1,2,2,128,128]{4,3,2,1,0:T(8,128)(2,1)} %get-tuple-element.24), channel_id=1, source_target_pairs={{0,3},{1,2},{2,1},{3,0},{4,7},{5,6},{6,5},{7,4},{8,11},{9,10},{10,... | collective-permute-start | bytes 393224 | tf_op jit(solution)/shard_map/ppermute | solution.py:22
  51.1 0.9 %copy-start = (bf16[1,2,2,128,128]{4,3,2,1,0:T(8,128)(2,1)S(1)}, bf16[1,2,2,128,128]{4,3,2,1,0:T(8,128)(2,1)}, u32[]{:S(2)}) copy-start(bf16[1,2,2,128,128]{4,3,2,1,0:T(8,128)(2,1)} %get-tuple-element.21.refs_0_) | copy-start | bytes 393220

commit v3 on v2

--- a/solution.py
+++ b/solution.py
@@ -235,9 +235,12 @@
     widths, place_ref, odd_ref, bit_shifts_ref, occupation_ref, neighbors_ref, coupling_ref, *refs
 ):
     taken = sum(widths)
-    arrived, out_refs, bent_ref = list(refs[:taken]), refs[taken:-1], refs[-1]
+    arrived, weights_ref, out_refs = list(refs[:taken]), refs[taken], refs[taken + 1 : -1]
+    bent_ref = refs[-1]
     terms = [[arrived.pop(0) for _ in range(width)] for width in widths]
     weights = weights_of(len(terms), odd_ref, bit_shifts_ref, occupation_ref)
+    for at, weight in enumerate(weights):
+        weights_ref[at] = jnp.full(weights_ref.shape[1:], weight, jnp.float32)
     span = bent_ref.shape[0] // max(widths)
     for piece in range(max(widths)):
 
@@ -262,15 +265,14 @@
     arrays = [array for term in terms for array in term]
     return pl.pallas_call(
         functools.partial(sum_couple_kernel, [len(term) for term in terms]),
-        out_shape=[
-            jax.ShapeDtypeStruct((count, blocks // atoms, *own), jnp.bfloat16)
-            for _ in range(atoms)
-        ],
+        out_shape=[pltpu.VMEM((len(terms), 8, own[-1]), jnp.float32)]
+        + [jax.ShapeDtypeStruct((count, blocks // atoms, *own), jnp.bfloat16)] * atoms,
         grid=(count,),
         in_specs=[SMEM] * len(scalars)
         + [VMEM]
         + [pl.BlockSpec((1, *array.shape[1:]), lambda e: (e, 0, 0, 0, 0)) for array in arrays],
-        out_specs=[
+        out_specs=[VMEM]
+        + [
             pl.BlockSpec((1, blocks // atoms, *own), lambda e: (e, 0, 0, 0, 0))
             for _ in range(atoms)
         ],
@@ -323,11 +325,10 @@
     )(place, *in_vmem(pieces))
 
 
-def last_kernel(
-    terms, energies, first, place_ref, odd_ref, bit_shifts_ref, occupation_ref, *refs
-):
+def last_kernel(terms, energies, first, weights_ref, *refs):
     arrived, (_, out_ref, result, sems) = refs[:terms], refs[terms:]
-    weights = weights_of(terms, odd_ref, bit_shifts_ref, occupation_ref)
+    weights = [weights_ref[at, :1] for at in range(terms)]
+    place = lax.axis_index("atom")
     distances, count = result.shape[:2]
     stores = []
     for d in range(distances):
@@ -336,7 +337,7 @@
             for weight, term in zip(weights[1:], arrived[1:]):
                 total += weight * term[d, e].astype(jnp.float32)
             result[d, e] = total.astype(jnp.bfloat16)
-            row = (place_ref[0] ^ d) * energies + first + e
+            row = (place ^ d) * energies + first + e
             store = pltpu.make_async_copy(result.at[d, e], out_ref.at[row], sems.at[d, e])
             store.start()
             stores.append(store)
@@ -344,20 +345,20 @@
         store.wait()
 
 
-def place_second(scalars, arrived, out, energies, first):
+def place_second(weights, arrived, out, energies, first):
     shape, terms = arrived[0].shape, len(arrived)
     return pl.pallas_call(
         functools.partial(last_kernel, terms, energies, first),
         out_shape=jax.ShapeDtypeStruct(out.shape, out.dtype),
-        in_specs=[SMEM] * len(scalars) + [VMEM] * terms + [ANY],
+        in_specs=[VMEM] * (terms + 1) + [ANY],
         out_specs=ANY,
         scratch_shapes=[
             pltpu.VMEM(shape, jnp.bfloat16),
             pltpu.SemaphoreType.DMA(shape[:2]),
         ],
-        input_output_aliases={len(scalars) + terms: 0},
+        input_output_aliases={terms + 1: 0},
         name="place_second",
-    )(*scalars, *in_vmem(arrived), out)
+    )(*in_vmem([weights]), *in_vmem(arrived), out)
 
 
 def stack_kernel(distances, *refs):
@@ -434,7 +435,7 @@
     for term in range(terms):
         arrived_b[term] = exchange(exchanged_b, term)
 
-    coupled_a = sum_couple(
+    weights, *coupled_a = sum_couple(
         (place, odd, bit_shifts, occupation, table),
         coupling,
         [arrived_a[term] for term in range(terms)],
@@ -445,8 +446,7 @@
         exchanged_a.append(flip(coupled_a[distance], "atom", distance))
     out = place_first(place, exchanged_a, energies)
     arrived_b = [arrived_b[term] for term in range(terms)]
-    scalars = (place, odd, bit_shifts, occupation)
-    return place_second(scalars, arrived_b, out, energies, half)
+    return place_second(weights, arrived_b, out, energies, half)
 
 
 def solution(mesh):

time: 61 us -> 60.3 us (0.989)
  Pallas kernels: 13.9 us -> 13.2 us
    pallas_call x1, Pallas kernels: 1.66 us -> 0.98 us  [place_second(): pl.pallas_call(functools.partial(last_kernel, terms, energies, first), ou...]
  transfers between devices with their start and end apart: 13 -> 13, of which waited for: 7 -> 7; matrix products, arithmetic and copies ran while one was open for 0% -> 0% of each run, Pallas kernels for 13% -> 14%
where the time goes in v3:
time: 60.3 us; the launch traced here: 60 us
  waiting for transfers between devices  28.6 us (47%)
  starting transfers between devices  16.4 us (27%)
  Pallas kernels  13.2 us (22%)
  local copies, waits for them, and re-layouts  1.68 us (3%)
    ppermute x7, waiting for transfers between devices, exchange(): return lax.ppermute(value, 'win', pairs)  15.6 us
    ppermute x6, waiting for transfers between devices, flip(): return lax.ppermute(value, axis, pairs)  13 us
    ppermute x7, starting transfers between devices, exchange(): return lax.ppermute(value, 'win', pairs)  11.2 us
    ppermute x6, starting transfers between devices, flip(): return lax.ppermute(value, axis, pairs)  5.19 us
    pallas_call x1, Pallas kernels, lesser_couple(): pl.pallas_call(functools.partial(lesser_couple_kernel, first), out_shape=...  4.15 us
    pallas_call x1, Pallas kernels, sum_couple(): pl.pallas_call(functools.partial(sum_couple_kernel, [len(term) for term i...  3.23 us
    unnamed x8, local copies, waits for them, and re-layouts  1.68 us
    pallas_call x1, Pallas kernels, lesser_rest(): pl.pallas_call(functools.partial(lesser_rest_kernel, first), out_shape=[k...  1.62 us
  transfers between devices with their start and end apart: 13, of which 7 were waited for; matrix products, arithmetic and copies ran while one was open for 0% of the time, Pallas kernels for 14%

profile of v3, /device:TPU:0, one launch (start us, length us, event | category | flops | bytes accessed | tf_op | source)
XLA Modules:
  0.0 60.0 jit_solution(12989171158086942947)
XLA Ops:
  0.0 4.1 %lesser_couple.1 = (bf16[1,2,2,128,128]{4,3,2,1,0:T(8,128)(2,1)S(1)}, bf16[1,2,2,128,128]{4,3,2,1,0:T(8,128)(2,1)S(1)}, bf16[1,2,2,128,128]{4,3,2,1,0:T(8,128)(2,1)S(1)}, bf16[1,2,2,128,128]{4,3,2,1,0:T(8,128)(2,1)S(1)}) custom-call(s32[1]{0:T(128)} %bitcast.place_ref, s32[3,8]{1,0:T(4,128)} %bitcast.3, bf16[3,128,128]{2,1,0:T(8,128)(2,1)} %coupling_ref.3, ...), custom_call_target="tpu_custom_call" | custom-call | flops 671088640 | bytes 1572864 | tf_op jit(solution)/shard_map/lesser_couple/pallas_call | solution.py:215
  4.2 0.6 collective-permute-start.4
  4.7 1.6 %lesser_begin.1.refs_2_ = bf16[1,4,2,128,128]{4,3,2,1,0:T(8,128)(2,1)S(1)} custom-call(bf16[2,8,2,128,128]{4,3,2,1,0:T(8,128)(2,1)} %refs_0_.3, bf16[2,8,2,128,128]{4,3,2,1,0:T(8,128)(2,1)} %refs_1_.3), custom_call_target="tpu_custom_call" | custom-call | flops 134217728 | bytes 786432 | tf_op jit(solution)/shard_map/lesser_begin/pallas_call | solution.py:170
  6.3 1.6 %lesser_rest.1 = (bf16[1,4,2,128,128]{4,3,2,1,0:T(8,128)(2,1)S(1)}, bf16[1,8,2,128,128]{4,3,2,1,0:T(8,128)(2,1)S(1)}) custom-call(bf16[2,8,2,128,128]{4,3,2,1,0:T(8,128)(2,1)} %refs_0_.3, bf16[2,8,2,128,128]{4,3,2,1,0:T(8,128)(2,1)} %refs_1_.3, bf16[1,4,2,128,128]{4,3,2,1,0:T(8,128)(2,1)S(1)} %lesser_begin.1.refs_2_), custom_call_target="tpu_custom_call" | custom-call | flops 134217728 | bytes 786432 | tf_op jit(solution)/shard_map/lesser_rest/pallas_call | solution.py:184
  8.0 3.6 %collective-permute-start.3 = (bf16[1,8,2,128,128]{4,3,2,1,0:T(8,128)(2,1)S(1)}, bf16[1,8,2,128,128]{4,3,2,1,0:T(8,128)(2,1)S(1)}, u32[]{:S(2)}, u32[]{:S(2)}) collective-permute-start(bf16[1,8,2,128,128]{4,3,2,1,0:T(8,128)(2,1)S(1)} %get-tuple-element.16), channel_id=1, source_target_pairs={{0,16},{4,20},{8,0},{12,4},{16,24},{20,28},{24,8},{28,12},{1,17},{... | collective-permute-start | bytes 1572872 | tf_op jit(solution)/shard_map/ppermute | solution.py:403
  11.6 1.5 %collective-permute-start = (bf16[1,8,2,128,128]{4,3,2,1,0:T(8,128)(2,1)S(1)}, bf16[1,8,2,128,128]{4,3,2,1,0:T(8,128)(2,1)}, u32[]{:S(2)}, u32[]{:S(2)}) collective-permute-start(bf16[1,8,2,128,128]{4,3,2,1,0:T(8,128)(2,1)S(1)} %get-tuple-element.16), channel_id=1, source_target_pairs={{0,4},{4,0},{8,12},{12,8},{16,20},{20,16},{24,28},{28,24},{1,5},{5... | collective-permute-start | bytes 1572872 | tf_op jit(solution)/shard_map/ppermute | solution.py:403
  13.1 1.5 %collective-permute-start.5 = (bf16[1,2,2,128,128]{4,3,2,1,0:T(8,128)(2,1)S(1)}, bf16[1,2,2,128,128]{4,3,2,1,0:T(8,128)(2,1)S(1)}, u32[]{:S(2)}, u32[]{:S(2)}) collective-permute-start(bf16[1,2,2,128,128]{4,3,2,1,0:T(8,128)(2,1)S(1)} %get-tuple-element.21), channel_id=1, source_target_pairs={{0,2},{1,3},{2,0},{3,1},{4,6},{5,7},{6,4},{7,5},{8,10},{9,11},{10,... | collective-permute-start | bytes 393224 | tf_op jit(solution)/shard_map/ppermute | solution.py:22
  14.6 0.0 collective-permute-start.1
  14.6 1.9 %collective-permute-start.2 = (bf16[1,4,2,128,128]{4,3,2,1,0:T(8,128)(2,1)S(1)}, bf16[1,4,2,128,128]{4,3,2,1,0:T(8,128)(2,1)S(1)}, u32[]{:S(2)}, u32[]{:S(2)}) collective-permute-start(bf16[1,4,2,128,128]{4,3,2,1,0:T(8,128)(2,1)S(1)} %get-tuple-element.17), channel_id=1, source_target_pairs={{0,8},{4,12},{8,24},{12,28},{16,0},{20,4},{24,16},{28,20},{1,9},{5... | collective-permute-start | bytes 786440 | tf_op jit(solution)/shard_map/ppermute | solution.py:403
  16.5 1.9 %collective-permute-done.5.refs_2_ = bf16[1,2,2,128,128]{4,3,2,1,0:T(8,128)(2,1)S(1)} collective-permute-done((bf16[1,2,2,128,128]{4,3,2,1,0:T(8,128)(2,1)S(1)}, bf16[1,2,2,128,128]{4,3,2,1,0:T(8,128)(2,1)S(1)}, u32[]{:S(2)}, u32[]{:S(2)}) %collective-permute-start.5) | collective-permute-done | bytes 131104 | tf_op jit(solution)/shard_map/ppermute | solution.py:22
  18.4 0.3 collective-permute-start.6
  18.7 5.4 %collective-permute-done.6.refs_3_ = bf16[1,2,2,128,128]{4,3,2,1,0:T(8,128)(2,1)S(1)} collective-permute-done((bf16[1,2,2,128,128]{4,3,2,1,0:T(8,128)(2,1)S(1)}, bf16[1,2,2,128,128]{4,3,2,1,0:T(8,128)(2,1)S(1)}, u32[]{:S(2)}, u32[]{:S(2)}) %collective-permute-start.6) | collective-permute-done | bytes 131104 | tf_op jit(solution)/shard_map/ppermute | solution.py:22
  24.1 0.8 %stack.1 = bf16[4,1,2,2,128,128]{5,4,3,2,1,0:T(8,128)(2,1)} custom-call(bf16[1,2,2,128,128]{4,3,2,1,0:T(8,128)(2,1)S(1)} %get-tuple-element.19.refs_0_, bf16[1,2,2,128,128]{4,3,2,1,0:T(8,128)(2,1)S(1)} %collective-permute-done.4.refs_1_, bf16[1,2,2,128,128]{4,3,2,1,0:T(8,128)(2,1)S(1)} %collective-permute-done.5.refs_2_, ...), custom_call_target="tpu_custom_call" | custom-call | tf_op jit(solution)/shard_map/stack/pallas_call | solution.py:375
  25.0 1.6 %collective-permute-start.9 = (bf16[4,1,2,2,128,128]{5,4,3,2,1,0:T(8,128)(2,1)}, bf16[4,1,2,2,128,128]{5,4,3,2,1,0:T(8,128)(2,1)S(1)}, u32[]{:S(2)}, u32[]{:S(2)}) collective-permute-start(bf16[4,1,2,2,128,128]{5,4,3,2,1,0:T(8,128)(2,1)} %stack.1), channel_id=1, source_target_pairs={{0,16},{4,20},{8,0},{12,4},{16,24},{20,28},{24,8},{28,12},{1,17},{... | collective-permute-start | bytes 1572872 | tf_op jit(solution)/shard_map/ppermute | solution.py:403
  26.6 4.4 %collective-permute-done.1.refs_1_ = bf16[1,4,2,128,128]{4,3,2,1,0:T(8,128)(2,1)S(1)} collective-permute-done((bf16[1,4,2,128,128]{4,3,2,1,0:T(8,128)(2,1)S(1)}, bf16[1,4,2,128,128]{4,3,2,1,0:T(8,128)(2,1)S(1)}, u32[]{:S(2)}, u32[]{:S(2)}) %collective-permute-start.1) | collective-permute-done | bytes 262176 | tf_op jit(solution)/shard_map/ppermute | solution.py:403
  31.1 1.0 %collective-permute-start.8 = (bf16[4,1,2,2,128,128]{5,4,3,2,1,0:T(8,128)(2,1)}, bf16[4,1,2,2,128,128]{5,4,3,2,1,0:T(8,128)(2,1)S(1)}, u32[]{:S(2)}, u32[]{:S(2)}) collective-permute-start(bf16[4,1,2,2,128,128]{5,4,3,2,1,0:T(8,128)(2,1)} %stack.1), channel_id=1, source_target_pairs={{0,8},{4,12},{8,24},{12,28},{16,0},{20,4},{24,16},{28,20},{1,9},{5... | collective-permute-start | bytes 1572872 | tf_op jit(solution)/shard_map/ppermute | solution.py:403
  32.1 5.0 %collective-permute-done.2.refs_2_ = bf16[1,4,2,128,128]{4,3,2,1,0:T(8,128)(2,1)S(1)} collective-permute-done((bf16[1,4,2,128,128]{4,3,2,1,0:T(8,128)(2,1)S(1)}, bf16[1,4,2,128,128]{4,3,2,1,0:T(8,128)(2,1)S(1)}, u32[]{:S(2)}, u32[]{:S(2)}) %collective-permute-start.2) | collective-permute-done | bytes 262176 | tf_op jit(solution)/shard_map/ppermute | solution.py:403
  37.1 1.5 %collective-permute-start.7 = (bf16[4,1,2,2,128,128]{5,4,3,2,1,0:T(8,128)(2,1)}, bf16[4,1,2,2,128,128]{5,4,3,2,1,0:T(8,128)(2,1)S(1)}, u32[]{:S(2)}, u32[]{:S(2)}) collective-permute-start(bf16[4,1,2,2,128,128]{5,4,3,2,1,0:T(8,128)(2,1)} %stack.1), channel_id=1, source_target_pairs={{0,4},{4,0},{8,12},{12,8},{16,20},{20,16},{24,28},{28,24},{1,5},{5... | collective-permute-start | bytes 1572872 | tf_op jit(solution)/shard_map/ppermute | solution.py:403
  38.6 0.0 collective-permute-done.refs_0_
  38.6 0.8 %copy-done.1 = bf16[1,8,2,128,128]{4,3,2,1,0:T(8,128)(2,1)} copy-done((bf16[1,8,2,128,128]{4,3,2,1,0:T(8,128)(2,1)}, bf16[1,8,2,128,128]{4,3,2,1,0:T(8,128)(2,1)S(1)}, u32[]{:S(2)}) %copy-start.1) | copy-done | bytes 524312
  39.4 3.2 %sum_couple.1 = (f32[3,8,128]{2,1,0:T(8,128)S(1)}, bf16[1,2,2,128,128]{4,3,2,1,0:T(8,128)(2,1)}, bf16[1,2,2,128,128]{4,3,2,1,0:T(8,128)(2,1)}, bf16[1,2,2,128,12...) custom-call(s32[1]{0:T(128)} %bitcast.place_ref, s32[1]{0:T(128)} %bitcast.1.odd_ref, s32[3]{0:T(128)} %bit_shifts_ref.1, ...), custom_call_target="tpu_custom_call" | custom-call | flops 402653184 | bytes 1572864 | tf_op jit(solution)/shard_map/sum_couple/pallas_call | solution.py:266
  42.6 0.0 collective-permute-start.10
  42.6 1.5 %collective-permute-start.11 = (bf16[1,2,2,128,128]{4,3,2,1,0:T(8,128)(2,1)}, bf16[1,2,2,128,128]{4,3,2,1,0:T(8,128)(2,1)S(1)}, u32[]{:S(2)}, u32[]{:S(2)}) collective-permute-start(bf16[1,2,2,128,128]{4,3,2,1,0:T(8,128)(2,1)} %get-tuple-element.25), channel_id=1, source_target_pairs={{0,2},{1,3},{2,0},{3,1},{4,6},{5,7},{6,4},{7,5},{8,10},{9,11},{10,... | collective-permute-start | bytes 393224 | tf_op jit(solution)/shard_map/ppermute | solution.py:22
  44.2 0.0 collective-permute-done.10.refs_1_
  44.2 1.3 %collective-permute-start.12 = (bf16[1,2,2,128,128]{4,3,2,1,0:T(8,128)(2,1)}, bf16[1,2,2,128,128]{4,3,2,1,0:T(8,128)(2,1)S(1)}, u32[]{:S(2)}, u32[]{:S(2)}) collective-permute-start(bf16[1,2,2,128,128]{4,3,2,1,0:T(8,128)(2,1)} %get-tuple-element.26), channel_id=1, source_target_pairs={{0,3},{1,2},{2,1},{3,0},{4,7},{5,6},{6,5},{7,4},{8,11},{9,10},{10,... | collective-permute-start | bytes 393224 | tf_op jit(solution)/shard_map/ppermute | solution.py:22
  45.5 3.8 %collective-permute-done.11.refs_2_ = bf16[1,2,2,128,128]{4,3,2,1,0:T(8,128)(2,1)S(1)} collective-permute-done((bf16[1,2,2,128,128]{4,3,2,1,0:T(8,128)(2,1)}, bf16[1,2,2,128,128]{4,3,2,1,0:T(8,128)(2,1)S(1)}, u32[]{:S(2)}, u32[]{:S(2)}) %collective-permute-start.11) | collective-permute-done | bytes 131104 | tf_op jit(solution)/shard_map/ppermute | solution.py:22
  49.2 1.9 %collective-permute-done.12.refs_3_ = bf16[1,2,2,128,128]{4,3,2,1,0:T(8,128)(2,1)S(1)} collective-permute-done((bf16[1,2,2,128,128]{4,3,2,1,0:T(8,128)(2,1)}, bf16[1,2,2,128,128]{4,3,2,1,0:T(8,128)(2,1)S(1)}, u32[]{:S(2)}, u32[]{:S(2)}) %collective-permute-start.12) | collective-permute-done | bytes 131104 | tf_op jit(solution)/shard_map/ppermute | solution.py:22
  51.1 0.9 %copy-done = bf16[1,2,2,128,128]{4,3,2,1,0:T(8,128)(2,1)S(1)} copy-done((bf16[1,2,2,128,128]{4,3,2,1,0:T(8,128)(2,1)S(1)}, bf16[1,2,2,128,128]{4,3,2,1,0:T(8,128)(2,1)}, u32[]{:S(2)}) %copy-start) | copy-done | bytes 131096
  52.0 0.8 %place_first.1.refs_3_ = bf16[8,2,2,128,128]{4,3,2,1,0:T(8,128)(2,1)} custom-call(s32[1]{0:T(128)} %bitcast.place_ref, bf16[1,2,2,128,128]{4,3,2,1,0:T(8,128)(2,1)S(1)} %copy-done, bf16[1,2,2,128,128]{4,3,2,1,0:T(8,128)(2,1)S(1)} %collective-permute-done.10.refs_1_, bf16[1,2,2,128,128]{4,3,2,1,0:T(8,128)(2,1)S(1)} %collective-permute-done.11.refs_2_, ...), custom_call_target="tpu_custom_call" | custom-call | tf_op jit(solution)/shard_map/place_first/pallas_call | solution.py:318
  52.8 6.2 %collective-permute-done.8.refs_1_ = bf16[4,1,2,2,128,128]{5,4,3,2,1,0:T(8,128)(2,1)S(1)} collective-permute-done((bf16[4,1,2,2,128,128]{5,4,3,2,1,0:T(8,128)(2,1)}, bf16[4,1,2,2,128,128]{5,4,3,2,1,0:T(8,128)(2,1)S(1)}, u32[]{:S(2)}, u32[]{:S(2)}) %collective-permute-start.8) | collective-permute-done | bytes 524320 | tf_op jit(solution)/shard_map/ppermute | solution.py:403
  59.0 0.0 collective-permute-done.7.refs_0_
  59.0 1.0 %place_second.1 = bf16[8,2,2,128,128]{4,3,2,1,0:T(8,128)(2,1)} custom-call(f32[3,8,128]{2,1,0:T(8,128)S(1)} %get-tuple-element.18.weights_ref, bf16[4,1,2,2,128,128]{5,4,3,2,1,0:T(8,128)(2,1)S(1)} %collective-permute-done.7.refs_0_, bf16[4,1,2,2,128,128]{5,4,3,2,1,0:T(8,128)(2,1)S(1)} %collective-permute-done.8.refs_1_, ...), custom_call_target="tpu_custom_call", output_to_operand_aliasing={{}: (4, {})} | custom-call | tf_op jit(solution)/shard_map/place_second/pallas_call | solution.py:350
  (9 shorter events, 0.0 us)
Async XLA Ops:
  4.2 10.5 %collective-permute-start.4 = (bf16[1,2,2,128,128]{4,3,2,1,0:T(8,128)(2,1)S(1)}, bf16[1,2,2,128,128]{4,3,2,1,0:T(8,128)(2,1)S(1)}, u32[]{:S(2)}, u32[]{:S(2)}) collective-permute-start(bf16[1,2,2,128,128]{4,3,2,1,0:T(8,128)(2,1)S(1)} %get-tuple-element.20), channel_id=1, source_target_pairs={{0,1},{1,0},{2,3},{3,2},{4,5},{5,4},{6,7},{7,6},{8,9},{9,8},{10,11... | collective-permute-start | bytes 393224 | tf_op jit(solution)/shard_map/ppermute | solution.py:22
  8.0 30.6 %collective-permute-start.3 = (bf16[1,8,2,128,128]{4,3,2,1,0:T(8,128)(2,1)S(1)}, bf16[1,8,2,128,128]{4,3,2,1,0:T(8,128)(2,1)S(1)}, u32[]{:S(2)}, u32[]{:S(2)}) collective-permute-start(bf16[1,8,2,128,128]{4,3,2,1,0:T(8,128)(2,1)S(1)} %get-tuple-element.16), channel_id=1, source_target_pairs={{0,16},{4,20},{8,0},{12,4},{16,24},{20,28},{24,8},{28,12},{1,17},{... | collective-permute-start | bytes 1572872 | tf_op jit(solution)/shard_map/ppermute | solution.py:403
  11.6 27.0 %collective-permute-start = (bf16[1,8,2,128,128]{4,3,2,1,0:T(8,128)(2,1)S(1)}, bf16[1,8,2,128,128]{4,3,2,1,0:T(8,128)(2,1)}, u32[]{:S(2)}, u32[]{:S(2)}) collective-permute-start(bf16[1,8,2,128,128]{4,3,2,1,0:T(8,128)(2,1)S(1)} %get-tuple-element.16), channel_id=1, source_target_pairs={{0,4},{4,0},{8,12},{12,8},{16,20},{20,16},{24,28},{28,24},{1,5},{5... | collective-permute-start | bytes 1572872 | tf_op jit(solution)/shard_map/ppermute | solution.py:403
  13.1 5.3 %collective-permute-start.5 = (bf16[1,2,2,128,128]{4,3,2,1,0:T(8,128)(2,1)S(1)}, bf16[1,2,2,128,128]{4,3,2,1,0:T(8,128)(2,1)S(1)}, u32[]{:S(2)}, u32[]{:S(2)}) collective-permute-start(bf16[1,2,2,128,128]{4,3,2,1,0:T(8,128)(2,1)S(1)} %get-tuple-element.21), channel_id=1, source_target_pairs={{0,2},{1,3},{2,0},{3,1},{4,6},{5,7},{6,4},{7,5},{8,10},{9,11},{10,... | collective-permute-start | bytes 393224 | tf_op jit(solution)/shard_map/ppermute | solution.py:22
  14.6 16.4 %collective-permute-start.1 = (bf16[1,4,2,128,128]{4,3,2,1,0:T(8,128)(2,1)S(1)}, bf16[1,4,2,128,128]{4,3,2,1,0:T(8,128)(2,1)S(1)}, u32[]{:S(2)}, u32[]{:S(2)}) collective-permute-start(bf16[1,4,2,128,128]{4,3,2,1,0:T(8,128)(2,1)S(1)} %lesser_begin.1.refs_2_), channel_id=1, source_target_pairs={{0,8},{4,12},{8,24},{12,28},{16,0},{20,4},{24,16},{28,20},{1,9},{5... | collective-permute-start | bytes 786440 | tf_op jit(solution)/shard_map/ppermute | solution.py:403
  14.6 22.5 %collective-permute-start.2 = (bf16[1,4,2,128,128]{4,3,2,1,0:T(8,128)(2,1)S(1)}, bf16[1,4,2,128,128]{4,3,2,1,0:T(8,128)(2,1)S(1)}, u32[]{:S(2)}, u32[]{:S(2)}) collective-permute-start(bf16[1,4,2,128,128]{4,3,2,1,0:T(8,128)(2,1)S(1)} %get-tuple-element.17), channel_id=1, source_target_pairs={{0,8},{4,12},{8,24},{12,28},{16,0},{20,4},{24,16},{28,20},{1,9},{5... | collective-permute-start | bytes 786440 | tf_op jit(solution)/shard_map/ppermute | solution.py:403
  18.4 5.7 %collective-permute-start.6 = (bf16[1,2,2,128,128]{4,3,2,1,0:T(8,128)(2,1)S(1)}, bf16[1,2,2,128,128]{4,3,2,1,0:T(8,128)(2,1)S(1)}, u32[]{:S(2)}, u32[]{:S(2)}) collective-permute-start(bf16[1,2,2,128,128]{4,3,2,1,0:T(8,128)(2,1)S(1)} %get-tuple-element.22), channel_id=1, source_target_pairs={{0,3},{1,2},{2,1},{3,0},{4,7},{5,6},{6,5},{7,4},{8,11},{9,10},{10,... | collective-permute-start | bytes 393224 | tf_op jit(solution)/shard_map/ppermute | solution.py:22
  25.0 27.8 %collective-permute-start.9 = (bf16[4,1,2,2,128,128]{5,4,3,2,1,0:T(8,128)(2,1)}, bf16[4,1,2,2,128,128]{5,4,3,2,1,0:T(8,128)(2,1)S(1)}, u32[]{:S(2)}, u32[]{:S(2)}) collective-permute-start(bf16[4,1,2,2,128,128]{5,4,3,2,1,0:T(8,128)(2,1)} %stack.1), channel_id=1, source_target_pairs={{0,16},{4,20},{8,0},{12,4},{16,24},{20,28},{24,8},{28,12},{1,17},{... | collective-permute-start | bytes 1572872 | tf_op jit(solution)/shard_map/ppermute | solution.py:403
  31.1 7.6 %copy-start.2 = (bf16[1,4,2,128,128]{4,3,2,1,0:T(8,128)(2,1)}, bf16[1,4,2,128,128]{4,3,2,1,0:T(8,128)(2,1)S(1)}, u32[]{:S(2)}) copy-start(bf16[1,4,2,128,128]{4,3,2,1,0:T(8,128)(2,1)S(1)} %collective-permute-done.1.refs_1_) | copy-start | bytes 786436
  31.1 27.9 %collective-permute-start.8 = (bf16[4,1,2,2,128,128]{5,4,3,2,1,0:T(8,128)(2,1)}, bf16[4,1,2,2,128,128]{5,4,3,2,1,0:T(8,128)(2,1)S(1)}, u32[]{:S(2)}, u32[]{:S(2)}) collective-permute-start(bf16[4,1,2,2,128,128]{5,4,3,2,1,0:T(8,128)(2,1)} %stack.1), channel_id=1, source_target_pairs={{0,8},{4,12},{8,24},{12,28},{16,0},{20,4},{24,16},{28,20},{1,9},{5... | collective-permute-start | bytes 1572872 | tf_op jit(solution)/shard_map/ppermute | solution.py:403
  37.1 1.5 %copy-start.3 = (bf16[1,4,2,128,128]{4,3,2,1,0:T(8,128)(2,1)}, bf16[1,4,2,128,128]{4,3,2,1,0:T(8,128)(2,1)S(1)}, u32[]{:S(2)}) copy-start(bf16[1,4,2,128,128]{4,3,2,1,0:T(8,128)(2,1)S(1)} %collective-permute-done.2.refs_2_) | copy-start | bytes 786436
  37.1 21.9 %collective-permute-start.7 = (bf16[4,1,2,2,128,128]{5,4,3,2,1,0:T(8,128)(2,1)}, bf16[4,1,2,2,128,128]{5,4,3,2,1,0:T(8,128)(2,1)S(1)}, u32[]{:S(2)}, u32[]{:S(2)}) collective-permute-start(bf16[4,1,2,2,128,128]{5,4,3,2,1,0:T(8,128)(2,1)} %stack.1), channel_id=1, source_target_pairs={{0,4},{4,0},{8,12},{12,8},{16,20},{20,16},{24,28},{28,24},{1,5},{5... | collective-permute-start | bytes 1572872 | tf_op jit(solution)/shard_map/ppermute | solution.py:403
  38.6 0.8 %copy-start.1 = (bf16[1,8,2,128,128]{4,3,2,1,0:T(8,128)(2,1)}, bf16[1,8,2,128,128]{4,3,2,1,0:T(8,128)(2,1)S(1)}, u32[]{:S(2)}) copy-start(bf16[1,8,2,128,128]{4,3,2,1,0:T(8,128)(2,1)S(1)} %collective-permute-done.3.refs_3_) | copy-start | bytes 1572868
  42.6 1.6 %collective-permute-start.10 = (bf16[1,2,2,128,128]{4,3,2,1,0:T(8,128)(2,1)}, bf16[1,2,2,128,128]{4,3,2,1,0:T(8,128)(2,1)S(1)}, u32[]{:S(2)}, u32[]{:S(2)}) collective-permute-start(bf16[1,2,2,128,128]{4,3,2,1,0:T(8,128)(2,1)} %get-tuple-element.24), channel_id=1, source_target_pairs={{0,1},{1,0},{2,3},{3,2},{4,5},{5,4},{6,7},{7,6},{8,9},{9,8},{10,11... | collective-permute-start | bytes 393224 | tf_op jit(solution)/shard_map/ppermute | solution.py:22
  42.6 6.6 %collective-permute-start.11 = (bf16[1,2,2,128,128]{4,3,2,1,0:T(8,128)(2,1)}, bf16[1,2,2,128,128]{4,3,2,1,0:T(8,128)(2,1)S(1)}, u32[]{:S(2)}, u32[]{:S(2)}) collective-permute-start(bf16[1,2,2,128,128]{4,3,2,1,0:T(8,128)(2,1)} %get-tuple-element.25), channel_id=1, source_target_pairs={{0,2},{1,3},{2,0},{3,1},{4,6},{5,7},{6,4},{7,5},{8,10},{9,11},{10,... | collective-permute-start | bytes 393224 | tf_op jit(solution)/shard_map/ppermute | solution.py:22
  44.2 6.9 %collective-permute-start.12 = (bf16[1,2,2,128,128]{4,3,2,1,0:T(8,128)(2,1)}, bf16[1,2,2,128,128]{4,3,2,1,0:T(8,128)(2,1)S(1)}, u32[]{:S(2)}, u32[]{:S(2)}) collective-permute-start(bf16[1,2,2,128,128]{4,3,2,1,0:T(8,128)(2,1)} %get-tuple-element.26), channel_id=1, source_target_pairs={{0,3},{1,2},{2,1},{3,0},{4,7},{5,6},{6,5},{7,4},{8,11},{9,10},{10,... | collective-permute-start | bytes 393224 | tf_op jit(solution)/shard_map/ppermute | solution.py:22
  51.1 0.9 %copy-start = (bf16[1,2,2,128,128]{4,3,2,1,0:T(8,128)(2,1)S(1)}, bf16[1,2,2,128,128]{4,3,2,1,0:T(8,128)(2,1)}, u32[]{:S(2)}) copy-start(bf16[1,2,2,128,128]{4,3,2,1,0:T(8,128)(2,1)} %get-tuple-element.23.refs_0_) | copy-start | bytes 393220

commit v4 on v3

--- a/solution.py
+++ b/solution.py
@@ -12,9 +12,11 @@
 SMEM = pl.BlockSpec(memory_space=pltpu.SMEM)
 VMEM = pl.BlockSpec(memory_space=pltpu.VMEM)
 ANY = pl.BlockSpec(memory_space=pl.ANY)
+HBM = pl.BlockSpec(memory_space=pltpu.HBM)
 UNROLL = 8
 GROUP = 4
 RESIDENT_BYTES = 1600 * 1024
+PARAMS = pltpu.CompilerParams(vmem_limit_bytes=40 * 2**20)
 
 
 def flip(value, axis, mask):
@@ -29,7 +31,7 @@
 
 
 def over_blocks(count, step):
-    chunk = math.gcd(count, UNROLL)
+    chunk = count if count <= UNROLL else math.gcd(count, UNROLL)
     if count == chunk:
         for block in range(count):
             step(block)
@@ -70,25 +72,28 @@
     for i in items:
         for copy in loads[i]:
             copy.wait()
-    for i in items:
-        both = lesser_of(green[i, 0], green[i, 1], sigma[i, 0], sigma[i, 1])
-        yield i, both.astype(jnp.bfloat16)
-
-
-def lesser_of(real, imag, sigma_real, sigma_imag):
-    left = jnp.concatenate([real, imag], axis=1)
+    products = [product_of(green[i], sigma[i]) for i in items]
+    for i, product in zip(items, products):
+        yield i, lesser_of(product, green[i]).astype(jnp.bfloat16)
+
+
+def product_of(green, sigma):
     right = jnp.concatenate(
         [
-            jnp.concatenate([sigma_real, sigma_imag], axis=1),
-            jnp.concatenate([-sigma_imag, sigma_real], axis=1),
+            jnp.concatenate([sigma[0], sigma[1]], axis=1),
+            jnp.concatenate([-sigma[1], sigma[0]], axis=1),
         ],
         axis=0,
     )
-    product = contract(left, right, ((1,), (0,))).astype(jnp.bfloat16)
+    left = jnp.concatenate([green[0], green[1]], axis=1)
+    return contract(left, right, ((1,), (0,))).astype(jnp.bfloat16)
+
+
+def lesser_of(product, green):
     flipped = jnp.concatenate(
         [
-            jnp.concatenate([real, -imag], axis=1),
-            jnp.concatenate([imag, real], axis=1),
+            jnp.concatenate([green[0], -green[1]], axis=1),
+            jnp.concatenate([green[1], green[0]], axis=1),
         ],
         axis=0,
     )
@@ -170,10 +175,11 @@
     return pl.pallas_call(
         functools.partial(lesser_kernel, first, 0),
         out_shape=kept((count, cut, *own)),
-        in_specs=[ANY, ANY],
+        in_specs=[HBM, HBM],
         out_specs=VMEM,
         scratch_shapes=lesser_scratch(count, cut, own),
         cost_estimate=lesser_cost(count, cut, own[-1]),
+        compiler_params=PARAMS,
         name="lesser_begin",
     )(retarded, sigma_in)
 
@@ -184,10 +190,11 @@
     return pl.pallas_call(
         functools.partial(lesser_rest_kernel, first),
         out_shape=[kept((count, rest, *own)), kept((count, blocks, *own))],
-        in_specs=[ANY, ANY, VMEM],
+        in_specs=[HBM, HBM, VMEM],
         out_specs=[VMEM, VMEM],
         scratch_shapes=lesser_scratch(count, rest, own),
         cost_estimate=lesser_cost(count, rest, own[-1]),
+        compiler_params=PARAMS,
         name="lesser_rest",
     )(retarded, sigma_in, *in_vmem([begun]))
 
@@ -215,7 +222,7 @@
     return pl.pallas_call(
         functools.partial(lesser_couple_kernel, first),
         out_shape=[kept((count, blocks // atoms, *own))] * atoms,
-        in_specs=[SMEM, SMEM, VMEM, ANY, ANY],
+        in_specs=[SMEM, SMEM, VMEM, HBM, HBM],
         out_specs=[VMEM] * atoms,
         scratch_shapes=[
             pltpu.VMEM((blocks, directions, *own), jnp.bfloat16),
@@ -227,6 +234,7 @@
             bytes_accessed=count * blocks * 12 * size**2,
             transcendentals=0,
         ),
+        compiler_params=PARAMS,
         name="lesser_couple",
     )(place, neighbors, coupling, retarded, sigma_in)
 
@@ -241,26 +249,27 @@
     weights = weights_of(len(terms), odd_ref, bit_shifts_ref, occupation_ref)
     for at, weight in enumerate(weights):
         weights_ref[at] = jnp.full(weights_ref.shape[1:], weight, jnp.float32)
-    span = bent_ref.shape[0] // max(widths)
-    for piece in range(max(widths)):
-
-        def one(at, piece=piece):
+    cuts = [piece.shape[1] for piece in max(terms, key=len)]
+    for piece, span in enumerate(cuts):
+        before = sum(cuts[:piece])
+
+        def one(at, piece=piece, before=before):
             parts = []
             for part in range(2):
                 total = None
                 for weight, term in zip(weights, terms):
-                    block = at if len(term) > 1 else piece * span + at
+                    block = at if len(term) > 1 else before + at
                     value = term[piece % len(term)][0, block, part].astype(jnp.float32)
                     total = weight * value if total is None else total + weight * value
                 parts.append(total.astype(jnp.bfloat16))
-            bend(coupling_ref, jnp.concatenate(parts, axis=1), bent_ref, piece * span + at)
+            bend(coupling_ref, jnp.concatenate(parts, axis=1), bent_ref, before + at)
 
         over_blocks(span, one)
     unbend(place_ref, neighbors_ref, coupling_ref, bent_ref, out_refs, 0)
 
 
 def sum_couple(scalars, coupling, terms, atoms):
-    count, blocks, *own = terms[0][0].shape
+    count, blocks, *own = min(terms, key=len)[0].shape
     directions = coupling.shape[0]
     arrays = [array for term in terms for array in term]
     return pl.pallas_call(
@@ -282,6 +291,7 @@
             bytes_accessed=count * blocks * 12 * own[-1] ** 2,
             transcendentals=0,
         ),
+        compiler_params=PARAMS,
         name="sum_couple",
     )(*scalars, coupling, *arrays)
 
@@ -321,6 +331,7 @@
         in_specs=[SMEM] + [VMEM] * len(pieces),
         out_specs=ANY,
         scratch_shapes=[pltpu.SemaphoreType.DMA((len(pieces),))],
+        compiler_params=PARAMS,
         name="place_first",
     )(place, *in_vmem(pieces))
 
@@ -357,6 +368,7 @@
             pltpu.SemaphoreType.DMA(shape[:2]),
         ],
         input_output_aliases={terms + 1: 0},
+        compiler_params=PARAMS,
         name="place_second",
     )(*in_vmem([weights]), *in_vmem(arrived), out)
 
@@ -378,6 +390,7 @@
         in_specs=[VMEM] * len(pieces),
         out_specs=ANY,
         scratch_shapes=[pltpu.SemaphoreType.DMA((len(pieces),))],
+        compiler_params=PARAMS,
         name="stack",
     )(*in_vmem(pieces))
 
@@ -410,9 +423,12 @@
     terms = len(term_masks(windows))
     half = energies // 2
     rest = energies - half
-    cut = blocks // 2
+    cut = blocks * 3 // 8
     place = lax.axis_index("atom").astype(jnp.int32).reshape(1)
     odd = oddness(lax.axis_index("win"), windows).astype(jnp.int32).reshape(1)
+    retarded, sigma_in = [
+        pltpu.with_memory_space_constraint(array, pltpu.HBM) for array in (retarded, sigma_in)
+    ]
     table = neighbors.T
     begun = lesser_begin(retarded, sigma_in, 0, half, cut)
     arrived_begun = exchange(begun, terms - 2)

time: 60.3 us -> 65.2 us (1.081)
  waiting for transfers between devices: 28.6 us -> 33.1 us
  local copies, waits for them, and re-layouts: 1.68 us -> 4.72 us
  Pallas kernels: 13.2 us -> 11.8 us
  starting transfers between devices: 16.4 us -> 15 us
    ppermute x7, waiting for transfers between devices: 15.6 us -> 19.6 us  [exchange(): return lax.ppermute(value, 'win', pairs)]
    unnamed x8 -> x14, local copies, waits for them, and re-layouts: 1.68 us -> 4.72 us
    pallas_call x1, Pallas kernels: 3.23 us -> 1.75 us  [sum_couple(): pl.pallas_call(functools.partial(sum_couple_kernel, [len(term) for term i...]
    ppermute x7, starting transfers between devices: 11.2 us -> 10.3 us  [exchange(): return lax.ppermute(value, 'win', pairs)]
    pallas_call x1, Pallas kernels: 1.62 us -> 2.46 us  [lesser_rest(): pl.pallas_call(functools.partial(lesser_rest_kernel, first), out_shape=[k...]
  transfers between devices with their start and end apart: 13 -> 13, of which waited for: 7 -> 6; matrix products, arithmetic and copies ran while one was open for 0% -> 0% of each run, Pallas kernels for 14% -> 11%
where the time goes in v4:
time: 65.2 us; the launch traced here: 64.8 us
  waiting for transfers between devices  33.1 us (51%)
  starting transfers between devices  15 us (23%)
  Pallas kernels  11.8 us (18%)
  local copies, waits for them, and re-layouts  4.72 us (7%)
    ppermute x7, waiting for transfers between devices, exchange(): return lax.ppermute(value, 'win', pairs)  19.6 us
    ppermute x6, waiting for transfers between devices, flip(): return lax.ppermute(value, axis, pairs)  13.5 us
    ppermute x7, starting transfers between devices, exchange(): return lax.ppermute(value, 'win', pairs)  10.3 us
    ppermute x6, starting transfers between devices, flip(): return lax.ppermute(value, axis, pairs)  4.79 us
    unnamed x14, local copies, waits for them, and re-layouts  4.72 us
    pallas_call x1, Pallas kernels, lesser_couple(): pl.pallas_call(functools.partial(lesser_couple_kernel, first), out_shape=...  3.67 us
    pallas_call x1, Pallas kernels, lesser_rest(): pl.pallas_call(functools.partial(lesser_rest_kernel, first), out_shape=[k...  2.46 us
    pallas_call x1, Pallas kernels, sum_couple(): pl.pallas_call(functools.partial(sum_couple_kernel, [len(term) for term i...  1.75 us
  transfers between devices with their start and end apart: 13, of which 6 were waited for; matrix products, arithmetic and copies ran while one was open for 0% of the time, Pallas kernels for 11%

profile of v4, /device:TPU:0, one launch (start us, length us, event | category | flops | bytes accessed | tf_op | source)
XLA Modules:
  0.0 64.8 jit_solution(13850621181583686921)
XLA Ops:
  0.0 0.7 %copy-done.4 = s32[8,3]{0,1:T(4,128)S(1)} copy-done((s32[8,3]{0,1:T(4,128)S(1)}, s32[8,3]{0,1:T(4,128)}, u32[]{:S(2)}) %copy-start.4) | copy-done | bytes 120
  0.7 0.9 %copy-done.2 = bf16[3,128,128]{2,1,0:T(8,128)(2,1)S(1)} copy-done((bf16[3,128,128]{2,1,0:T(8,128)(2,1)S(1)}, bf16[3,128,128]{2,1,0:T(8,128)(2,1)}, u32[]{:S(2)}) %copy-start.2) | copy-done | bytes 98328
  1.6 3.7 %lesser_couple.1 = (bf16[1,2,2,128,128]{4,3,2,1,0:T(8,128)(2,1)S(1)}, bf16[1,2,2,128,128]{4,3,2,1,0:T(8,128)(2,1)S(1)}, bf16[1,2,2,128,128]{4,3,2,1,0:T(8,128)(2,1)S(1)}, bf16[1,2,2,128,128]{4,3,2,1,0:T(8,128)(2,1)S(1)}) custom-call(s32[1]{0:T(128)} %bitcast.place_ref, s32[3,8]{1,0:T(4,128)S(1)} %bitcast.3, bf16[3,128,128]{2,1,0:T(8,128)(2,1)S(1)} %copy-done.2, ...), custom_call_target="tpu_custom_call" | custom-call | flops 671088640 | bytes 1572864 | tf_op jit(solution)/shard_map/lesser_couple/pallas_call | solution.py:222
  5.3 0.6 collective-permute-start.4
  5.8 1.4 %lesser_begin.1.refs_2_ = bf16[1,3,2,128,128]{4,3,2,1,0:T(8,128)(2,1)S(1)} custom-call(bf16[2,8,2,128,128]{4,3,2,1,0:T(8,128)(2,1)} %refs_0_.3, bf16[2,8,2,128,128]{4,3,2,1,0:T(8,128)(2,1)} %refs_1_.3), custom_call_target="tpu_custom_call" | custom-call | flops 100663296 | bytes 589824 | tf_op jit(solution)/shard_map/lesser_begin/pallas_call | solution.py:175
  7.3 2.5 %lesser_rest.1 = (bf16[1,5,2,128,128]{4,3,2,1,0:T(8,128)(2,1)S(1)}, bf16[1,8,2,128,128]{4,3,2,1,0:T(8,128)(2,1)}) custom-call(bf16[2,8,2,128,128]{4,3,2,1,0:T(8,128)(2,1)} %refs_0_.3, bf16[2,8,2,128,128]{4,3,2,1,0:T(8,128)(2,1)} %refs_1_.3, bf16[1,3,2,128,128]{4,3,2,1,0:T(8,128)(2,1)S(1)} %lesser_begin.1.refs_2_), custom_call_target="tpu_custom_call" | custom-call | flops 167772160 | bytes 983040 | tf_op jit(solution)/shard_map/lesser_rest/pallas_call | solution.py:190
  9.7 2.6 %collective-permute-start.2 = (bf16[1,5,2,128,128]{4,3,2,1,0:T(8,128)(2,1)S(1)}, bf16[1,5,2,128,128]{4,3,2,1,0:T(8,128)(2,1)S(1)}, u32[]{:S(2)}, u32[]{:S(2)}) collective-permute-start(bf16[1,5,2,128,128]{4,3,2,1,0:T(8,128)(2,1)S(1)} %get-tuple-element.17), channel_id=1, source_target_pairs={{0,8},{4,12},{8,24},{12,28},{16,0},{20,4},{24,16},{28,20},{1,9},{5... | collective-permute-start | bytes 983048 | tf_op jit(solution)/shard_map/ppermute | solution.py:416
  12.4 1.5 %collective-permute-start = (bf16[1,8,2,128,128]{4,3,2,1,0:T(8,128)(2,1)}, bf16[1,8,2,128,128]{4,3,2,1,0:T(8,128)(2,1)S(1)}, u32[]{:S(2)}, u32[]{:S(2)}) collective-permute-start(bf16[1,8,2,128,128]{4,3,2,1,0:T(8,128)(2,1)} %get-tuple-element.16), channel_id=1, source_target_pairs={{0,4},{4,0},{8,12},{12,8},{16,20},{20,16},{24,28},{28,24},{1,5},{5... | collective-permute-start | bytes 1572872 | tf_op jit(solution)/shard_map/ppermute | solution.py:416
  13.8 1.3 %collective-permute-start.3 = (bf16[1,8,2,128,128]{4,3,2,1,0:T(8,128)(2,1)}, bf16[1,8,2,128,128]{4,3,2,1,0:T(8,128)(2,1)S(1)}, u32[]{:S(2)}, u32[]{:S(2)}) collective-permute-start(bf16[1,8,2,128,128]{4,3,2,1,0:T(8,128)(2,1)} %get-tuple-element.16), channel_id=1, source_target_pairs={{0,16},{4,20},{8,0},{12,4},{16,24},{20,28},{24,8},{28,12},{1,17},{... | collective-permute-start | bytes 1572872 | tf_op jit(solution)/shard_map/ppermute | solution.py:416
  15.2 1.5 %collective-permute-start.5 = (bf16[1,2,2,128,128]{4,3,2,1,0:T(8,128)(2,1)S(1)}, bf16[1,2,2,128,128]{4,3,2,1,0:T(8,128)(2,1)S(1)}, u32[]{:S(2)}, u32[]{:S(2)}) collective-permute-start(bf16[1,2,2,128,128]{4,3,2,1,0:T(8,128)(2,1)S(1)} %get-tuple-element.21), channel_id=1, source_target_pairs={{0,2},{1,3},{2,0},{3,1},{4,6},{5,7},{6,4},{7,5},{8,10},{9,11},{10,... | collective-permute-start | bytes 393224 | tf_op jit(solution)/shard_map/ppermute | solution.py:24
  16.7 1.2 %collective-permute-start.1 = (bf16[1,3,2,128,128]{4,3,2,1,0:T(8,128)(2,1)S(1)}, bf16[1,3,2,128,128]{4,3,2,1,0:T(8,128)(2,1)S(1)}, u32[]{:S(2)}, u32[]{:S(2)}) collective-permute-start(bf16[1,3,2,128,128]{4,3,2,1,0:T(8,128)(2,1)S(1)} %lesser_begin.1.refs_2_), channel_id=1, source_target_pairs={{0,8},{4,12},{8,24},{12,28},{16,0},{20,4},{24,16},{28,20},{1,9},{5... | collective-permute-start | bytes 589832 | tf_op jit(solution)/shard_map/ppermute | solution.py:416
  18.0 2.3 %collective-permute-done.5.refs_2_ = bf16[1,2,2,128,128]{4,3,2,1,0:T(8,128)(2,1)S(1)} collective-permute-done((bf16[1,2,2,128,128]{4,3,2,1,0:T(8,128)(2,1)S(1)}, bf16[1,2,2,128,128]{4,3,2,1,0:T(8,128)(2,1)S(1)}, u32[]{:S(2)}, u32[]{:S(2)}) %collective-permute-start.5) | collective-permute-done | bytes 131104 | tf_op jit(solution)/shard_map/ppermute | solution.py:24
  20.3 5.7 %collective-permute-done.6.refs_3_ = bf16[1,2,2,128,128]{4,3,2,1,0:T(8,128)(2,1)S(1)} collective-permute-done((bf16[1,2,2,128,128]{4,3,2,1,0:T(8,128)(2,1)S(1)}, bf16[1,2,2,128,128]{4,3,2,1,0:T(8,128)(2,1)S(1)}, u32[]{:S(2)}, u32[]{:S(2)}) %collective-permute-start.6) | collective-permute-done | bytes 131104 | tf_op jit(solution)/shard_map/ppermute | solution.py:24
  26.0 0.7 %stack.1 = bf16[4,1,2,2,128,128]{5,4,3,2,1,0:T(8,128)(2,1)S(1)} custom-call(bf16[1,2,2,128,128]{4,3,2,1,0:T(8,128)(2,1)S(1)} %get-tuple-element.19.refs_0_, bf16[1,2,2,128,128]{4,3,2,1,0:T(8,128)(2,1)S(1)} %collective-permute-done.4.refs_1_, bf16[1,2,2,128,128]{4,3,2,1,0:T(8,128)(2,1)S(1)} %collective-permute-done.5.refs_2_, ...), custom_call_target="tpu_custom_call" | custom-call | tf_op jit(solution)/shard_map/stack/pallas_call | solution.py:387
  26.7 0.6 collective-permute-start.7
  27.3 9.9 %collective-permute-done.1.refs_1_ = bf16[1,3,2,128,128]{4,3,2,1,0:T(8,128)(2,1)S(1)} collective-permute-done((bf16[1,3,2,128,128]{4,3,2,1,0:T(8,128)(2,1)S(1)}, bf16[1,3,2,128,128]{4,3,2,1,0:T(8,128)(2,1)S(1)}, u32[]{:S(2)}, u32[]{:S(2)}) %collective-permute-start.1) | collective-permute-done | bytes 196640 | tf_op jit(solution)/shard_map/ppermute | solution.py:416
  37.2 0.7 %copy-done = bf16[1,3,2,128,128]{4,3,2,1,0:T(8,128)(2,1)} copy-done((bf16[1,3,2,128,128]{4,3,2,1,0:T(8,128)(2,1)}, bf16[1,3,2,128,128]{4,3,2,1,0:T(8,128)(2,1)S(1)}, u32[]{:S(2)}) %copy-start) | copy-done | bytes 196632
  37.9 0.8 %collective-permute-start.8 = (bf16[4,1,2,2,128,128]{5,4,3,2,1,0:T(8,128)(2,1)S(1)}, bf16[4,1,2,2,128,128]{5,4,3,2,1,0:T(8,128)(2,1)S(1)}, u32[]{:S(2)}, u32[]{:S(2)}) collective-permute-start(bf16[4,1,2,2,128,128]{5,4,3,2,1,0:T(8,128)(2,1)S(1)} %stack.1), channel_id=1, source_target_pairs={{0,8},{4,12},{8,24},{12,28},{16,0},{20,4},{24,16},{28,20},{1,9},{5... | collective-permute-start | bytes 1572872 | tf_op jit(solution)/shard_map/ppermute | solution.py:416
  38.7 2.1 %collective-permute-start.9 = (bf16[4,1,2,2,128,128]{5,4,3,2,1,0:T(8,128)(2,1)S(1)}, bf16[4,1,2,2,128,128]{5,4,3,2,1,0:T(8,128)(2,1)S(1)}, u32[]{:S(2)}, u32[]{:S(2)}) collective-permute-start(bf16[4,1,2,2,128,128]{5,4,3,2,1,0:T(8,128)(2,1)S(1)} %stack.1), channel_id=1, source_target_pairs={{0,16},{4,20},{8,0},{12,4},{16,24},{20,28},{24,8},{28,12},{1,17},{... | collective-permute-start | bytes 1572872 | tf_op jit(solution)/shard_map/ppermute | solution.py:416
  40.8 0.6 copy-done.5
  41.5 0.0 copy-done.6
  41.5 0.9 %copy-done.1 = bf16[1,3,2,128,128]{4,3,2,1,0:T(8,128)(2,1)S(1)} copy-done((bf16[1,3,2,128,128]{4,3,2,1,0:T(8,128)(2,1)S(1)}, bf16[1,3,2,128,128]{4,3,2,1,0:T(8,128)(2,1)}, u32[]{:S(2)}) %copy-start.1) | copy-done | bytes 196632
  42.4 0.9 %copy-done.3 = bf16[3,128,128]{2,1,0:T(8,128)(2,1)S(1)} copy-done((bf16[3,128,128]{2,1,0:T(8,128)(2,1)S(1)}, bf16[3,128,128]{2,1,0:T(8,128)(2,1)}, u32[]{:S(2)}) %copy-start.3) | copy-done | bytes 98328
  43.3 1.7 %sum_couple.1 = (f32[3,8,128]{2,1,0:T(8,128)S(1)}, bf16[1,2,2,128,128]{4,3,2,1,0:T(8,128)(2,1)S(1)}, bf16[1,2,2,128,128]{4,3,2,1,0:T(8,128)(2,1)S(1)}, bf16[1,2,...) custom-call(s32[1]{0:T(128)} %bitcast.place_ref, s32[1]{0:T(128)} %bitcast.1.odd_ref, s32[3]{0:T(128)S(1)} %copy-done.5, ...), custom_call_target="tpu_custom_call" | custom-call | flops 402653184 | bytes 1572864 | tf_op jit(solution)/shard_map/sum_couple/pallas_call | solution.py:275
  45.1 0.1 collective-permute-start.10
  45.2 1.6 %collective-permute-start.11 = (bf16[1,2,2,128,128]{4,3,2,1,0:T(8,128)(2,1)S(1)}, bf16[1,2,2,128,128]{4,3,2,1,0:T(8,128)(2,1)S(1)}, u32[]{:S(2)}, u32[]{:S(2)}) collective-permute-start(bf16[1,2,2,128,128]{4,3,2,1,0:T(8,128)(2,1)S(1)} %get-tuple-element.25), channel_id=1, source_target_pairs={{0,2},{1,3},{2,0},{3,1},{4,6},{5,7},{6,4},{7,5},{8,10},{9,11},{10,... | collective-permute-start | bytes 393224 | tf_op jit(solution)/shard_map/ppermute | solution.py:24
  46.8 1.0 %collective-permute-start.12 = (bf16[1,2,2,128,128]{4,3,2,1,0:T(8,128)(2,1)S(1)}, bf16[1,2,2,128,128]{4,3,2,1,0:T(8,128)(2,1)S(1)}, u32[]{:S(2)}, u32[]{:S(2)}) collective-permute-start(bf16[1,2,2,128,128]{4,3,2,1,0:T(8,128)(2,1)S(1)} %get-tuple-element.26), channel_id=1, source_target_pairs={{0,3},{1,2},{2,1},{3,0},{4,7},{5,6},{6,5},{7,4},{8,11},{9,10},{10,... | collective-permute-start | bytes 393224 | tf_op jit(solution)/shard_map/ppermute | solution.py:24
  47.8 3.8 %collective-permute-done.11.refs_2_ = bf16[1,2,2,128,128]{4,3,2,1,0:T(8,128)(2,1)S(1)} collective-permute-done((bf16[1,2,2,128,128]{4,3,2,1,0:T(8,128)(2,1)S(1)}, bf16[1,2,2,128,128]{4,3,2,1,0:T(8,128)(2,1)S(1)}, u32[]{:S(2)}, u32[]{:S(2)}) %collective-permute-start.11) | collective-permute-done | bytes 131104 | tf_op jit(solution)/shard_map/ppermute | solution.py:24
  51.6 1.7 %collective-permute-done.12.refs_3_ = bf16[1,2,2,128,128]{4,3,2,1,0:T(8,128)(2,1)S(1)} collective-permute-done((bf16[1,2,2,128,128]{4,3,2,1,0:T(8,128)(2,1)S(1)}, bf16[1,2,2,128,128]{4,3,2,1,0:T(8,128)(2,1)S(1)}, u32[]{:S(2)}, u32[]{:S(2)}) %collective-permute-start.12) | collective-permute-done | bytes 131104 | tf_op jit(solution)/shard_map/ppermute | solution.py:24
  53.3 0.8 %place_first.1.refs_3_ = bf16[8,2,2,128,128]{4,3,2,1,0:T(8,128)(2,1)} custom-call(s32[1]{0:T(128)} %bitcast.place_ref, bf16[1,2,2,128,128]{4,3,2,1,0:T(8,128)(2,1)S(1)} %get-tuple-element.23.refs_0_, bf16[1,2,2,128,128]{4,3,2,1,0:T(8,128)(2,1)S(1)} %collective-permute-done.10.refs_1_, bf16[1,2,2,128,128]{4,3,2,1,0:T(8,128)(2,1)S(1)} %collective-permute-done.11.refs_2_, ...), custom_call_target="tpu_custom_call" | custom-call | tf_op jit(solution)/shard_map/place_first/pallas_call | solution.py:328
  54.2 9.6 %collective-permute-done.9.refs_2_ = bf16[4,1,2,2,128,128]{5,4,3,2,1,0:T(8,128)(2,1)S(1)} collective-permute-done((bf16[4,1,2,2,128,128]{5,4,3,2,1,0:T(8,128)(2,1)S(1)}, bf16[4,1,2,2,128,128]{5,4,3,2,1,0:T(8,128)(2,1)S(1)}, u32[]{:S(2)}, u32[]{:S(2)}) %collective-permute-start.9) | collective-permute-done | bytes 524320 | tf_op jit(solution)/shard_map/ppermute | solution.py:416
  63.8 1.0 %place_second.1 = bf16[8,2,2,128,128]{4,3,2,1,0:T(8,128)(2,1)} custom-call(f32[3,8,128]{2,1,0:T(8,128)S(1)} %get-tuple-element.18.weights_ref, bf16[4,1,2,2,128,128]{5,4,3,2,1,0:T(8,128)(2,1)S(1)} %collective-permute-done.7.refs_0_, bf16[4,1,2,2,128,128]{5,4,3,2,1,0:T(8,128)(2,1)S(1)} %collective-permute-done.8.refs_1_, ...), custom_call_target="tpu_custom_call", output_to_operand_aliasing={{}: (4, {})} | custom-call | tf_op jit(solution)/shard_map/place_second/pallas_call | solution.py:361
  (15 shorter events, 0.0 us)
Async XLA Ops:
  0.0 0.7 %copy-start.4 = (s32[8,3]{0,1:T(4,128)S(1)}, s32[8,3]{0,1:T(4,128)}, u32[]{:S(2)}) copy-start(s32[8,3]{0,1:T(4,128)} %param.10) | copy-start | bytes 292
  0.7 0.9 %copy-start.2 = (bf16[3,128,128]{2,1,0:T(8,128)(2,1)S(1)}, bf16[3,128,128]{2,1,0:T(8,128)(2,1)}, u32[]{:S(2)}) copy-start(bf16[3,128,128]{2,1,0:T(8,128)(2,1)} %coupling_ref.3) | copy-start | bytes 294916
  5.3 11.5 %collective-permute-start.4 = (bf16[1,2,2,128,128]{4,3,2,1,0:T(8,128)(2,1)S(1)}, bf16[1,2,2,128,128]{4,3,2,1,0:T(8,128)(2,1)S(1)}, u32[]{:S(2)}, u32[]{:S(2)}) collective-permute-start(bf16[1,2,2,128,128]{4,3,2,1,0:T(8,128)(2,1)S(1)} %get-tuple-element.20), channel_id=1, source_target_pairs={{0,1},{1,0},{2,3},{3,2},{4,5},{5,4},{6,7},{7,6},{8,9},{9,8},{10,11... | collective-permute-start | bytes 393224 | tf_op jit(solution)/shard_map/ppermute | solution.py:24
  9.7 29.0 %collective-permute-start.2 = (bf16[1,5,2,128,128]{4,3,2,1,0:T(8,128)(2,1)S(1)}, bf16[1,5,2,128,128]{4,3,2,1,0:T(8,128)(2,1)S(1)}, u32[]{:S(2)}, u32[]{:S(2)}) collective-permute-start(bf16[1,5,2,128,128]{4,3,2,1,0:T(8,128)(2,1)S(1)} %get-tuple-element.17), channel_id=1, source_target_pairs={{0,8},{4,12},{8,24},{12,28},{16,0},{20,4},{24,16},{28,20},{1,9},{5... | collective-permute-start | bytes 983048 | tf_op jit(solution)/shard_map/ppermute | solution.py:416
  12.4 28.5 %collective-permute-start = (bf16[1,8,2,128,128]{4,3,2,1,0:T(8,128)(2,1)}, bf16[1,8,2,128,128]{4,3,2,1,0:T(8,128)(2,1)S(1)}, u32[]{:S(2)}, u32[]{:S(2)}) collective-permute-start(bf16[1,8,2,128,128]{4,3,2,1,0:T(8,128)(2,1)} %get-tuple-element.16), channel_id=1, source_target_pairs={{0,4},{4,0},{8,12},{12,8},{16,20},{20,16},{24,28},{28,24},{1,5},{5... | collective-permute-start | bytes 1572872 | tf_op jit(solution)/shard_map/ppermute | solution.py:416
  13.8 27.0 %collective-permute-start.3 = (bf16[1,8,2,128,128]{4,3,2,1,0:T(8,128)(2,1)}, bf16[1,8,2,128,128]{4,3,2,1,0:T(8,128)(2,1)S(1)}, u32[]{:S(2)}, u32[]{:S(2)}) collective-permute-start(bf16[1,8,2,128,128]{4,3,2,1,0:T(8,128)(2,1)} %get-tuple-element.16), channel_id=1, source_target_pairs={{0,16},{4,20},{8,0},{12,4},{16,24},{20,28},{24,8},{28,12},{1,17},{... | collective-permute-start | bytes 1572872 | tf_op jit(solution)/shard_map/ppermute | solution.py:416
  15.2 5.1 %collective-permute-start.5 = (bf16[1,2,2,128,128]{4,3,2,1,0:T(8,128)(2,1)S(1)}, bf16[1,2,2,128,128]{4,3,2,1,0:T(8,128)(2,1)S(1)}, u32[]{:S(2)}, u32[]{:S(2)}) collective-permute-start(bf16[1,2,2,128,128]{4,3,2,1,0:T(8,128)(2,1)S(1)} %get-tuple-element.21), channel_id=1, source_target_pairs={{0,2},{1,3},{2,0},{3,1},{4,6},{5,7},{6,4},{7,5},{8,10},{9,11},{10,... | collective-permute-start | bytes 393224 | tf_op jit(solution)/shard_map/ppermute | solution.py:24
  16.7 20.5 %collective-permute-start.1 = (bf16[1,3,2,128,128]{4,3,2,1,0:T(8,128)(2,1)S(1)}, bf16[1,3,2,128,128]{4,3,2,1,0:T(8,128)(2,1)S(1)}, u32[]{:S(2)}, u32[]{:S(2)}) collective-permute-start(bf16[1,3,2,128,128]{4,3,2,1,0:T(8,128)(2,1)S(1)} %lesser_begin.1.refs_2_), channel_id=1, source_target_pairs={{0,8},{4,12},{8,24},{12,28},{16,0},{20,4},{24,16},{28,20},{1,9},{5... | collective-permute-start | bytes 589832 | tf_op jit(solution)/shard_map/ppermute | solution.py:416
  20.3 5.7 %collective-permute-start.6 = (bf16[1,2,2,128,128]{4,3,2,1,0:T(8,128)(2,1)S(1)}, bf16[1,2,2,128,128]{4,3,2,1,0:T(8,128)(2,1)S(1)}, u32[]{:S(2)}, u32[]{:S(2)}) collective-permute-start(bf16[1,2,2,128,128]{4,3,2,1,0:T(8,128)(2,1)S(1)} %get-tuple-element.22), channel_id=1, source_target_pairs={{0,3},{1,2},{2,1},{3,0},{4,7},{5,6},{6,5},{7,4},{8,11},{9,10},{10,... | collective-permute-start | bytes 393224 | tf_op jit(solution)/shard_map/ppermute | solution.py:24
  26.7 27.5 %collective-permute-start.7 = (bf16[4,1,2,2,128,128]{5,4,3,2,1,0:T(8,128)(2,1)S(1)}, bf16[4,1,2,2,128,128]{5,4,3,2,1,0:T(8,128)(2,1)S(1)}, u32[]{:S(2)}, u32[]{:S(2)}) collective-permute-start(bf16[4,1,2,2,128,128]{5,4,3,2,1,0:T(8,128)(2,1)S(1)} %stack.1), channel_id=1, source_target_pairs={{0,4},{4,0},{8,12},{12,8},{16,20},{20,16},{24,28},{28,24},{1,5},{5... | collective-permute-start | bytes 1572872 | tf_op jit(solution)/shard_map/ppermute | solution.py:416
  37.2 0.7 %copy-start = (bf16[1,3,2,128,128]{4,3,2,1,0:T(8,128)(2,1)}, bf16[1,3,2,128,128]{4,3,2,1,0:T(8,128)(2,1)S(1)}, u32[]{:S(2)}) copy-start(bf16[1,3,2,128,128]{4,3,2,1,0:T(8,128)(2,1)S(1)} %collective-permute-done.1.refs_1_) | copy-start | bytes 589828
  37.9 16.3 %collective-permute-start.8 = (bf16[4,1,2,2,128,128]{5,4,3,2,1,0:T(8,128)(2,1)S(1)}, bf16[4,1,2,2,128,128]{5,4,3,2,1,0:T(8,128)(2,1)S(1)}, u32[]{:S(2)}, u32[]{:S(2)}) collective-permute-start(bf16[4,1,2,2,128,128]{5,4,3,2,1,0:T(8,128)(2,1)S(1)} %stack.1), channel_id=1, source_target_pairs={{0,8},{4,12},{8,24},{12,28},{16,0},{20,4},{24,16},{28,20},{1,9},{5... | collective-permute-start | bytes 1572872 | tf_op jit(solution)/shard_map/ppermute | solution.py:416
  38.7 25.1 %collective-permute-start.9 = (bf16[4,1,2,2,128,128]{5,4,3,2,1,0:T(8,128)(2,1)S(1)}, bf16[4,1,2,2,128,128]{5,4,3,2,1,0:T(8,128)(2,1)S(1)}, u32[]{:S(2)}, u32[]{:S(2)}) collective-permute-start(bf16[4,1,2,2,128,128]{5,4,3,2,1,0:T(8,128)(2,1)S(1)} %stack.1), channel_id=1, source_target_pairs={{0,16},{4,20},{8,0},{12,4},{16,24},{20,28},{24,8},{28,12},{1,17},{... | collective-permute-start | bytes 1572872 | tf_op jit(solution)/shard_map/ppermute | solution.py:416
  40.8 0.7 %copy-start.5 = (s32[3]{0:T(128)S(1)}, s32[3]{0:T(128)}, u32[]{:S(2)}) copy-start(s32[3]{0:T(128)} %bit_shifts_ref.1) | copy-start | bytes 40
  40.8 0.7 %copy-start.6 = (f32[3]{0:T(128)S(1)}, f32[3]{0:T(128)}, u32[]{:S(2)}) copy-start(f32[3]{0:T(128)} %occupation_ref.1) | copy-start | bytes 40
  41.5 0.9 %copy-start.1 = (bf16[1,3,2,128,128]{4,3,2,1,0:T(8,128)(2,1)S(1)}, bf16[1,3,2,128,128]{4,3,2,1,0:T(8,128)(2,1)}, u32[]{:S(2)}) copy-start(bf16[1,3,2,128,128]{4,3,2,1,0:T(8,128)(2,1)} %copy-done) | copy-start | bytes 589828
  42.4 0.9 %copy-start.3 = (bf16[3,128,128]{2,1,0:T(8,128)(2,1)S(1)}, bf16[3,128,128]{2,1,0:T(8,128)(2,1)}, u32[]{:S(2)}) copy-start(bf16[3,128,128]{2,1,0:T(8,128)(2,1)} %coupling_ref.3) | copy-start | bytes 294916
  45.1 1.7 %collective-permute-start.10 = (bf16[1,2,2,128,128]{4,3,2,1,0:T(8,128)(2,1)S(1)}, bf16[1,2,2,128,128]{4,3,2,1,0:T(8,128)(2,1)S(1)}, u32[]{:S(2)}, u32[]{:S(2)}) collective-permute-start(bf16[1,2,2,128,128]{4,3,2,1,0:T(8,128)(2,1)S(1)} %get-tuple-element.24), channel_id=1, source_target_pairs={{0,1},{1,0},{2,3},{3,2},{4,5},{5,4},{6,7},{7,6},{8,9},{9,8},{10,11... | collective-permute-start | bytes 393224 | tf_op jit(solution)/shard_map/ppermute | solution.py:24
  45.2 6.4 %collective-permute-start.11 = (bf16[1,2,2,128,128]{4,3,2,1,0:T(8,128)(2,1)S(1)}, bf16[1,2,2,128,128]{4,3,2,1,0:T(8,128)(2,1)S(1)}, u32[]{:S(2)}, u32[]{:S(2)}) collective-permute-start(bf16[1,2,2,128,128]{4,3,2,1,0:T(8,128)(2,1)S(1)} %get-tuple-element.25), channel_id=1, source_target_pairs={{0,2},{1,3},{2,0},{3,1},{4,6},{5,7},{6,4},{7,5},{8,10},{9,11},{10,... | collective-permute-start | bytes 393224 | tf_op jit(solution)/shard_map/ppermute | solution.py:24
  46.8 6.5 %collective-permute-start.12 = (bf16[1,2,2,128,128]{4,3,2,1,0:T(8,128)(2,1)S(1)}, bf16[1,2,2,128,128]{4,3,2,1,0:T(8,128)(2,1)S(1)}, u32[]{:S(2)}, u32[]{:S(2)}) collective-permute-start(bf16[1,2,2,128,128]{4,3,2,1,0:T(8,128)(2,1)S(1)} %get-tuple-element.26), channel_id=1, source_target_pairs={{0,3},{1,2},{2,1},{3,0},{4,7},{5,6},{6,5},{7,4},{8,11},{9,10},{10,... | collective-permute-start | bytes 393224 | tf_op jit(solution)/shard_map/ppermute | solution.py:24

commit v5 on v4

--- a/solution.py
+++ b/solution.py
@@ -15,8 +15,9 @@
 HBM = pl.BlockSpec(memory_space=pltpu.HBM)
 UNROLL = 8
 GROUP = 4
+NEARS = 4
 RESIDENT_BYTES = 1600 * 1024
-PARAMS = pltpu.CompilerParams(vmem_limit_bytes=40 * 2**20)
+PARAMS = pltpu.CompilerParams(vmem_limit_bytes=24 * 2**20)
 
 
 def flip(value, axis, mask):
@@ -336,19 +337,19 @@
     )(place, *in_vmem(pieces))
 
 
-def last_kernel(terms, energies, first, weights_ref, *refs):
-    arrived, (_, out_ref, result, sems) = refs[:terms], refs[terms:]
+def weighted_kernel(terms, energies, first, near, weights_ref, *refs):
+    arrived, (last_ref, _, out_ref, result, sems) = refs[: terms - 1], refs[terms - 1 :]
     weights = [weights_ref[at, :1] for at in range(terms)]
     place = lax.axis_index("atom")
     distances, count = result.shape[:2]
     stores = []
     for d in range(distances):
         for e in range(count):
-            total = weights[0] * arrived[0][d, e].astype(jnp.float32)
-            for weight, term in zip(weights[1:], arrived[1:]):
-                total += weight * term[d, e].astype(jnp.float32)
+            total = weights[-1] * last_ref[d, e].astype(jnp.float32)
+            for weight, term in zip(weights, arrived):
+                total += weight * term[near + d, e].astype(jnp.float32)
             result[d, e] = total.astype(jnp.bfloat16)
-            row = (place ^ d) * energies + first + e
+            row = (place ^ (near + d)) * energies + first + e
             store = pltpu.make_async_copy(result.at[d, e], out_ref.at[row], sems.at[d, e])
             store.start()
             stores.append(store)
@@ -356,40 +357,48 @@
         store.wait()
 
 
-def place_second(weights, arrived, out, energies, first):
-    shape, terms = arrived[0].shape, len(arrived)
-    return pl.pallas_call(
-        functools.partial(last_kernel, terms, energies, first),
+def place_sum(weights, arrived, last, out, energies, first, near):
+    terms = len(arrived) + 1
+    return pl.pallas_call(
+        functools.partial(weighted_kernel, terms, energies, first, near),
         out_shape=jax.ShapeDtypeStruct(out.shape, out.dtype),
         in_specs=[VMEM] * (terms + 1) + [ANY],
         out_specs=ANY,
         scratch_shapes=[
-            pltpu.VMEM(shape, jnp.bfloat16),
-            pltpu.SemaphoreType.DMA(shape[:2]),
+            pltpu.VMEM(last.shape, jnp.bfloat16),
+            pltpu.SemaphoreType.DMA(last.shape[:2]),
         ],
         input_output_aliases={terms + 1: 0},
         compiler_params=PARAMS,
-        name="place_second",
-    )(*in_vmem([weights]), *in_vmem(arrived), out)
-
-
-def stack_kernel(distances, *refs):
-    pieces, out_ref, sems = refs[:distances], refs[distances], refs[distances + 1]
+        cost_estimate=pl.CostEstimate(
+            flops=2 * terms * last.size, bytes_accessed=2 * (terms + 1) * last.size, transcendentals=0
+        ),
+        name="place_sum",
+    )(*in_vmem([weights]), *in_vmem([*arrived, last]), out)
+
+
+def stack_kernel(near, *refs):
+    *pieces, whole_ref, near_ref, far_ref, sems = refs
     copies = []
     for distance, piece in enumerate(pieces):
-        copies.append(pltpu.make_async_copy(piece, out_ref.at[distance], sems.at[distance]))
-        copies[-1].start()
+        part = near_ref.at[distance] if distance < near else far_ref.at[distance - near]
+        for at, target in enumerate((whole_ref.at[distance], part)):
+            copies.append(pltpu.make_async_copy(piece, target, sems.at[at, distance]))
+            copies[-1].start()
     for copy in copies:
         copy.wait()
 
 
-def stack(pieces):
-    return pl.pallas_call(
-        functools.partial(stack_kernel, len(pieces)),
-        out_shape=jax.ShapeDtypeStruct((len(pieces), *pieces[0].shape), jnp.bfloat16),
-        in_specs=[VMEM] * len(pieces),
-        out_specs=ANY,
-        scratch_shapes=[pltpu.SemaphoreType.DMA((len(pieces),))],
+def stack(pieces, near):
+    own, count = pieces[0].shape, len(pieces)
+    return pl.pallas_call(
+        functools.partial(stack_kernel, near),
+        out_shape=[
+            jax.ShapeDtypeStruct((size, *own), jnp.bfloat16) for size in (count, near, count - near)
+        ],
+        in_specs=[VMEM] * count,
+        out_specs=[ANY] * 3,
+        scratch_shapes=[pltpu.SemaphoreType.DMA((2, count))],
         compiler_params=PARAMS,
         name="stack",
     )(*in_vmem(pieces))
@@ -446,10 +455,13 @@
     exchanged_b = [coupled_b[0]]
     for distance in range(1, atoms):
         exchanged_b.append(flip(coupled_b[distance], "atom", distance))
-    exchanged_b = stack(exchanged_b)
-    arrived_b = {}
-    for term in range(terms):
-        arrived_b[term] = exchange(exchanged_b, term)
+    near = atoms - max(atoms // NEARS, 1)
+    whole_b, near_b, far_b = stack(exchanged_b, near)
+    arrived_b = []
+    for term in range(terms - 1):
+        arrived_b.append(exchange(whole_b, term))
+    arrived_near = exchange(near_b, terms - 1)
+    arrived_far = exchange(far_b, terms - 1)
 
     weights, *coupled_a = sum_couple(
         (place, odd, bit_shifts, occupation, table),
@@ -461,8 +473,8 @@
     for distance in range(1, atoms):
         exchanged_a.append(flip(coupled_a[distance], "atom", distance))
     out = place_first(place, exchanged_a, energies)
-    arrived_b = [arrived_b[term] for term in range(terms)]
-    return place_second(weights, arrived_b, out, energies, half)
+    out = place_sum(weights, arrived_b, arrived_near, out, energies, half, 0)
+    return place_sum(weights, arrived_b, arrived_far, out, energies, half, near)
 
 
 def solution(mesh):

time: 65.2 us -> 68 us (1.043)
  waiting for transfers between devices: 33.1 us -> 36 us
  local copies, waits for them, and re-layouts: 4.72 us -> 2.88 us
  Pallas kernels: 11.8 us -> 13 us
    ppermute x7 -> x8, waiting for transfers between devices: 19.6 us -> 23.2 us  [exchange(): return lax.ppermute(value, 'win', pairs)]
    unnamed x14, local copies, waits for them, and re-layouts: 4.72 us -> 2.88 us
    pallas_call x2 -> x3, Pallas kernels: 1.67 us -> 2.88 us  [the longest x2 1.65 us: place_sum(): pl.pallas_call(functools.partial(weighted_kernel, terms, energies, first,...]
    ppermute x7 -> x8, starting transfers between devices: 10.3 us -> 10.6 us  [exchange(): return lax.ppermute(value, 'win', pairs)]
  transfers between devices with their start and end apart: 13 -> 14, of which waited for: 6 -> 7; matrix products, arithmetic and copies ran while one was open for 0% -> 0% of each run, Pallas kernels for 11% -> 13%
where the time goes in v5:
time: 68 us; the launch traced here: 67.6 us
  waiting for transfers between devices  36 us (53%)
  starting transfers between devices  15.6 us (23%)
  Pallas kernels  13 us (19%)
  local copies, waits for them, and re-layouts  2.88 us (4%)
    ppermute x8, waiting for transfers between devices, exchange(): return lax.ppermute(value, 'win', pairs)  23.2 us
    ppermute x6, waiting for transfers between devices, flip(): return lax.ppermute(value, axis, pairs)  12.9 us
    ppermute x8, starting transfers between devices, exchange(): return lax.ppermute(value, 'win', pairs)  10.6 us
    ppermute x6, starting transfers between devices, flip(): return lax.ppermute(value, axis, pairs)  4.94 us
    pallas_call x1, Pallas kernels, lesser_couple(): pl.pallas_call(functools.partial(lesser_couple_kernel, first), out_shape=...  3.67 us
    unnamed x14, local copies, waits for them, and re-layouts  2.88 us
    pallas_call x1, Pallas kernels, lesser_rest(): pl.pallas_call(functools.partial(lesser_rest_kernel, first), out_shape=[k...  2.46 us
    pallas_call x1, Pallas kernels, sum_couple(): pl.pallas_call(functools.partial(sum_couple_kernel, [len(term) for term i...  1.74 us
  transfers between devices with their start and end apart: 14, of which 7 were waited for; matrix products, arithmetic and copies ran while one was open for 0% of the time, Pallas kernels for 13%

profile of v5, /device:TPU:0, one launch (start us, length us, event | category | flops | bytes accessed | tf_op | source)
XLA Modules:
  0.0 67.6 jit_solution(5741386848666636170)
XLA Ops:
  0.0 0.7 %copy-done.2 = s32[8,3]{0,1:T(4,128)S(1)} copy-done((s32[8,3]{0,1:T(4,128)S(1)}, s32[8,3]{0,1:T(4,128)}, u32[]{:S(2)}) %copy-start.2) | copy-done | bytes 120
  0.7 0.9 %copy-done = bf16[3,128,128]{2,1,0:T(8,128)(2,1)S(1)} copy-done((bf16[3,128,128]{2,1,0:T(8,128)(2,1)S(1)}, bf16[3,128,128]{2,1,0:T(8,128)(2,1)}, u32[]{:S(2)}) %copy-start) | copy-done | bytes 98328
  1.6 3.7 %lesser_couple.1 = (bf16[1,2,2,128,128]{4,3,2,1,0:T(8,128)(2,1)S(1)}, bf16[1,2,2,128,128]{4,3,2,1,0:T(8,128)(2,1)S(1)}, bf16[1,2,2,128,128]{4,3,2,1,0:T(8,128)(2,1)S(1)}, bf16[1,2,2,128,128]{4,3,2,1,0:T(8,128)(2,1)S(1)}) custom-call(s32[1]{0:T(128)} %bitcast.place_ref, s32[3,8]{1,0:T(4,128)S(1)} %bitcast.3, bf16[3,128,128]{2,1,0:T(8,128)(2,1)S(1)} %copy-done, ...), custom_call_target="tpu_custom_call" | custom-call | flops 671088640 | bytes 1572864 | tf_op jit(solution)/shard_map/lesser_couple/pallas_call | solution.py:223
  5.3 0.6 collective-permute-start.4
  5.8 1.4 %lesser_begin.1.refs_2_ = bf16[1,3,2,128,128]{4,3,2,1,0:T(8,128)(2,1)S(1)} custom-call(bf16[2,8,2,128,128]{4,3,2,1,0:T(8,128)(2,1)} %refs_0_.3, bf16[2,8,2,128,128]{4,3,2,1,0:T(8,128)(2,1)} %refs_1_.3), custom_call_target="tpu_custom_call" | custom-call | flops 100663296 | bytes 589824 | tf_op jit(solution)/shard_map/lesser_begin/pallas_call | solution.py:176
  7.3 2.5 %lesser_rest.1 = (bf16[1,5,2,128,128]{4,3,2,1,0:T(8,128)(2,1)S(1)}, bf16[1,8,2,128,128]{4,3,2,1,0:T(8,128)(2,1)}) custom-call(bf16[2,8,2,128,128]{4,3,2,1,0:T(8,128)(2,1)} %refs_0_.3, bf16[2,8,2,128,128]{4,3,2,1,0:T(8,128)(2,1)} %refs_1_.3, bf16[1,3,2,128,128]{4,3,2,1,0:T(8,128)(2,1)S(1)} %lesser_begin.1.refs_2_), custom_call_target="tpu_custom_call" | custom-call | flops 167772160 | bytes 983040 | tf_op jit(solution)/shard_map/lesser_rest/pallas_call | solution.py:191
  9.7 2.6 %collective-permute-start = (bf16[1,8,2,128,128]{4,3,2,1,0:T(8,128)(2,1)}, bf16[1,8,2,128,128]{4,3,2,1,0:T(8,128)(2,1)S(1)}, u32[]{:S(2)}, u32[]{:S(2)}) collective-permute-start(bf16[1,8,2,128,128]{4,3,2,1,0:T(8,128)(2,1)} %get-tuple-element.19), channel_id=1, source_target_pairs={{0,4},{4,0},{8,12},{12,8},{16,20},{20,16},{24,28},{28,24},{1,5},{5... | collective-permute-start | bytes 1572872 | tf_op jit(solution)/shard_map/ppermute | solution.py:425
  12.3 2.6 %collective-permute-start.3 = (bf16[1,8,2,128,128]{4,3,2,1,0:T(8,128)(2,1)}, bf16[1,8,2,128,128]{4,3,2,1,0:T(8,128)(2,1)S(1)}, u32[]{:S(2)}, u32[]{:S(2)}) collective-permute-start(bf16[1,8,2,128,128]{4,3,2,1,0:T(8,128)(2,1)} %get-tuple-element.19), channel_id=1, source_target_pairs={{0,16},{4,20},{8,0},{12,4},{16,24},{20,28},{24,8},{28,12},{1,17},{... | collective-permute-start | bytes 1572872 | tf_op jit(solution)/shard_map/ppermute | solution.py:425
  14.9 1.5 %collective-permute-start.5 = (bf16[1,2,2,128,128]{4,3,2,1,0:T(8,128)(2,1)S(1)}, bf16[1,2,2,128,128]{4,3,2,1,0:T(8,128)(2,1)S(1)}, u32[]{:S(2)}, u32[]{:S(2)}) collective-permute-start(bf16[1,2,2,128,128]{4,3,2,1,0:T(8,128)(2,1)S(1)} %get-tuple-element.24), channel_id=1, source_target_pairs={{0,2},{1,3},{2,0},{3,1},{4,6},{5,7},{6,4},{7,5},{8,10},{9,11},{10,... | collective-permute-start | bytes 393224 | tf_op jit(solution)/shard_map/ppermute | solution.py:25
  16.4 1.9 %collective-permute-start.1 = (bf16[1,3,2,128,128]{4,3,2,1,0:T(8,128)(2,1)S(1)}, bf16[1,3,2,128,128]{4,3,2,1,0:T(8,128)(2,1)S(1)}, u32[]{:S(2)}, u32[]{:S(2)}) collective-permute-start(bf16[1,3,2,128,128]{4,3,2,1,0:T(8,128)(2,1)S(1)} %lesser_begin.1.refs_2_), channel_id=1, source_target_pairs={{0,8},{4,12},{8,24},{12,28},{16,0},{20,4},{24,16},{28,20},{1,9},{5... | collective-permute-start | bytes 589832 | tf_op jit(solution)/shard_map/ppermute | solution.py:425
  18.3 1.9 %collective-permute-done.5.refs_2_ = bf16[1,2,2,128,128]{4,3,2,1,0:T(8,128)(2,1)S(1)} collective-permute-done((bf16[1,2,2,128,128]{4,3,2,1,0:T(8,128)(2,1)S(1)}, bf16[1,2,2,128,128]{4,3,2,1,0:T(8,128)(2,1)S(1)}, u32[]{:S(2)}, u32[]{:S(2)}) %collective-permute-start.5) | collective-permute-done | bytes 131104 | tf_op jit(solution)/shard_map/ppermute | solution.py:25
  20.2 0.2 collective-permute-start.6
  20.4 5.5 %collective-permute-done.6.refs_3_ = bf16[1,2,2,128,128]{4,3,2,1,0:T(8,128)(2,1)S(1)} collective-permute-done((bf16[1,2,2,128,128]{4,3,2,1,0:T(8,128)(2,1)S(1)}, bf16[1,2,2,128,128]{4,3,2,1,0:T(8,128)(2,1)S(1)}, u32[]{:S(2)}, u32[]{:S(2)}) %collective-permute-start.6) | collective-permute-done | bytes 131104 | tf_op jit(solution)/shard_map/ppermute | solution.py:25
  25.9 1.2 %stack.1 = (bf16[4,1,2,2,128,128]{5,4,3,2,1,0:T(8,128)(2,1)}, bf16[3,1,2,2,128,128]{5,4,3,2,1,0:T(8,128)(2,1)S(1)}, bf16[1,1,2,2,128,128]{5,4,3,2,1,0:T(8,128)(2,1)S(1)}) custom-call(bf16[1,2,2,128,128]{4,3,2,1,0:T(8,128)(2,1)S(1)} %get-tuple-element.22.refs_0_, bf16[1,2,2,128,128]{4,3,2,1,0:T(8,128)(2,1)S(1)} %collective-permute-done.4.refs_1_, ...), custom_call_target="tpu_custom_call" | custom-call | tf_op jit(solution)/shard_map/stack/pallas_call | solution.py:394
  27.2 0.6 copy-done.5
  27.8 0.5 collective-permute-start.7
  28.4 11.3 %collective-permute-done.1.refs_1_ = bf16[1,3,2,128,128]{4,3,2,1,0:T(8,128)(2,1)S(1)} collective-permute-done((bf16[1,3,2,128,128]{4,3,2,1,0:T(8,128)(2,1)S(1)}, bf16[1,3,2,128,128]{4,3,2,1,0:T(8,128)(2,1)S(1)}, u32[]{:S(2)}, u32[]{:S(2)}) %collective-permute-start.1) | collective-permute-done | bytes 196640 | tf_op jit(solution)/shard_map/ppermute | solution.py:425
  39.7 0.7 %collective-permute-start.8 = (bf16[4,1,2,2,128,128]{5,4,3,2,1,0:T(8,128)(2,1)}, bf16[4,1,2,2,128,128]{5,4,3,2,1,0:T(8,128)(2,1)S(1)}, u32[]{:S(2)}, u32[]{:S(2)}) collective-permute-start(bf16[4,1,2,2,128,128]{5,4,3,2,1,0:T(8,128)(2,1)} %get-tuple-element.26), channel_id=1, source_target_pairs={{0,8},{4,12},{8,24},{12,28},{16,0},{20,4},{24,16},{28,20},{1,9},{5... | collective-permute-start | bytes 1572872 | tf_op jit(solution)/shard_map/ppermute | solution.py:425
  40.4 2.2 %collective-permute-start.10 = (bf16[3,1,2,2,128,128]{5,4,3,2,1,0:T(8,128)(2,1)S(1)}, bf16[3,1,2,2,128,128]{5,4,3,2,1,0:T(8,128)(2,1)S(1)}, u32[]{:S(2)}, u32[]{:S(2)}) collective-permute-start(bf16[3,1,2,2,128,128]{5,4,3,2,1,0:T(8,128)(2,1)S(1)} %get-tuple-element.28), channel_id=1, source_target_pairs={{0,16},{4,20},{8,0},{12,4},{16,24},{20,28},{24,8},{28,12},{1,17},{... | collective-permute-start | bytes 1179656 | tf_op jit(solution)/shard_map/ppermute | solution.py:425
  42.7 0.6 copy-done.3
  43.3 1.7 %sum_couple.1 = (f32[3,8,128]{2,1,0:T(8,128)S(1)}, bf16[1,2,2,128,128]{4,3,2,1,0:T(8,128)(2,1)S(1)}, bf16[1,2,2,128,128]{4,3,2,1,0:T(8,128)(2,1)S(1)}, bf16[1,2,...) custom-call(s32[1]{0:T(128)} %bitcast.place_ref, s32[1]{0:T(128)} %bitcast.1.odd_ref, s32[3]{0:T(128)S(1)} %copy-done.3, ...), custom_call_target="tpu_custom_call" | custom-call | flops 402653184 | bytes 1572864 | tf_op jit(solution)/shard_map/sum_couple/pallas_call | solution.py:276
  45.1 0.1 collective-permute-start.11
  45.1 1.6 %collective-permute-start.12 = (bf16[1,2,2,128,128]{4,3,2,1,0:T(8,128)(2,1)S(1)}, bf16[1,2,2,128,128]{4,3,2,1,0:T(8,128)(2,1)S(1)}, u32[]{:S(2)}, u32[]{:S(2)}) collective-permute-start(bf16[1,2,2,128,128]{4,3,2,1,0:T(8,128)(2,1)S(1)} %get-tuple-element.31), channel_id=1, source_target_pairs={{0,2},{1,3},{2,0},{3,1},{4,6},{5,7},{6,4},{7,5},{8,10},{9,11},{10,... | collective-permute-start | bytes 393224 | tf_op jit(solution)/shard_map/ppermute | solution.py:25
  46.7 1.0 %collective-permute-start.13 = (bf16[1,2,2,128,128]{4,3,2,1,0:T(8,128)(2,1)S(1)}, bf16[1,2,2,128,128]{4,3,2,1,0:T(8,128)(2,1)S(1)}, u32[]{:S(2)}, u32[]{:S(2)}) collective-permute-start(bf16[1,2,2,128,128]{4,3,2,1,0:T(8,128)(2,1)S(1)} %get-tuple-element.32), channel_id=1, source_target_pairs={{0,3},{1,2},{2,1},{3,0},{4,7},{5,6},{6,5},{7,4},{8,11},{9,10},{10,... | collective-permute-start | bytes 393224 | tf_op jit(solution)/shard_map/ppermute | solution.py:25
  47.7 3.8 %collective-permute-done.12.refs_2_ = bf16[1,2,2,128,128]{4,3,2,1,0:T(8,128)(2,1)S(1)} collective-permute-done((bf16[1,2,2,128,128]{4,3,2,1,0:T(8,128)(2,1)S(1)}, bf16[1,2,2,128,128]{4,3,2,1,0:T(8,128)(2,1)S(1)}, u32[]{:S(2)}, u32[]{:S(2)}) %collective-permute-start.12) | collective-permute-done | bytes 131104 | tf_op jit(solution)/shard_map/ppermute | solution.py:25
  51.6 0.1 collective-permute-start.9
  51.7 1.6 %collective-permute-done.13.refs_3_ = bf16[1,2,2,128,128]{4,3,2,1,0:T(8,128)(2,1)S(1)} collective-permute-done((bf16[1,2,2,128,128]{4,3,2,1,0:T(8,128)(2,1)S(1)}, bf16[1,2,2,128,128]{4,3,2,1,0:T(8,128)(2,1)S(1)}, u32[]{:S(2)}, u32[]{:S(2)}) %collective-permute-start.13) | collective-permute-done | bytes 131104 | tf_op jit(solution)/shard_map/ppermute | solution.py:25
  53.3 0.8 %place_first.1.refs_3_ = bf16[8,2,2,128,128]{4,3,2,1,0:T(8,128)(2,1)} custom-call(s32[1]{0:T(128)} %bitcast.place_ref, bf16[1,2,2,128,128]{4,3,2,1,0:T(8,128)(2,1)S(1)} %get-tuple-element.29.refs_0_, bf16[1,2,2,128,128]{4,3,2,1,0:T(8,128)(2,1)S(1)} %collective-permute-done.11.refs_1_, bf16[1,2,2,128,128]{4,3,2,1,0:T(8,128)(2,1)S(1)} %collective-permute-done.12.refs_2_, ...), custom_call_target="tpu_custom_call" | custom-call | tf_op jit(solution)/shard_map/place_first/pallas_call | solution.py:329
  54.1 8.9 %collective-permute-done.10.refs_2_ = bf16[3,1,2,2,128,128]{5,4,3,2,1,0:T(8,128)(2,1)S(1)} collective-permute-done((bf16[3,1,2,2,128,128]{5,4,3,2,1,0:T(8,128)(2,1)S(1)}, bf16[3,1,2,2,128,128]{5,4,3,2,1,0:T(8,128)(2,1)S(1)}, u32[]{:S(2)}, u32[]{:S(2)}) %collective-permute-start.10) | collective-permute-done | bytes 393248 | tf_op jit(solution)/shard_map/ppermute | solution.py:425
  63.1 2.9 %collective-permute-done.8.refs_1_ = bf16[4,1,2,2,128,128]{5,4,3,2,1,0:T(8,128)(2,1)S(1)} collective-permute-done((bf16[4,1,2,2,128,128]{5,4,3,2,1,0:T(8,128)(2,1)}, bf16[4,1,2,2,128,128]{5,4,3,2,1,0:T(8,128)(2,1)S(1)}, u32[]{:S(2)}, u32[]{:S(2)}) %collective-permute-start.8) | collective-permute-done | bytes 524320 | tf_op jit(solution)/shard_map/ppermute | solution.py:425
  65.9 0.9 %place_sum.2.refs_3_ = bf16[8,2,2,128,128]{4,3,2,1,0:T(8,128)(2,1)} custom-call(f32[3,8,128]{2,1,0:T(8,128)S(1)} %get-tuple-element.21.weights_ref, bf16[4,1,2,2,128,128]{5,4,3,2,1,0:T(8,128)(2,1)S(1)} %collective-permute-done.7.refs_0_, bf16[4,1,2,2,128,128]{5,4,3,2,1,0:T(8,128)(2,1)S(1)} %collective-permute-done.8.refs_1_, ...), custom_call_target="tpu_custom_call", output_to_operand_aliasing={{}: (4, {})} | custom-call | flops 1179648 | bytes 1572864 | tf_op jit(solution)/shard_map/place_sum/pallas_call | solution.py:362
  66.9 0.8 %place_sum.3 = bf16[8,2,2,128,128]{4,3,2,1,0:T(8,128)(2,1)} custom-call(f32[3,8,128]{2,1,0:T(8,128)S(1)} %get-tuple-element.21.weights_ref, bf16[4,1,2,2,128,128]{5,4,3,2,1,0:T(8,128)(2,1)S(1)} %collective-permute-done.7.refs_0_, bf16[4,1,2,2,128,128]{5,4,3,2,1,0:T(8,128)(2,1)S(1)} %collective-permute-done.8.refs_1_, ...), custom_call_target="tpu_custom_call", output_to_operand_aliasing={{}: (4, {})} | custom-call | flops 393216 | bytes 524288 | tf_op jit(solution)/shard_map/place_sum/pallas_call | solution.py:362
  (18 shorter events, 0.1 us)
Async XLA Ops:
  0.0 0.7 %copy-start.2 = (s32[8,3]{0,1:T(4,128)S(1)}, s32[8,3]{0,1:T(4,128)}, u32[]{:S(2)}) copy-start(s32[8,3]{0,1:T(4,128)} %param.10) | copy-start | bytes 292
  0.7 0.9 %copy-start = (bf16[3,128,128]{2,1,0:T(8,128)(2,1)S(1)}, bf16[3,128,128]{2,1,0:T(8,128)(2,1)}, u32[]{:S(2)}) copy-start(bf16[3,128,128]{2,1,0:T(8,128)(2,1)} %coupling_ref.3) | copy-start | bytes 294916
  5.3 11.1 %collective-permute-start.4 = (bf16[1,2,2,128,128]{4,3,2,1,0:T(8,128)(2,1)S(1)}, bf16[1,2,2,128,128]{4,3,2,1,0:T(8,128)(2,1)S(1)}, u32[]{:S(2)}, u32[]{:S(2)}) collective-permute-start(bf16[1,2,2,128,128]{4,3,2,1,0:T(8,128)(2,1)S(1)} %get-tuple-element.23), channel_id=1, source_target_pairs={{0,1},{1,0},{2,3},{3,2},{4,5},{5,4},{6,7},{7,6},{8,9},{9,8},{10,11... | collective-permute-start | bytes 393224 | tf_op jit(solution)/shard_map/ppermute | solution.py:25
  9.7 32.9 %collective-permute-start = (bf16[1,8,2,128,128]{4,3,2,1,0:T(8,128)(2,1)}, bf16[1,8,2,128,128]{4,3,2,1,0:T(8,128)(2,1)S(1)}, u32[]{:S(2)}, u32[]{:S(2)}) collective-permute-start(bf16[1,8,2,128,128]{4,3,2,1,0:T(8,128)(2,1)} %get-tuple-element.19), channel_id=1, source_target_pairs={{0,4},{4,0},{8,12},{12,8},{16,20},{20,16},{24,28},{28,24},{1,5},{5... | collective-permute-start | bytes 1572872 | tf_op jit(solution)/shard_map/ppermute | solution.py:425
  12.3 30.4 %collective-permute-start.3 = (bf16[1,8,2,128,128]{4,3,2,1,0:T(8,128)(2,1)}, bf16[1,8,2,128,128]{4,3,2,1,0:T(8,128)(2,1)S(1)}, u32[]{:S(2)}, u32[]{:S(2)}) collective-permute-start(bf16[1,8,2,128,128]{4,3,2,1,0:T(8,128)(2,1)} %get-tuple-element.19), channel_id=1, source_target_pairs={{0,16},{4,20},{8,0},{12,4},{16,24},{20,28},{24,8},{28,12},{1,17},{... | collective-permute-start | bytes 1572872 | tf_op jit(solution)/shard_map/ppermute | solution.py:425
  14.9 5.3 %collective-permute-start.5 = (bf16[1,2,2,128,128]{4,3,2,1,0:T(8,128)(2,1)S(1)}, bf16[1,2,2,128,128]{4,3,2,1,0:T(8,128)(2,1)S(1)}, u32[]{:S(2)}, u32[]{:S(2)}) collective-permute-start(bf16[1,2,2,128,128]{4,3,2,1,0:T(8,128)(2,1)S(1)} %get-tuple-element.24), channel_id=1, source_target_pairs={{0,2},{1,3},{2,0},{3,1},{4,6},{5,7},{6,4},{7,5},{8,10},{9,11},{10,... | collective-permute-start | bytes 393224 | tf_op jit(solution)/shard_map/ppermute | solution.py:25
  16.4 24.0 %collective-permute-start.2 = (bf16[1,5,2,128,128]{4,3,2,1,0:T(8,128)(2,1)S(1)}, bf16[1,5,2,128,128]{4,3,2,1,0:T(8,128)(2,1)S(1)}, u32[]{:S(2)}, u32[]{:S(2)}) collective-permute-start(bf16[1,5,2,128,128]{4,3,2,1,0:T(8,128)(2,1)S(1)} %get-tuple-element.20), channel_id=1, source_target_pairs={{0,8},{4,12},{8,24},{12,28},{16,0},{20,4},{24,16},{28,20},{1,9},{5... | collective-permute-start | bytes 983048 | tf_op jit(solution)/shard_map/ppermute | solution.py:425
  16.4 23.3 %collective-permute-start.1 = (bf16[1,3,2,128,128]{4,3,2,1,0:T(8,128)(2,1)S(1)}, bf16[1,3,2,128,128]{4,3,2,1,0:T(8,128)(2,1)S(1)}, u32[]{:S(2)}, u32[]{:S(2)}) collective-permute-start(bf16[1,3,2,128,128]{4,3,2,1,0:T(8,128)(2,1)S(1)} %lesser_begin.1.refs_2_), channel_id=1, source_target_pairs={{0,8},{4,12},{8,24},{12,28},{16,0},{20,4},{24,16},{28,20},{1,9},{5... | collective-permute-start | bytes 589832 | tf_op jit(solution)/shard_map/ppermute | solution.py:425
  20.2 5.7 %collective-permute-start.6 = (bf16[1,2,2,128,128]{4,3,2,1,0:T(8,128)(2,1)S(1)}, bf16[1,2,2,128,128]{4,3,2,1,0:T(8,128)(2,1)S(1)}, u32[]{:S(2)}, u32[]{:S(2)}) collective-permute-start(bf16[1,2,2,128,128]{4,3,2,1,0:T(8,128)(2,1)S(1)} %get-tuple-element.25), channel_id=1, source_target_pairs={{0,3},{1,2},{2,1},{3,0},{4,7},{5,6},{6,5},{7,4},{8,11},{9,10},{10,... | collective-permute-start | bytes 393224 | tf_op jit(solution)/shard_map/ppermute | solution.py:25
  25.9 16.7 %copy-start.1 = (bf16[3,128,128]{2,1,0:T(8,128)(2,1)S(1)}, bf16[3,128,128]{2,1,0:T(8,128)(2,1)}, u32[]{:S(2)}) copy-start(bf16[3,128,128]{2,1,0:T(8,128)(2,1)} %coupling_ref.3) | copy-start | bytes 294916
  27.2 0.7 copy-start.5
  27.8 35.2 %collective-permute-start.7 = (bf16[4,1,2,2,128,128]{5,4,3,2,1,0:T(8,128)(2,1)}, bf16[4,1,2,2,128,128]{5,4,3,2,1,0:T(8,128)(2,1)S(1)}, u32[]{:S(2)}, u32[]{:S(2)}) collective-permute-start(bf16[4,1,2,2,128,128]{5,4,3,2,1,0:T(8,128)(2,1)} %get-tuple-element.26), channel_id=1, source_target_pairs={{0,4},{4,0},{8,12},{12,8},{16,20},{20,16},{24,28},{28,24},{1,5},{5... | collective-permute-start | bytes 1572872 | tf_op jit(solution)/shard_map/ppermute | solution.py:425
  39.7 26.2 %collective-permute-start.8 = (bf16[4,1,2,2,128,128]{5,4,3,2,1,0:T(8,128)(2,1)}, bf16[4,1,2,2,128,128]{5,4,3,2,1,0:T(8,128)(2,1)S(1)}, u32[]{:S(2)}, u32[]{:S(2)}) collective-permute-start(bf16[4,1,2,2,128,128]{5,4,3,2,1,0:T(8,128)(2,1)} %get-tuple-element.26), channel_id=1, source_target_pairs={{0,8},{4,12},{8,24},{12,28},{16,0},{20,4},{24,16},{28,20},{1,9},{5... | collective-permute-start | bytes 1572872 | tf_op jit(solution)/shard_map/ppermute | solution.py:425
  40.4 22.6 %collective-permute-start.10 = (bf16[3,1,2,2,128,128]{5,4,3,2,1,0:T(8,128)(2,1)S(1)}, bf16[3,1,2,2,128,128]{5,4,3,2,1,0:T(8,128)(2,1)S(1)}, u32[]{:S(2)}, u32[]{:S(2)}) collective-permute-start(bf16[3,1,2,2,128,128]{5,4,3,2,1,0:T(8,128)(2,1)S(1)} %get-tuple-element.28), channel_id=1, source_target_pairs={{0,16},{4,20},{8,0},{12,4},{16,24},{20,28},{24,8},{28,12},{1,17},{... | collective-permute-start | bytes 1179656 | tf_op jit(solution)/shard_map/ppermute | solution.py:425
  42.6 0.7 copy-start.3
  42.6 0.7 copy-start.4
  43.3 8.3 %copy-start.6 = (bf16[1,1,2,2,128,128]{5,4,3,2,1,0:T(8,128)(2,1)S(1)}, bf16[1,1,2,2,128,128]{5,4,3,2,1,0:T(8,128)(2,1)}, u32[]{:S(2)}) copy-start(bf16[1,1,2,2,128,128]{5,4,3,2,1,0:T(8,128)(2,1)} %copy-done.5) | copy-start | bytes 393220
  45.1 1.7 %collective-permute-start.11 = (bf16[1,2,2,128,128]{4,3,2,1,0:T(8,128)(2,1)S(1)}, bf16[1,2,2,128,128]{4,3,2,1,0:T(8,128)(2,1)S(1)}, u32[]{:S(2)}, u32[]{:S(2)}) collective-permute-start(bf16[1,2,2,128,128]{4,3,2,1,0:T(8,128)(2,1)S(1)} %get-tuple-element.30), channel_id=1, source_target_pairs={{0,1},{1,0},{2,3},{3,2},{4,5},{5,4},{6,7},{7,6},{8,9},{9,8},{10,11... | collective-permute-start | bytes 393224 | tf_op jit(solution)/shard_map/ppermute | solution.py:25
  45.1 6.4 %collective-permute-start.12 = (bf16[1,2,2,128,128]{4,3,2,1,0:T(8,128)(2,1)S(1)}, bf16[1,2,2,128,128]{4,3,2,1,0:T(8,128)(2,1)S(1)}, u32[]{:S(2)}, u32[]{:S(2)}) collective-permute-start(bf16[1,2,2,128,128]{4,3,2,1,0:T(8,128)(2,1)S(1)} %get-tuple-element.31), channel_id=1, source_target_pairs={{0,2},{1,3},{2,0},{3,1},{4,6},{5,7},{6,4},{7,5},{8,10},{9,11},{10,... | collective-permute-start | bytes 393224 | tf_op jit(solution)/shard_map/ppermute | solution.py:25
  46.7 6.6 %collective-permute-start.13 = (bf16[1,2,2,128,128]{4,3,2,1,0:T(8,128)(2,1)S(1)}, bf16[1,2,2,128,128]{4,3,2,1,0:T(8,128)(2,1)S(1)}, u32[]{:S(2)}, u32[]{:S(2)}) collective-permute-start(bf16[1,2,2,128,128]{4,3,2,1,0:T(8,128)(2,1)S(1)} %get-tuple-element.32), channel_id=1, source_target_pairs={{0,3},{1,2},{2,1},{3,0},{4,7},{5,6},{6,5},{7,4},{8,11},{9,10},{10,... | collective-permute-start | bytes 393224 | tf_op jit(solution)/shard_map/ppermute | solution.py:25
  51.6 15.3 %collective-permute-start.9 = (bf16[1,1,2,2,128,128]{5,4,3,2,1,0:T(8,128)(2,1)S(1)}, bf16[1,1,2,2,128,128]{5,4,3,2,1,0:T(8,128)(2,1)S(1)}, u32[]{:S(2)}, u32[]{:S(2)}) collective-permute-start(bf16[1,1,2,2,128,128]{5,4,3,2,1,0:T(8,128)(2,1)S(1)} %copy-done.6), channel_id=1, source_target_pairs={{0,16},{4,20},{8,0},{12,4},{16,24},{20,28},{24,8},{28,12},{1,17},{... | collective-permute-start | bytes 393224 | tf_op jit(solution)/shard_map/ppermute | solution.py:425
